TPU v7x, 256 devices: a whole 4x4x8 slice. The times are simulated.
256 devices in a mesh: chain: 16 (over z, y_lo), cand: 16 (over y_hi, x, core).
Axes of the slice: x: 4, y: 4 (y_hi: 2, y_lo: 2; y = y_hi * 2 + y_lo), z: 8, core: 2. Of those that a mesh axis runs over, the one named last changes fastest.
Arguments:
- archive_inputs: float32 [32, 3072], P(None, 'chain'), may hold values from -6 to 6
- candidate_inputs: float32 [32, 2048], P(None, 'cand'), may hold values from -6 to 6
- lengthscales: float32 [32], replicated, may hold values from 3 to 10
- factor: float32 [3072, 3072], P('chain'), as said below
Outputs:
- whitened: float32 [3072, 2048], P('chain', 'cand')
- corrected_cov: float32 [2048, 2048], P('chain', 'cand')
Inputs may be any that keep to these rules, and one draw needn't show every extreme that they name: factor is lower triangular (zeros above the diagonal); its diagonal lies between 0.2 * sqrt(3072) and 0.5 * sqrt(3072).
All inputs are finite; a program needn't handle non-finite values.
Results may differ from a plain program's by a relative error of at most 0.000076.
Values sent between devices are 32-bit elements; how exact they have to be, the bound alone decides.
No kernel may reach another device: no remote copies, remote signals or barrier semaphores. Data moves between devices by JAX's collectives and lax.ppermute only.
A program may use at most 64 MiB of HBM per device.

v0:
```python
import jax
import jax.numpy as jnp
from jax import lax
from jax.sharding import PartitionSpec as P


def picked(value, axis, root):
    return lax.dynamic_index_in_dim(lax.all_gather(value, axis), root, 0, keepdims=False)


def in_one_piece(arrays, axis, dim, along):
    widths = [a.shape[along] for a in arrays]
    both = jnp.concatenate(arrays, axis=along)
    whole = lax.all_gather(both, axis, axis=dim, tiled=True)
    return tuple(jnp.split(whole, [sum(widths[:k]) for k in range(1, len(widths))], axis=along))


def cut_along(value, dim, size):
    dims = value.shape
    tiles = value.reshape(*dims[:dim], size, dims[dim] // size, *dims[dim + 1 :])
    return jnp.moveaxis(tiles, dim, 0)


def sum_at_owner(value, axis, dim):
    tiles = cut_along(value, dim, lax.axis_size(axis))
    arrived = lax.all_to_all(tiles, axis, split_axis=0, concat_axis=0, tiled=True)
    return arrived.sum(axis=0)


def matern(first_set, second_set):
    differ = first_set[:, :, None] - second_set[:, None, :]
    radius = jnp.sqrt(5.0 * jnp.sum(differ * differ, axis=0))
    return (1.0 + radius + radius * radius / 3.0) * jnp.exp(-radius)


def shards(archive_inputs, candidate_inputs, lengthscales, factor):
    height = factor.shape[0]
    column_count = candidate_inputs.shape[1]
    sections = lax.axis_size("chain")
    position = lax.axis_index("chain")
    scaling = 1.0 / lengthscales
    scaled_archive = archive_inputs * scaling[:, None]
    scaled_candidates = candidate_inputs * scaling[:, None]
    cross_tile = matern(scaled_archive, scaled_candidates)
    own_diagonal = lax.dynamic_slice_in_dim(factor, position * height, height, 1)
    inverse_block = jax.scipy.linalg.solve_triangular(
        own_diagonal, jnp.eye(height, dtype=jnp.float32), lower=True
    )

    def solve_own(residue):
        return jnp.dot(inverse_block, residue, precision=lax.Precision.HIGHEST)

    def skip_solve(residue):
        return jnp.zeros_like(residue)

    def advance(sender, state_pair):
        residue, stored = state_pair
        solved = lax.cond(position == sender, solve_own, skip_solve, residue)
        solved_panel = picked(solved, "chain", sender)

        def apply_update(current):
            coupling = lax.dynamic_slice_in_dim(factor, sender * height, height, 1)
            return current - jnp.dot(coupling, solved_panel, precision=lax.Precision.HIGHEST)

        def keep_residue(current):
            return current

        residue = lax.cond(position > sender, apply_update, keep_residue, residue)
        stored = lax.dynamic_update_slice(
            stored, solved_panel[None], (sender, jnp.int32(0), jnp.int32(0))
        )
        return (residue, stored)

    initial = (cross_tile, jnp.zeros((sections, height, column_count), jnp.float32))
    residue, stored = lax.fori_loop(0, sections, advance, initial)
    own_panel = lax.dynamic_index_in_dim(stored, position, 0, keepdims=False)
    all_columns = column_count * lax.axis_size("cand")
    slab_width = all_columns // sections
    offset = position * slab_width
    every_panel, every_input = in_one_piece((own_panel, candidate_inputs), "cand", 1, 0)
    shared = sum_at_owner(
        jnp.dot(every_panel.T, own_panel, precision=lax.Precision.HIGHEST), "chain", 0
    )
    chosen = lax.dynamic_slice_in_dim(every_input, offset, slab_width, 1)
    prior_cov = matern(chosen * scaling[:, None], scaled_candidates)
    return (own_panel, prior_cov - shared)


def solution(mesh):
    return jax.shard_map(
        shards,
        mesh=mesh,
        in_specs=(P(None, "chain"), P(None, "cand"), P(), P("chain", None)),
        out_specs=(P("chain", "cand"), P("chain", "cand")),
        check_vma=False,
    )
```

profile of v0, /device:TPU:2, one launch (start us, length us, event | category | flops | bytes accessed | tf_op | source)
XLA Modules:
  0.0 1332.7 jit_solution(2131224545127510033)
XLA Ops:
  8.1 1.1 dynamic-slice_select_fusion
  9.3 19.7 %custom-call.4 = f32[2,128,128]{1,2,0:T(8,128)S(1)} custom-call(f32[2,128,128]{2,1,0:T(8,128)S(1)} %pad_maximum_fusion.1), custom_call_target="InvertDiagBlocksLowerTriangular" | custom-call | tf_op jit(solution)/shard_map/jit(_solve_triangular)/triangular_solve | solution.py:46
  30.3 1.0 multiply_reduce_fusion
  31.3 1195.2 %while.20 = (s32[]{:T(128)}, f32[192,128]{1,0:T(8,128)S(1)}, f32[16,192,128]{2,1,0:T(8,128)S(1)}, s32[]{:T(128)}, f32[192,192]{1,0:T(8,128)S(1)}, /*index=5*/f32[192,3072]{1,0:T(8,128)}, s32[]{:T(128)}) while((s32[]{:T(128)}, f32[192,128]{1,0:T(8,128)S(1)}, f32[16,192,128]{2,1,0:T(8,128)S(1)}, s32[]{:T(128)}, f32[192,192]{1,0:T(8,128)S(1)}, ...), condition=%wide.region_6.7_spmd, body=%wide.region_1.6_spmd.sunk | while | flops 113270792 | bytes 6537515 | solution.py:75
  32.4 75.1 %all-gather.8.cloned.1.call-done = f32[3072,128]{1,0:T(8,128)} async-done(((f32[192,128]{1,0:T(8,128)}), f32[3072,128]{1,0:T(8,128)}) %all-gather.8.cloned.1.call-update) | async-done | bytes 1572880 | tf_op jit(solution)/shard_map/while/body/eval_jaxpr/all_gather | solution.py:8
  107.5 0.9 constant_dynamic-update-slice_fusion.2
  109.2 73.6 %all-gather.8.cloned.1.call-done = f32[3072,128]{1,0:T(8,128)} async-done(((f32[192,128]{1,0:T(8,128)}), f32[3072,128]{1,0:T(8,128)}) %all-gather.8.cloned.1.call-update) | async-done | bytes 1572880 | tf_op jit(solution)/shard_map/while/body/eval_jaxpr/all_gather | solution.py:8
  182.8 0.9 constant_dynamic-update-slice_fusion.2
  184.5 73.6 %all-gather.8.cloned.1.call-done = f32[3072,128]{1,0:T(8,128)} async-done(((f32[192,128]{1,0:T(8,128)}), f32[3072,128]{1,0:T(8,128)}) %all-gather.8.cloned.1.call-update) | async-done | bytes 1572880 | tf_op jit(solution)/shard_map/while/body/eval_jaxpr/all_gather | solution.py:8
  258.1 0.9 constant_dynamic-update-slice_fusion.2
  259.9 73.3 %all-gather.8.cloned.1.call-done = f32[3072,128]{1,0:T(8,128)} async-done(((f32[192,128]{1,0:T(8,128)}), f32[3072,128]{1,0:T(8,128)}) %all-gather.8.cloned.1.call-update) | async-done | bytes 1572880 | tf_op jit(solution)/shard_map/while/body/eval_jaxpr/all_gather | solution.py:8
  333.2 0.9 constant_dynamic-update-slice_fusion.2
  334.9 73.3 %all-gather.8.cloned.1.call-done = f32[3072,128]{1,0:T(8,128)} async-done(((f32[192,128]{1,0:T(8,128)}), f32[3072,128]{1,0:T(8,128)}) %all-gather.8.cloned.1.call-update) | async-done | bytes 1572880 | tf_op jit(solution)/shard_map/while/body/eval_jaxpr/all_gather | solution.py:8
  408.2 0.9 constant_dynamic-update-slice_fusion.2
  409.9 73.3 %all-gather.8.cloned.1.call-done = f32[3072,128]{1,0:T(8,128)} async-done(((f32[192,128]{1,0:T(8,128)}), f32[3072,128]{1,0:T(8,128)}) %all-gather.8.cloned.1.call-update) | async-done | bytes 1572880 | tf_op jit(solution)/shard_map/while/body/eval_jaxpr/all_gather | solution.py:8
  483.2 0.9 constant_dynamic-update-slice_fusion.2
  485.0 73.6 %all-gather.8.cloned.1.call-done = f32[3072,128]{1,0:T(8,128)} async-done(((f32[192,128]{1,0:T(8,128)}), f32[3072,128]{1,0:T(8,128)}) %all-gather.8.cloned.1.call-update) | async-done | bytes 1572880 | tf_op jit(solution)/shard_map/while/body/eval_jaxpr/all_gather | solution.py:8
  558.6 0.9 constant_dynamic-update-slice_fusion.2
  560.3 73.6 %all-gather.8.cloned.1.call-done = f32[3072,128]{1,0:T(8,128)} async-done(((f32[192,128]{1,0:T(8,128)}), f32[3072,128]{1,0:T(8,128)}) %all-gather.8.cloned.1.call-update) | async-done | bytes 1572880 | tf_op jit(solution)/shard_map/while/body/eval_jaxpr/all_gather | solution.py:8
  633.9 0.9 constant_dynamic-update-slice_fusion.2
  635.6 73.6 %all-gather.8.cloned.1.call-done = f32[3072,128]{1,0:T(8,128)} async-done(((f32[192,128]{1,0:T(8,128)}), f32[3072,128]{1,0:T(8,128)}) %all-gather.8.cloned.1.call-update) | async-done | bytes 1572880 | tf_op jit(solution)/shard_map/while/body/eval_jaxpr/all_gather | solution.py:8
  711.0 72.0 %all-gather.8.cloned.1.call-done = f32[3072,128]{1,0:T(8,128)} async-done(((f32[192,128]{1,0:T(8,128)}), f32[3072,128]{1,0:T(8,128)}) %all-gather.8.cloned.1.call-update) | async-done | bytes 1572880 | tf_op jit(solution)/shard_map/while/body/eval_jaxpr/all_gather | solution.py:8
  784.7 72.3 %all-gather.8.cloned.1.call-done = f32[3072,128]{1,0:T(8,128)} async-done(((f32[192,128]{1,0:T(8,128)}), f32[3072,128]{1,0:T(8,128)}) %all-gather.8.cloned.1.call-update) | async-done | bytes 1572880 | tf_op jit(solution)/shard_map/while/body/eval_jaxpr/all_gather | solution.py:8
  858.7 72.0 %all-gather.8.cloned.1.call-done = f32[3072,128]{1,0:T(8,128)} async-done(((f32[192,128]{1,0:T(8,128)}), f32[3072,128]{1,0:T(8,128)}) %all-gather.8.cloned.1.call-update) | async-done | bytes 1572880 | tf_op jit(solution)/shard_map/while/body/eval_jaxpr/all_gather | solution.py:8
  932.3 72.3 %all-gather.8.cloned.1.call-done = f32[3072,128]{1,0:T(8,128)} async-done(((f32[192,128]{1,0:T(8,128)}), f32[3072,128]{1,0:T(8,128)}) %all-gather.8.cloned.1.call-update) | async-done | bytes 1572880 | tf_op jit(solution)/shard_map/while/body/eval_jaxpr/all_gather | solution.py:8
  1006.3 72.0 %all-gather.8.cloned.1.call-done = f32[3072,128]{1,0:T(8,128)} async-done(((f32[192,128]{1,0:T(8,128)}), f32[3072,128]{1,0:T(8,128)}) %all-gather.8.cloned.1.call-update) | async-done | bytes 1572880 | tf_op jit(solution)/shard_map/while/body/eval_jaxpr/all_gather | solution.py:8
  1080.0 72.0 %all-gather.8.cloned.1.call-done = f32[3072,128]{1,0:T(8,128)} async-done(((f32[192,128]{1,0:T(8,128)}), f32[3072,128]{1,0:T(8,128)}) %all-gather.8.cloned.1.call-update) | async-done | bytes 1572880 | tf_op jit(solution)/shard_map/while/body/eval_jaxpr/all_gather | solution.py:8
  1153.7 72.0 %all-gather.8.cloned.1.call-done = f32[3072,128]{1,0:T(8,128)} async-done(((f32[192,128]{1,0:T(8,128)}), f32[3072,128]{1,0:T(8,128)}) %all-gather.8.cloned.1.call-update) | async-done | bytes 1572880 | tf_op jit(solution)/shard_map/while/body/eval_jaxpr/all_gather | solution.py:8
  1227.4 55.2 %all-gather.6.cloned.1.call-done = f32[224,2048]{1,0:T(8,128)} async-done(((f32[224,128]{1,0:T(8,128)}), f32[224,2048]{1,0:T(8,128)}) %all-gather.6.cloned.1.call-update) | async-done | bytes 1835024 | tf_op jit(solution)/shard_map/all_gather | solution.py:14
  1282.6 5.8 fusion.3
  1288.4 7.3 all-to-all-start
  1296.5 28.3 %all-to-all-done = f32[16,128,128]{2,1,0:T(8,128)S(1)} async-done(((f32[16,128,128]{2,1,0:T(8,128)}), f32[16,128,128]{2,1,0:T(8,128)S(1)}, u32[]{:S(2)}, u32[]{:S(2)}) %all-to-all-start) | async-done | bytes 1048608 | tf_op jit(solution)/shard_map/all_to_all | solution.py:26
  (154 shorter events, 23.4 us)
Async XLA Ops:
  8.0 22.1 %copy-start.4 = (f32[32]{0:T(128)S(1)}, f32[32]{0:T(128)}, u32[]{:S(2)}) copy-start(f32[32]{0:T(128)} %param.12) | copy-start | bytes 388
  8.0 22.1 %copy-start.2 = (f32[32,128]{1,0:T(8,128)S(1)}, f32[32,128]{1,0:T(8,128)}, u32[]{:S(2)}) copy-start(f32[32,128]{1,0:T(8,128)} %param.11) | copy-start | bytes 49156
  8.0 22.2 %copy-start.3 = (f32[32,192]{1,0:T(8,128)S(1)}, f32[32,192]{1,0:T(8,128)}, u32[]{:S(2)}) copy-start(f32[32,192]{1,0:T(8,128)} %param.10) | copy-start | bytes 73732
  31.3 76.1 %all-gather.8.cloned.1.call-start = ((), (), s32[]{:S(2)}) async-start(), calls=%async_computation.2 | async-start | bytes 1671168 | tf_op jit(solution)/shard_map/while/body/eval_jaxpr/all_gather | solution.py:8
  31.7 0.6 copy-start
  108.4 74.4 %all-gather.8.cloned.1.call-start = ((), (), s32[]{:S(2)}) async-start(), calls=%async_computation.2 | async-start | bytes 1671168 | tf_op jit(solution)/shard_map/while/body/eval_jaxpr/all_gather | solution.py:8
  108.5 0.6 copy-start
  183.8 74.4 %all-gather.8.cloned.1.call-start = ((), (), s32[]{:S(2)}) async-start(), calls=%async_computation.2 | async-start | bytes 1671168 | tf_op jit(solution)/shard_map/while/body/eval_jaxpr/all_gather | solution.py:8
  183.8 0.6 copy-start
  259.1 74.1 %all-gather.8.cloned.1.call-start = ((), (), s32[]{:S(2)}) async-start(), calls=%async_computation.2 | async-start | bytes 1671168 | tf_op jit(solution)/shard_map/while/body/eval_jaxpr/all_gather | solution.py:8
  259.2 0.6 copy-start
  334.1 74.1 %all-gather.8.cloned.1.call-start = ((), (), s32[]{:S(2)}) async-start(), calls=%async_computation.2 | async-start | bytes 1671168 | tf_op jit(solution)/shard_map/while/body/eval_jaxpr/all_gather | solution.py:8
  334.2 0.6 copy-start
  409.2 74.1 %all-gather.8.cloned.1.call-start = ((), (), s32[]{:S(2)}) async-start(), calls=%async_computation.2 | async-start | bytes 1671168 | tf_op jit(solution)/shard_map/while/body/eval_jaxpr/all_gather | solution.py:8
  409.3 0.6 copy-start
  484.2 74.4 %all-gather.8.cloned.1.call-start = ((), (), s32[]{:S(2)}) async-start(), calls=%async_computation.2 | async-start | bytes 1671168 | tf_op jit(solution)/shard_map/while/body/eval_jaxpr/all_gather | solution.py:8
  484.3 0.6 copy-start
  559.5 74.4 %all-gather.8.cloned.1.call-start = ((), (), s32[]{:S(2)}) async-start(), calls=%async_computation.2 | async-start | bytes 1671168 | tf_op jit(solution)/shard_map/while/body/eval_jaxpr/all_gather | solution.py:8
  559.6 0.6 copy-start
  634.9 74.4 %all-gather.8.cloned.1.call-start = ((), (), s32[]{:S(2)}) async-start(), calls=%async_computation.2 | async-start | bytes 1671168 | tf_op jit(solution)/shard_map/while/body/eval_jaxpr/all_gather | solution.py:8
  710.2 72.8 %all-gather.8.cloned.1.call-start = ((), (), s32[]{:S(2)}) async-start(), calls=%async_computation.2 | async-start | bytes 1671168 | tf_op jit(solution)/shard_map/while/body/eval_jaxpr/all_gather | solution.py:8
  783.9 73.0 %all-gather.8.cloned.1.call-start = ((), (), s32[]{:S(2)}) async-start(), calls=%async_computation.2 | async-start | bytes 1671168 | tf_op jit(solution)/shard_map/while/body/eval_jaxpr/all_gather | solution.py:8
  857.9 72.7 %all-gather.8.cloned.1.call-start = ((), (), s32[]{:S(2)}) async-start(), calls=%async_computation.2 | async-start | bytes 1671168 | tf_op jit(solution)/shard_map/while/body/eval_jaxpr/all_gather | solution.py:8
  858.0 0.6 copy-start
  931.6 73.0 %all-gather.8.cloned.1.call-start = ((), (), s32[]{:S(2)}) async-start(), calls=%async_computation.2 | async-start | bytes 1671168 | tf_op jit(solution)/shard_map/while/body/eval_jaxpr/all_gather | solution.py:8
  1005.6 72.7 %all-gather.8.cloned.1.call-start = ((), (), s32[]{:S(2)}) async-start(), calls=%async_computation.2 | async-start | bytes 1671168 | tf_op jit(solution)/shard_map/while/body/eval_jaxpr/all_gather | solution.py:8
  1079.2 72.7 %all-gather.8.cloned.1.call-start = ((), (), s32[]{:S(2)}) async-start(), calls=%async_computation.2 | async-start | bytes 1671168 | tf_op jit(solution)/shard_map/while/body/eval_jaxpr/all_gather | solution.py:8
  1152.9 72.7 %all-gather.8.cloned.1.call-start = ((), (), s32[]{:S(2)}) async-start(), calls=%async_computation.2 | async-start | bytes 1671168 | tf_op jit(solution)/shard_map/while/body/eval_jaxpr/all_gather | solution.py:8
  1226.6 56.0 %all-gather.6.cloned.1.call-start = ((), (), s32[]{:S(2)}) async-start(), calls=%async_computation.1 | async-start | bytes 1949696 | tf_op jit(solution)/shard_map/all_gather | solution.py:14
  1226.6 61.8 %copy-start.1 = (f32[192,128]{1,0:T(8,128)}, f32[192,128]{1,0:T(8,128)S(1)}, u32[]{:S(2)}) copy-start(f32[192,128]{1,0:T(8,128)S(1)} %dynamic-slice_bitcast_fusion) | copy-start | bytes 294916
  1288.4 7.3 slice-start
  1288.4 36.4 %all-to-all-start = ((f32[16,128,128]{2,1,0:T(8,128)}), f32[16,128,128]{2,1,0:T(8,128)S(1)}, u32[]{:S(2)}, u32[]{:S(2)}) async-start(f32[16,128,128]{2,1,0:T(8,128)} %fusion.3), calls=%async_computation | async-start | bytes 2097152 | tf_op jit(solution)/shard_map/all_to_all | solution.py:26
  (7 other events, 4.5 us)
Sparse Core Ops, SparseCore 0:
  34.5 72.9 all-gather.7
  111.6 71.1 all-gather.7
  186.9 71.1 all-gather.7
  262.0 71.1 all-gather.7
  337.0 71.1 all-gather.7
  412.0 71.1 all-gather.7
  487.4 71.1 all-gather.7
  562.7 71.1 all-gather.7
  638.1 71.1 all-gather.7
  713.1 69.8 all-gather.7
  787.1 69.8 all-gather.7
  860.8 69.8 all-gather.7
  934.8 69.8 all-gather.7
  1008.4 69.8 all-gather.7
  1082.1 69.8 all-gather.7
  1155.8 69.8 all-gather.7
Sparse Core Ops, SparseCore 1:
  1229.6 52.9 all-gather.5
where the time goes:
time: 1330 us
  waiting for transfers between devices  1250 us (94%)
  local copies, waits for them, and re-layouts  24.9 us (2%)
  other arithmetic  24.3 us (2%)
  between operations  15.4 us (1%)
    all_gather x16, waiting for transfers between devices, picked(): lax.all_gather(value, axis)  1170 us
    all_gather x1, waiting for transfers between devices, in_one_piece(): whole = lax.all_gather(both, axis, axis=dim, tiled=True)  55.2 us
    all_to_all x1, waiting for transfers between devices, sum_at_owner(): lax.all_to_all(tiles, axis, split_axis=0, concat_axis=0, tiled=True)  28.3 us
  transfers between devices with their start and end apart: 18, of which 18 were waited for; matrix products, arithmetic and copies ran while one was open for 0% of the time, Pallas kernels for 0%

commit v1 on v0

v1 whole, which is shorter than its diff:
```python
import jax
import jax.numpy as jnp
from jax import lax
from jax.experimental import pallas as pl
from jax.experimental.pallas import tpu as pltpu
from jax.sharding import PartitionSpec as P

HIGH = lax.Precision.HIGHEST
BASE = 32


def matern(first_set, second_set):
    differ = first_set[:, :, None] - second_set[:, None, :]
    radius = jnp.sqrt(5.0 * jnp.sum(differ * differ, axis=0))
    return (1.0 + radius + radius * radius / 3.0) * jnp.exp(-radius)


def mm(a, b):
    return jnp.dot(a, b, precision=HIGH, preferred_element_type=jnp.float32)


def invert_kernel(l_ref, d_ref):
    size = l_ref.shape[0]
    count = size // BASE
    rows = lax.broadcasted_iota(jnp.int32, (BASE, BASE), 0)
    cols = lax.broadcasted_iota(jnp.int32, (BASE, BASE), 1)
    strict, solved = [], []
    for k in range(count):
        block = l_ref[k * BASE : (k + 1) * BASE, k * BASE : (k + 1) * BASE]
        diag = jnp.sum(jnp.where(rows == cols, block, 0.0), axis=1, keepdims=True)
        inv = 1.0 / diag
        strict.append(jnp.where(rows > cols, block * inv, 0.0))
        solved.append(jnp.where(rows == cols, inv, 0.0))
    for r in range(BASE - 1):
        for k in range(count):
            solved[k] = solved[k] - strict[k][:, r : r + 1] * solved[k][r : r + 1, :]
    d_ref[...] = jnp.zeros_like(d_ref)
    for k in range(count):
        d_ref[k * BASE : (k + 1) * BASE, k * BASE : (k + 1) * BASE] = solved[k]
    for k in range(0, count - 1, 2):
        a, b, c = k * BASE, (k + 1) * BASE, (k + 2) * BASE
        d_ref[b:c, a:b] = -mm(solved[k + 1], mm(l_ref[b:c, a:b], solved[k]))
    low = 2 * BASE
    while low < size:
        high = low + 2 * BASE
        d_ref[low:high, 0:low] = -mm(
            d_ref[low:high, low:high], mm(l_ref[low:high, 0:low], d_ref[0:low, 0:low])
        )
        low = high


def invert(block):
    return pl.pallas_call(
        invert_kernel, out_shape=jax.ShapeDtypeStruct(block.shape, jnp.float32)
    )(block)


def couple_kernel(d_ref, l_ref, g_ref):
    height = d_ref.shape[0]
    count = l_ref.shape[1] // height
    g_ref[0] = jnp.zeros((height, height), jnp.float32)
    inverse = d_ref[...]
    for k in range(count):
        g_ref[k + 1] = mm(inverse, l_ref[:, k * height : (k + 1) * height])


def couple(inverse, factor):
    height = inverse.shape[0]
    count = factor.shape[1] // height
    return pl.pallas_call(
        couple_kernel,
        out_shape=jax.ShapeDtypeStruct((count + 1, height, height), jnp.float32),
    )(inverse, factor)


def spread(value, axis, size, groups=None):
    copies = jnp.broadcast_to(value[None], (size,) + value.shape)
    return lax.all_to_all(copies, axis, 0, 0, axis_index_groups=groups, tiled=True)


def shards(archive_inputs, candidate_inputs, lengthscales, factor):
    height = factor.shape[0]
    chain = lax.axis_size("chain")
    cand = lax.axis_size("cand")
    quad = 4
    quads = chain // quad
    position = lax.axis_index("chain")
    scaling = 1.0 / lengthscales
    scaled_archive = archive_inputs * scaling[:, None]
    scaled_candidates = candidate_inputs * scaling[:, None]

    swap = [(a * cand + b, b * cand + a) for a in range(chain) for b in range(cand)]
    chosen = lax.ppermute(candidate_inputs, ("chain", "cand"), swap)
    own = lax.dynamic_slice_in_dim(factor, position * height, height, 1)
    inverse = invert(own)
    blocks = couple(inverse, factor)
    rows = mm(inverse, matern(scaled_archive, scaled_candidates))

    for t in range(chain - 1):
        near = [(t - k, t + 1 + k) for k in range(chain) if t - k >= 0 and t + 1 + k < chain]
        far = [(t - k, t + 2 + k) for k in range(chain) if t - k >= 0 and t + 2 + k < chain]
        first = lax.ppermute(rows, "chain", near)
        index = 2 * t + 2 - position
        step = mm(lax.dynamic_index_in_dim(blocks, index, 0, keepdims=False), first)
        if far:
            second = lax.ppermute(rows, "chain", far)
            step = step + mm(lax.dynamic_index_in_dim(blocks, index + 1, 0, keepdims=False), second)
        rows = rows - step

    turn = [
        ((quad * g + j) * cand + quad * m + i, (quad * g + i) * cand + quad * j + m)
        for g in range(quads)
        for i in range(quad)
        for j in range(quad)
        for m in range(cand // quad)
    ]
    turned = lax.ppermute(rows, ("chain", "cand"), turn)
    inside = [[quad * g + i for i in range(quad)] for g in range(quads)]
    across = [[quad * g + i for g in range(quads)] for i in range(quad)]
    mine = spread(rows, "chain", quad, inside)
    others = spread(turned, "cand", cand)
    width = rows.shape[1]
    others = others.reshape(quad, cand // quad, height, width)
    shares = jnp.einsum(
        "jmra,jrb->mab", others, mine, precision=HIGH, preferred_element_type=jnp.float32
    )
    shared = lax.all_to_all(shares, "chain", 0, 0, axis_index_groups=across, tiled=True).sum(axis=0)
    prior_cov = matern(chosen * scaling[:, None], scaled_candidates)
    return (rows, prior_cov - shared)


def solution(mesh):
    return jax.shard_map(
        shards,
        mesh=mesh,
        in_specs=(P(None, "chain"), P(None, "cand"), P(), P("chain", None)),
        out_specs=(P("chain", "cand"), P("chain", "cand")),
        check_vma=False,
    )
```

time: 1330 us -> 230 us (0.17)
  waiting for transfers between devices: 1250 us -> 37 us
  starting transfers between devices: 7.97 us -> 120 us
  blocking collectives: 0 us -> 28.4 us
  local copies, waits for them, and re-layouts: 24.9 us -> 2.71 us
  other arithmetic: 24.3 us -> 5.24 us
  matrix products: 7.1 us -> 22.1 us
  between operations: 15.4 us -> 1.34 us
    all_gather x17 -> x0, waiting for transfers between devices: 1220 us -> none  [the longest x16 1170 us: picked(): lax.all_gather(value, axis)]
    all_to_all x1 -> x2, starting transfers between devices: 7.27 us -> 83.6 us  [the longest x1 56.6 us: shards(): lax.all_to_all(shares, 'chain', 0, 0, axis_index_groups=across, tiled=True)]
    ppermute x0 -> x31, starting transfers between devices: none -> 36.5 us  [the longest x15 16.9 us: shards(): first = lax.ppermute(rows, 'chain', near)]
    all_to_all x0 -> x1, blocking collectives: none -> 28.4 us  [spread(): lax.all_to_all(copies, axis, 0, 0, axis_index_groups=groups, tiled=True)]
    ppermute x0 -> x31, waiting for transfers between devices: none -> 26.2 us  [the longest x1 9.09 us: shards(): turned = lax.ppermute(rows, ('chain', 'cand'), turn)]
    another operation x7 -> x0, other arithmetic: 20.9 us -> none  [shards(): jax.scipy.linalg.solve_triangular(own_diagonal, jnp.eye(height, dtype=jnp...]
    all_to_all x1 -> x2, waiting for transfers between devices: 28.3 us -> 10.7 us  [the longest x1 10.7 us: shards(): lax.all_to_all(shares, 'chain', 0, 0, axis_index_groups=across, tiled=True)]
    dot_general x2 -> x31, matrix products: 6.16 us -> 22.1 us  [the longest x30 18.8 us: mm(): return jnp.dot(a, b, precision=HIGH, preferred_element_type=jnp.float32)]
  transfers between devices with their start and end apart: 18 -> 33, of which waited for: 18 -> 15; matrix products, arithmetic and copies ran while one was open for 0% -> 5% of each run, Pallas kernels for 0% -> 4%
where the time goes in v1:
time: 230 us; the launch traced here: 227 us
  starting transfers between devices  120 us (52%)
  waiting for transfers between devices  37 us (16%)
  blocking collectives  28.4 us (12%)
  matrix products  22.1 us (10%)
  Pallas kernels  10.1 us (4%)
  other arithmetic  5.24 us (2%)
  local copies, waits for them, and re-layouts  2.71 us (1%)
    all_to_all x1, starting transfers between devices, shards(): lax.all_to_all(shares, 'chain', 0, 0, axis_index_groups=across, tiled=True)  56.6 us
    all_to_all x1, blocking collectives, spread(): lax.all_to_all(copies, axis, 0, 0, axis_index_groups=groups, tiled=True)  28.4 us
    all_to_all x1, starting transfers between devices, spread(): lax.all_to_all(copies, axis, 0, 0, axis_index_groups=groups, tiled=True)  27 us
    dot_general x30, matrix products, mm(): return jnp.dot(a, b, precision=HIGH, preferred_element_type=jnp.float32)  18.8 us
    ppermute x15, starting transfers between devices, shards(): first = lax.ppermute(rows, 'chain', near)  16.9 us
    ppermute x14, starting transfers between devices, shards(): second = lax.ppermute(rows, 'chain', far)  13.8 us
    all_to_all x1, waiting for transfers between devices, shards(): lax.all_to_all(shares, 'chain', 0, 0, axis_index_groups=across, tiled=True)  10.7 us
    ppermute x1, waiting for transfers between devices, shards(): turned = lax.ppermute(rows, ('chain', 'cand'), turn)  9.09 us
  transfers between devices with their start and end apart: 33, of which 15 were waited for; matrix products, arithmetic and copies ran while one was open for 5% of the time, Pallas kernels for 4%

profile of v1, /device:TPU:2, one launch (start us, length us, event | category | flops | bytes accessed | tf_op | source)
XLA Modules:
  0.0 227.0 jit_solution(11763633108108582135)
XLA Ops:
  0.6 3.8 %collective-permute-start.29 = (f32[32,128]{1,0:T(8,128)}, f32[32,128]{1,0:T(8,128)S(1)}, u32[]{:S(2)}, u32[]{:S(2)}) collective-permute-start(f32[32,128]{1,0:T(8,128)} %param.5), channel_id=1, source_target_pairs={{0,0},{1,16},{2,32},{3,48},{4,64},{5,80},{6,96},{7,112},{8,128},{9... | collective-permute-start | bytes 49160 | tf_op jit(solution)/shard_map/ppermute | solution.py:93
  5.9 1.8 constant_dynamic-slice_fusion.l_ref
  7.7 3.9 %shard_map.59.d_ref = f32[192,192]{1,0:T(8,128)} custom-call(f32[192,192]{1,0:T(8,128)} %constant_dynamic-slice_fusion.l_ref), custom_call_target="tpu_custom_call" | custom-call | tf_op jit(solution)/shard_map/pallas_call | solution.py:53
  11.6 1.4 broadcast_multiply_fusion.1
  15.3 1.4 collective-permute-start.1
  16.7 6.2 %shard_map.60 = f32[17,192,192]{2,1,0:T(8,128)} custom-call(f32[192,192]{1,0:T(8,128)} %shard_map.59.d_ref, f32[192,3072]{1,0:T(8,128)} %l_ref.1), custom_call_target="tpu_custom_call" | custom-call | tf_op jit(solution)/shard_map/pallas_call | solution.py:70
  22.9 2.3 %collective-permute-start = (f32[192,128]{1,0:T(8,128)S(1)}, f32[192,128]{1,0:T(8,128)S(1)}, u32[]{:S(2)}, u32[]{:S(2)}) collective-permute-start(f32[192,128]{1,0:T(8,128)S(1)} %fusion.87), channel_id=1, source_target_pairs={{0,16},{1,17},{2,18},{3,19},{4,20},{5,21},{6,22},{7,23},{8,24},{9,... | collective-permute-start | bytes 294920 | tf_op jit(solution)/shard_map/ppermute | solution.py:102
  26.5 1.4 collective-permute-done
  29.2 1.3 collective-permute-start.3
  30.5 1.3 collective-permute-start.2
  31.8 1.8 collective-permute-done.3
  36.9 1.3 collective-permute-start.5
  38.2 1.3 collective-permute-start.4
  39.5 1.8 collective-permute-done.5
  44.1 1.3 collective-permute-start.7
  45.4 1.3 collective-permute-start.6
  46.7 1.8 collective-permute-done.7
  50.1 1.3 collective-permute-start.9
  51.4 1.3 collective-permute-start.8
  55.2 1.3 collective-permute-start.11
  56.5 1.3 collective-permute-start.10
  60.5 1.3 collective-permute-start.13
  64.6 1.8 collective-permute-done.12
  69.0 2.4 %collective-permute-done.14 = f32[192,128]{1,0:T(8,128)S(1)} collective-permute-done((f32[192,128]{1,0:T(8,128)S(1)}, f32[192,128]{1,0:T(8,128)S(1)}, u32[]{:S(2)}, u32[]{:S(2)}) %collective-permute-start.14) | collective-permute-done | bytes 98336 | tf_op jit(solution)/shard_map/ppermute | solution.py:102
  85.0 1.3 collective-permute-start.28
  88.3 27.0 %all-to-all-start.1 = ((f32[4,192,128]{2,1,0:T(8,128)}), f32[4,192,128]{2,1,0:T(8,128)S(1)}, u32[]{:S(2)}, u32[]{:S(2)}) async-start(f32[4,192,128]{2,1,0:T(8,128)} %broadcast_in_dim.5), calls=%async_computation.1 | async-start | bytes 786432 | tf_op jit(solution)/shard_map/all_to_all | solution.py:78
  115.3 2.0 collective-permute-start.30
  117.3 9.1 %collective-permute-done.30 = f32[192,128]{1,0:T(8,128)S(1)} collective-permute-done((f32[192,128]{1,0:T(8,128)S(1)}, f32[192,128]{1,0:T(8,128)S(1)}, u32[]{:S(2)}, u32[]{:S(2)}) %collective-permute-start.30) | collective-permute-done | bytes 98336 | tf_op jit(solution)/shard_map/ppermute | solution.py:117
  126.6 28.4 %all_to_all.15 = f32[16,192,128]{2,1,0:T(8,128)S(1)} all-to-all(f32[16,192,128]{2,1,0:T(8,128)S(1)} %broadcast_in_dim.4), channel_id=1, replica_groups=mesh['chain'=16,'cand'=16] {'cand'}, dimensions={0} | all-to-all | bytes 3145728 | tf_op jit(solution)/shard_map/all_to_all | solution.py:78
  155.0 3.3 %convolution_bitcast_fusion = f32[4,128,128]{2,1,0:T(8,128)} fusion(f32[4,4,192,128]{3,2,1,0:T(8,128)S(1)} %bitcast.126, f32[4,192,128]{2,1,0:T(8,128)S(1)} %all-to-all-done.1), kind=kOutput, calls=%fused_computation.2 | convolution fusion | flops 603979776 | bytes 2228224 | tf_op jit(solution)/shard_map/jmra,jrb->mab/dot_general | solution.py:124
  158.3 56.6 %all-to-all-start.2 = ((f32[4,128,128]{2,1,0:T(8,128)}), f32[4,128,128]{2,1,0:T(8,128)S(1)}, u32[]{:S(2)}, u32[]{:S(2)}) async-start(f32[4,128,128]{2,1,0:T(8,128)} %convolution_bitcast_fusion), calls=%async_computation.2 | async-start | bytes 524288 | tf_op jit(solution)/shard_map/all_to_all | solution.py:127
  215.6 10.7 %all-to-all-done.2 = f32[4,128,128]{2,1,0:T(8,128)S(1)} async-done(((f32[4,128,128]{2,1,0:T(8,128)}), f32[4,128,128]{2,1,0:T(8,128)S(1)}, u32[]{:S(2)}, u32[]{:S(2)}) %all-to-all-start.2) | async-done | bytes 262176 | tf_op jit(solution)/shard_map/all_to_all | solution.py:127
  (86 shorter events, 41.1 us)
Async XLA Ops:
  0.6 11.0 %collective-permute-start.29 = (f32[32,128]{1,0:T(8,128)}, f32[32,128]{1,0:T(8,128)S(1)}, u32[]{:S(2)}, u32[]{:S(2)}) collective-permute-start(f32[32,128]{1,0:T(8,128)} %param.5), channel_id=1, source_target_pairs={{0,0},{1,16},{2,32},{3,48},{4,64},{5,80},{6,96},{7,112},{8,128},{9... | collective-permute-start | bytes 49160 | tf_op jit(solution)/shard_map/ppermute | solution.py:93
  15.3 10.0 %collective-permute-start.1 = (f32[192,128]{1,0:T(8,128)S(1)}, f32[192,128]{1,0:T(8,128)S(1)}, u32[]{:S(2)}, u32[]{:S(2)}) collective-permute-start(f32[192,128]{1,0:T(8,128)S(1)} %fusion.87), channel_id=1, source_target_pairs={{0,32},{1,33},{2,34},{3,35},{4,36},{5,37},{6,38},{7,39},{8,40},{9,... | collective-permute-start | bytes 294920 | tf_op jit(solution)/shard_map/ppermute | solution.py:106
  22.9 5.0 %collective-permute-start = (f32[192,128]{1,0:T(8,128)S(1)}, f32[192,128]{1,0:T(8,128)S(1)}, u32[]{:S(2)}, u32[]{:S(2)}) collective-permute-start(f32[192,128]{1,0:T(8,128)S(1)} %fusion.87), channel_id=1, source_target_pairs={{0,16},{1,17},{2,18},{3,19},{4,20},{5,21},{6,22},{7,23},{8,24},{9,... | collective-permute-start | bytes 294920 | tf_op jit(solution)/shard_map/ppermute | solution.py:102
  29.2 4.5 %collective-permute-start.3 = (f32[192,128]{1,0:T(8,128)S(1)}, f32[192,128]{1,0:T(8,128)S(1)}, u32[]{:S(2)}, u32[]{:S(2)}) collective-permute-start(f32[192,128]{1,0:T(8,128)S(1)} %fusion.13), channel_id=1, source_target_pairs={{16,48},{0,64},{17,49},{1,65},{18,50},{2,66},{19,51},{3,67},{20,52... | collective-permute-start | bytes 294920 | tf_op jit(solution)/shard_map/ppermute | solution.py:106
  30.5 5.2 %collective-permute-start.2 = (f32[192,128]{1,0:T(8,128)S(1)}, f32[192,128]{1,0:T(8,128)S(1)}, u32[]{:S(2)}, u32[]{:S(2)}) collective-permute-start(f32[192,128]{1,0:T(8,128)S(1)} %fusion.13), channel_id=1, source_target_pairs={{16,32},{0,48},{17,33},{1,49},{18,34},{2,50},{19,35},{3,51},{20,36... | collective-permute-start | bytes 294920 | tf_op jit(solution)/shard_map/ppermute | solution.py:102
  36.9 4.5 %collective-permute-start.5 = (f32[192,128]{1,0:T(8,128)S(1)}, f32[192,128]{1,0:T(8,128)S(1)}, u32[]{:S(2)}, u32[]{:S(2)}) collective-permute-start(f32[192,128]{1,0:T(8,128)S(1)} %fusion.12), channel_id=1, source_target_pairs={{32,64},{16,80},{0,96},{33,65},{17,81},{1,97},{34,66},{18,82},{2,9... | collective-permute-start | bytes 294920 | tf_op jit(solution)/shard_map/ppermute | solution.py:106
  38.2 4.6 %collective-permute-start.4 = (f32[192,128]{1,0:T(8,128)S(1)}, f32[192,128]{1,0:T(8,128)S(1)}, u32[]{:S(2)}, u32[]{:S(2)}) collective-permute-start(f32[192,128]{1,0:T(8,128)S(1)} %fusion.12), channel_id=1, source_target_pairs={{32,48},{16,64},{0,80},{33,49},{17,65},{1,81},{34,50},{18,66},{2,8... | collective-permute-start | bytes 294920 | tf_op jit(solution)/shard_map/ppermute | solution.py:102
  44.1 4.4 %collective-permute-start.7 = (f32[192,128]{1,0:T(8,128)S(1)}, f32[192,128]{1,0:T(8,128)S(1)}, u32[]{:S(2)}, u32[]{:S(2)}) collective-permute-start(f32[192,128]{1,0:T(8,128)S(1)} %fusion.11), channel_id=1, source_target_pairs={{48,80},{32,96},{16,112},{0,128},{49,81},{33,97},{17,113},{1,129},... | collective-permute-start | bytes 294920 | tf_op jit(solution)/shard_map/ppermute | solution.py:106
  45.4 4.4 %collective-permute-start.6 = (f32[192,128]{1,0:T(8,128)S(1)}, f32[192,128]{1,0:T(8,128)S(1)}, u32[]{:S(2)}, u32[]{:S(2)}) collective-permute-start(f32[192,128]{1,0:T(8,128)S(1)} %fusion.11), channel_id=1, source_target_pairs={{48,64},{32,80},{16,96},{0,112},{49,65},{33,81},{17,97},{1,113},{5... | collective-permute-start | bytes 294920 | tf_op jit(solution)/shard_map/ppermute | solution.py:102
  50.1 3.5 %collective-permute-start.9 = (f32[192,128]{1,0:T(8,128)S(1)}, f32[192,128]{1,0:T(8,128)S(1)}, u32[]{:S(2)}, u32[]{:S(2)}) collective-permute-start(f32[192,128]{1,0:T(8,128)S(1)} %fusion.10), channel_id=1, source_target_pairs={{64,96},{48,112},{32,128},{16,144},{0,160},{65,97},{49,113},{33,12... | collective-permute-start | bytes 294920 | tf_op jit(solution)/shard_map/ppermute | solution.py:106
  51.4 3.5 %collective-permute-start.8 = (f32[192,128]{1,0:T(8,128)S(1)}, f32[192,128]{1,0:T(8,128)S(1)}, u32[]{:S(2)}, u32[]{:S(2)}) collective-permute-start(f32[192,128]{1,0:T(8,128)S(1)} %fusion.10), channel_id=1, source_target_pairs={{64,80},{48,96},{32,112},{16,128},{0,144},{65,81},{49,97},{33,113}... | collective-permute-start | bytes 294920 | tf_op jit(solution)/shard_map/ppermute | solution.py:102
  55.2 3.5 %collective-permute-start.11 = (f32[192,128]{1,0:T(8,128)S(1)}, f32[192,128]{1,0:T(8,128)S(1)}, u32[]{:S(2)}, u32[]{:S(2)}) collective-permute-start(f32[192,128]{1,0:T(8,128)S(1)} %fusion.9), channel_id=1, source_target_pairs={{80,112},{64,128},{48,144},{32,160},{16,176},{0,192},{81,113},{65,... | collective-permute-start | bytes 294920 | tf_op jit(solution)/shard_map/ppermute | solution.py:106
  56.5 3.6 %collective-permute-start.10 = (f32[192,128]{1,0:T(8,128)S(1)}, f32[192,128]{1,0:T(8,128)S(1)}, u32[]{:S(2)}, u32[]{:S(2)}) collective-permute-start(f32[192,128]{1,0:T(8,128)S(1)} %fusion.9), channel_id=1, source_target_pairs={{80,96},{64,112},{48,128},{32,144},{16,160},{0,176},{81,97},{65,11... | collective-permute-start | bytes 294920 | tf_op jit(solution)/shard_map/ppermute | solution.py:102
  60.5 3.8 %collective-permute-start.13 = (f32[192,128]{1,0:T(8,128)S(1)}, f32[192,128]{1,0:T(8,128)S(1)}, u32[]{:S(2)}, u32[]{:S(2)}) collective-permute-start(f32[192,128]{1,0:T(8,128)S(1)} %fusion.8), channel_id=1, source_target_pairs={{96,128},{80,144},{64,160},{48,176},{32,192},{16,208},{0,224},{97,... | collective-permute-start | bytes 294920 | tf_op jit(solution)/shard_map/ppermute | solution.py:106
  61.8 4.6 %collective-permute-start.12 = (f32[192,128]{1,0:T(8,128)S(1)}, f32[192,128]{1,0:T(8,128)S(1)}, u32[]{:S(2)}, u32[]{:S(2)}) collective-permute-start(f32[192,128]{1,0:T(8,128)S(1)} %fusion.8), channel_id=1, source_target_pairs={{96,112},{80,128},{64,144},{48,160},{32,176},{16,192},{0,208},{97,... | collective-permute-start | bytes 294920 | tf_op jit(solution)/shard_map/ppermute | solution.py:102
  66.7 2.0 collective-permute-start.15
  67.4 4.0 %collective-permute-start.14 = (f32[192,128]{1,0:T(8,128)S(1)}, f32[192,128]{1,0:T(8,128)S(1)}, u32[]{:S(2)}, u32[]{:S(2)}) collective-permute-start(f32[192,128]{1,0:T(8,128)S(1)} %fusion.7), channel_id=1, source_target_pairs={{112,128},{96,144},{80,160},{64,176},{48,192},{32,208},{16,224},{0... | collective-permute-start | bytes 294920 | tf_op jit(solution)/shard_map/ppermute | solution.py:102
  71.7 1.4 collective-permute-start.17
  72.4 1.0 collective-permute-start.16
  73.7 1.5 collective-permute-start.19
  74.4 1.2 collective-permute-start.18
  75.9 1.4 collective-permute-start.21
  76.6 1.0 collective-permute-start.20
  78.0 1.4 collective-permute-start.23
  80.0 1.4 collective-permute-start.25
  80.7 1.0 collective-permute-start.24
  82.0 1.4 collective-permute-start.27
  82.7 1.0 collective-permute-start.26
  85.0 1.3 collective-permute-start.28
  88.3 38.1 %all-to-all-start.1 = ((f32[4,192,128]{2,1,0:T(8,128)}), f32[4,192,128]{2,1,0:T(8,128)S(1)}, u32[]{:S(2)}, u32[]{:S(2)}) async-start(f32[4,192,128]{2,1,0:T(8,128)} %broadcast_in_dim.5), calls=%async_computation.1 | async-start | bytes 786432 | tf_op jit(solution)/shard_map/all_to_all | solution.py:78
  115.3 11.1 %collective-permute-start.30 = (f32[192,128]{1,0:T(8,128)S(1)}, f32[192,128]{1,0:T(8,128)S(1)}, u32[]{:S(2)}, u32[]{:S(2)}) collective-permute-start(f32[192,128]{1,0:T(8,128)S(1)} %convolution_subtract_fusion), channel_id=1, source_target_pairs={{0,0},{4,1},{8,2},{12,3},{16,4},{20,5},{24,6},{28,7},{32,8},{36,9}... | collective-permute-start | bytes 294920 | tf_op jit(solution)/shard_map/ppermute | solution.py:117
  158.3 68.0 %all-to-all-start.2 = ((f32[4,128,128]{2,1,0:T(8,128)}), f32[4,128,128]{2,1,0:T(8,128)S(1)}, u32[]{:S(2)}, u32[]{:S(2)}) async-start(f32[4,128,128]{2,1,0:T(8,128)} %convolution_bitcast_fusion), calls=%async_computation.2 | async-start | bytes 524288 | tf_op jit(solution)/shard_map/all_to_all | solution.py:127
  (5 other events, 188.8 us)

commit v2 on v1

v2 whole, which is shorter than its diff:
```python
import jax
import jax.numpy as jnp
from jax import lax
from jax.experimental import pallas as pl
from jax.experimental.pallas import tpu as pltpu
from jax.sharding import PartitionSpec as P

HIGH = lax.Precision.HIGHEST
BASE = 32
QUAD = 4


def matern(first_set, second_set):
    differ = first_set[:, :, None] - second_set[:, None, :]
    radius = jnp.sqrt(5.0 * jnp.sum(differ * differ, axis=0))
    return (1.0 + radius + radius * radius / 3.0) * jnp.exp(-radius)


def mm(a, b):
    return jnp.dot(a, b, precision=HIGH, preferred_element_type=jnp.float32)


def invert_into(l_ref, d_ref):
    size = l_ref.shape[0]
    count = size // BASE
    rows = lax.broadcasted_iota(jnp.int32, (BASE, BASE), 0)
    cols = lax.broadcasted_iota(jnp.int32, (BASE, BASE), 1)
    strict, solved = [], []
    for k in range(count):
        block = l_ref[k * BASE : (k + 1) * BASE, k * BASE : (k + 1) * BASE]
        diag = jnp.sum(jnp.where(rows == cols, block, 0.0), axis=1, keepdims=True)
        inv = 1.0 / diag
        strict.append(jnp.where(rows > cols, block * inv, 0.0))
        solved.append(jnp.where(rows == cols, inv, 0.0))
    for r in range(BASE - 1):
        for k in range(count):
            solved[k] = solved[k] - strict[k][:, r : r + 1] * solved[k][r : r + 1, :]
    d_ref[...] = jnp.zeros_like(d_ref)
    for k in range(count):
        d_ref[k * BASE : (k + 1) * BASE, k * BASE : (k + 1) * BASE] = solved[k]
    for k in range(0, count - 1, 2):
        a, b, c = k * BASE, (k + 1) * BASE, (k + 2) * BASE
        d_ref[b:c, a:b] = -mm(solved[k + 1], mm(l_ref[b:c, a:b], solved[k]))
    low = 2 * BASE
    while low < size:
        high = low + 2 * BASE
        d_ref[low:high, 0:low] = -mm(
            d_ref[low:high, low:high], mm(l_ref[low:high, 0:low], d_ref[0:low, 0:low])
        )
        low = high


def first_kernel(where_ref, near_ref, last_ref, cross_ref, out_ref, d_ref, l_ref):
    height, width = cross_ref.shape
    member = where_ref[1]
    own = near_ref[:, 0:height]
    for k in range(1, QUAD):
        own = jnp.where(member == k, near_ref[:, k * height : (k + 1) * height], own)
    l_ref[...] = own
    invert_into(l_ref, d_ref)
    inverse = d_ref[...]
    inner = (QUAD - 1) * height
    column = lax.broadcasted_iota(jnp.int32, (height, inner), 1)
    scaled = mm(inverse, near_ref[:, 0:inner])
    scaled = jnp.where(column < member * height, scaled, 0.0)
    panel = mm(inverse, cross_ref[...])
    before = mm(inverse, last_ref[...])
    for j in range(QUAD):
        out_ref[j, :, 0:width] = panel
        out_ref[j, :, width : width + inner] = scaled
        out_ref[j, :, width + inner :] = before[:, j * height : (j + 1) * height]


def first(where, factor, cross):
    height, width = cross.shape
    span = QUAD * height
    return pl.pallas_call(
        first_kernel,
        grid_spec=pltpu.PrefetchScalarGridSpec(
            num_scalar_prefetch=1,
            grid=(1,),
            in_specs=[
                pl.BlockSpec((height, span), lambda _, s: (0, s[0])),
                pl.BlockSpec((height, span), lambda _, s: (0, jnp.maximum(s[0] - 1, 0))),
                pl.BlockSpec((height, width), lambda _, s: (0, 0)),
            ],
            out_specs=[
                pl.BlockSpec((QUAD, height, width + span), lambda _, s: (0, 0, 0)),
                pl.BlockSpec((height, height), lambda _, s: (0, 0)),
            ],
            scratch_shapes=[pltpu.VMEM((height, height), jnp.float32)],
        ),
        out_shape=[
            jax.ShapeDtypeStruct((QUAD, height, width + span), jnp.float32),
            jax.ShapeDtypeStruct((height, height), jnp.float32),
        ],
    )(where, factor, factor, cross)


def older_kernel(where_ref, d_ref, two_ref, three_ref, out_ref):
    height = d_ref.shape[0]
    inverse = d_ref[...]
    two = mm(inverse, two_ref[...])
    three = mm(inverse, three_ref[...])
    for j in range(QUAD):
        out_ref[j, :, 0:height] = two[:, j * height : (j + 1) * height]
        out_ref[j, :, height:] = three[:, j * height : (j + 1) * height]


def older(where, inverse, factor):
    height = inverse.shape[0]
    span = QUAD * height
    return pl.pallas_call(
        older_kernel,
        grid_spec=pltpu.PrefetchScalarGridSpec(
            num_scalar_prefetch=1,
            grid=(1,),
            in_specs=[
                pl.BlockSpec((height, height), lambda _, s: (0, 0)),
                pl.BlockSpec((height, span), lambda _, s: (0, jnp.maximum(s[0] - 2, 0))),
                pl.BlockSpec((height, span), lambda _, s: (0, jnp.maximum(s[0] - 3, 0))),
            ],
            out_specs=pl.BlockSpec((QUAD, height, 2 * height), lambda _, s: (0, 0, 0)),
        ),
        out_shape=jax.ShapeDtypeStruct((QUAD, height, 2 * height), jnp.float32),
    )(where, inverse, factor, factor)


def join_kernel(where_ref, got_ref, base_ref, last_ref):
    height, width = base_ref.shape
    inner = (QUAD - 1) * height
    member = where_ref[1]
    base = got_ref[0, :, 0:width]
    panels, lasts = [base], [got_ref[0, :, width + inner :]]
    last_ref[0:height, :] = lasts[0]
    for i in range(1, QUAD):
        scaled = got_ref[i, :, width : width + i * height]
        panel = got_ref[i, :, 0:width] - mm(scaled, jnp.concatenate(panels, axis=0))
        last = got_ref[i, :, width + inner :] - mm(scaled, last_ref[0 : i * height, :])
        panels.append(panel)
        last_ref[i * height : (i + 1) * height, :] = last
        base = jnp.where(member == i, panel, base)
    base_ref[...] = base


def join(where, got, width):
    height = got.shape[1]
    return pl.pallas_call(
        join_kernel,
        grid_spec=pltpu.PrefetchScalarGridSpec(
            num_scalar_prefetch=1,
            grid=(1,),
            in_specs=[pl.BlockSpec(got.shape, lambda _, s: (0, 0, 0))],
            out_specs=[
                pl.BlockSpec((height, width), lambda _, s: (0, 0)),
                pl.BlockSpec((QUAD * height, height), lambda _, s: (0, 0)),
            ],
        ),
        out_shape=[
            jax.ShapeDtypeStruct((height, width), jnp.float32),
            jax.ShapeDtypeStruct((QUAD * height, height), jnp.float32),
        ],
    )(where, got)


def join_older_kernel(got_ref, more_ref, out_ref):
    height = got_ref.shape[1]
    width = got_ref.shape[2] - QUAD * height
    out_ref[0:height, :] = more_ref[0]
    for i in range(1, QUAD):
        scaled = got_ref[i, :, width : width + i * height]
        out_ref[i * height : (i + 1) * height, :] = more_ref[i] - mm(scaled, out_ref[0 : i * height, :])


def join_older(got, more):
    height = got.shape[1]
    return pl.pallas_call(
        join_older_kernel,
        out_shape=jax.ShapeDtypeStruct((QUAD * height, 2 * height), jnp.float32),
    )(got, more)


def shards(archive_inputs, candidate_inputs, lengthscales, factor):
    height = factor.shape[0]
    width = candidate_inputs.shape[1]
    chain = lax.axis_size("chain")
    cand = lax.axis_size("cand")
    quads = chain // QUAD
    position = lax.axis_index("chain")
    group = position // QUAD
    where = jnp.stack([group, position % QUAD]).astype(jnp.int32)
    inside = [[QUAD * g + i for i in range(QUAD)] for g in range(quads)]
    across = [[QUAD * g + i for g in range(quads)] for i in range(QUAD)]
    scaling = 1.0 / lengthscales
    scaled_archive = archive_inputs * scaling[:, None]
    scaled_candidates = candidate_inputs * scaling[:, None]

    swap = [(a * cand + b, b * cand + a) for a in range(chain) for b in range(cand)]
    chosen = lax.ppermute(candidate_inputs, ("chain", "cand"), swap)
    sent, inverse = first(where, factor, matern(scaled_archive, scaled_candidates))
    got = lax.all_to_all(sent, "chain", 0, 0, axis_index_groups=inside, tiled=True)
    more = lax.all_to_all(
        older(where, inverse, factor), "chain", 0, 0, axis_index_groups=inside, tiled=True
    )
    base, last = join(where, got, width)
    earlier = join_older(got, more)
    two, three = earlier[:, 0:height], earlier[:, height:]
    mixed = jnp.where(group == 3, three, last)

    def shift(value, *hops):
        pairs = [(QUAD * a + i, QUAD * b + i) for a, b in hops for i in range(QUAD)]
        return lax.ppermute(value, "chain", pairs)

    def settle(total):
        parts = total.reshape(QUAD, height, width)
        parts = lax.all_to_all(parts, "chain", 0, 0, axis_index_groups=inside, tiled=True)
        return base - parts.sum(axis=0)

    rows = base
    total = mm(last, shift(rows, (0, 1)))
    ahead = shift(rows, (0, 2))
    rows = settle(total)
    total = total + mm(two, ahead) + mm(mixed, shift(rows, (1, 2), (0, 3)))
    ahead = shift(rows, (1, 3))
    rows = settle(total)
    total = total + mm(two, ahead) + mm(last, shift(rows, (2, 3)))
    rows = settle(total)

    turn = [
        ((QUAD * g + (i ^ j)) * cand + QUAD * m + i, (QUAD * g + i) * cand + QUAD * j + m)
        for g in range(quads)
        for i in range(QUAD)
        for j in range(QUAD)
        for m in range(cand // QUAD)
    ]
    turned = lax.ppermute(rows, ("chain", "cand"), turn)
    mine = [rows]
    for r in range(1, QUAD):
        pairs = [(QUAD * g + i, QUAD * g + (i ^ r)) for g in range(quads) for i in range(QUAD)]
        mine.append(lax.ppermute(rows, "chain", pairs))
    copies = jnp.broadcast_to(turned[None], (cand,) + turned.shape)
    others = lax.all_to_all(copies, "cand", 0, 0, tiled=True)
    others = others.reshape(QUAD, cand // QUAD, height, width)
    shares = jnp.einsum(
        "jmra,jrb->mab", others, jnp.stack(mine), precision=HIGH, preferred_element_type=jnp.float32
    )
    shared = lax.all_to_all(shares, "chain", 0, 0, axis_index_groups=across, tiled=True).sum(axis=0)
    prior_cov = matern(chosen * scaling[:, None], scaled_candidates)
    return (rows, prior_cov - shared)


def solution(mesh):
    return jax.shard_map(
        shards,
        mesh=mesh,
        in_specs=(P(None, "chain"), P(None, "cand"), P(), P("chain", None)),
        out_specs=(P("chain", "cand"), P("chain", "cand")),
        check_vma=False,
    )
```

time: 230 us -> 204 us (0.89)
  starting transfers between devices: 120 us -> 55.7 us
  blocking collectives: 28.4 us -> 55.9 us
  Pallas kernels: 10.1 us -> 23.2 us
  waiting for transfers between devices: 37 us -> 47.8 us
  matrix products: 22.1 us -> 11.4 us
    all_to_all x1, starting transfers between devices: 56.6 us -> 13.6 us  [shards(): lax.all_to_all(shares, 'chain', 0, 0, axis_index_groups=across, tiled=True)]
    all_to_all x1 -> x3, blocking collectives: 28.4 us -> 55.9 us  [the longest x1 37.6 us: shards(): lax.all_to_all(sent, 'chain', 0, 0, axis_index_groups=inside, tiled=True)]
    pallas_call x2 -> x4, Pallas kernels: 10.1 us -> 23.2 us  [the longest x1 7.78 us: first(): pl.pallas_call(first_kernel, grid_spec=pltpu.PrefetchScalarGridSpec(num_s...]
    ppermute x29 -> x8, starting transfers between devices: 30.7 us -> 17.8 us  [the longest x5 14.3 us: shift(): return lax.ppermute(value, 'chain', pairs)]
    all_to_all x1 -> x3, starting transfers between devices: 27 us -> 15.6 us  [the longest x1 8.4 us: shards(): others = lax.all_to_all(copies, 'cand', 0, 0, tiled=True)]
    dot_general x30 -> x5, matrix products: 18.8 us -> 8.09 us  [mm(): return jnp.dot(a, b, precision=HIGH, preferred_element_type=jnp.float32)]
    all_to_all x1 -> x3, waiting for transfers between devices: 0.01 us -> 10.5 us  [the longest x1 8.88 us: shards(): lax.all_to_all(older(where, inverse, factor), 'chain', 0, 0, axis_index_g...]
    ppermute x1, waiting for transfers between devices: 9.09 us -> 4.15 us  [shards(): turned = lax.ppermute(rows, ('chain', 'cand'), turn)]
  transfers between devices with their start and end apart: 33 -> 14, of which waited for: 15 -> 8; matrix products, arithmetic and copies ran while one was open for 5% -> 3% of each run, Pallas kernels for 4% -> 5%
where the time goes in v2:
time: 204 us; the launch traced here: 203 us
  blocking collectives  55.9 us (27%)
  starting transfers between devices  55.7 us (27%)
  waiting for transfers between devices  47.8 us (23%)
  Pallas kernels  23.2 us (11%)
  matrix products  11.4 us (6%)
  other arithmetic  6.02 us (3%)
  local copies, waits for them, and re-layouts  2.34 us (1%)
    all_to_all x1, blocking collectives, shards(): lax.all_to_all(sent, 'chain', 0, 0, axis_index_groups=inside, tiled=True)  37.6 us
    ppermute x3, waiting for transfers between devices, shards(): mine.append(lax.ppermute(rows, 'chain', pairs))  19.5 us
    all_to_all x2, blocking collectives, settle(): lax.all_to_all(parts, 'chain', 0, 0, axis_index_groups=inside, tiled=True)  18.3 us
    ppermute x5, starting transfers between devices, shift(): return lax.ppermute(value, 'chain', pairs)  14.3 us
    all_to_all x1, starting transfers between devices, shards(): lax.all_to_all(shares, 'chain', 0, 0, axis_index_groups=across, tiled=True)  13.6 us
    all_to_all x1, waiting for transfers between devices, shards(): lax.all_to_all(shares, 'chain', 0, 0, axis_index_groups=across, tiled=True)  10.2 us
    all_to_all x1, waiting for transfers between devices, shards(): lax.all_to_all(older(where, inverse, factor), 'chain', 0, 0, axis_index_g...  8.88 us
    all_to_all x1, starting transfers between devices, shards(): others = lax.all_to_all(copies, 'cand', 0, 0, tiled=True)  8.4 us
  transfers between devices with their start and end apart: 14, of which 8 were waited for; matrix products, arithmetic and copies ran while one was open for 3% of the time, Pallas kernels for 5%

profile of v2, /device:TPU:2, one launch (start us, length us, event | category | flops | bytes accessed | tf_op | source)
XLA Modules:
  0.0 203.3 jit_solution(1185297936056949179)
XLA Ops:
  0.6 3.8 %collective-permute-start.5 = (f32[32,128]{1,0:T(8,128)}, f32[32,128]{1,0:T(8,128)S(1)}, u32[]{:S(2)}, u32[]{:S(2)}) collective-permute-start(f32[32,128]{1,0:T(8,128)} %param.5), channel_id=1, source_target_pairs={{0,0},{1,16},{2,32},{3,48},{4,64},{5,80},{6,96},{7,112},{8,128},{9... | collective-permute-start | bytes 49160 | tf_op jit(solution)/shard_map/ppermute | solution.py:199
  8.2 1.0 multiply_reduce_fusion
  9.8 7.8 %shard_map.59 = (f32[4,192,896]{2,1,0:T(8,128)}, f32[192,192]{1,0:T(8,128)}) custom-call(s32[2]{0:T(128)} %pad_add_fusion.where_ref, f32[192,3072]{1,0:T(8,128)} %three_ref.1, f32[192,3072]{1,0:T(8,128)} %three_ref.1, f32[192,128]{1,0:T(8,128)} %exponential_multiply_fusion.cross_ref), custom_call_target="tpu_custom_call" | custom-call | tf_op jit(solution)/shard_map/pallas_call | solution.py:77
  17.6 37.6 %all_to_all.35.got_ref = f32[4,192,896]{2,1,0:T(8,128)} all-to-all(f32[4,192,896]{2,1,0:T(8,128)} %get-tuple-element.6), channel_id=1, replica_groups={{0,16,32,48},{64,80,96,112},{128,144,160,176},{192,208,224,240},{1,17,3..., dimensions={0} | all-to-all | bytes 5505024 | tf_op jit(solution)/shard_map/all_to_all | solution.py:201
  55.3 6.1 %shard_map.60 = (f32[192,128]{1,0:T(8,128)}, f32[768,192]{1,0:T(8,128)}) custom-call(s32[2]{0:T(128)} %pad_add_fusion.where_ref, f32[4,192,896]{2,1,0:T(8,128)} %all_to_all.35.got_ref), custom_call_target="tpu_custom_call" | custom-call | tf_op jit(solution)/shard_map/pallas_call | solution.py:148
  61.3 7.2 %collective-permute-start = (f32[192,128]{1,0:T(8,128)}, f32[192,128]{1,0:T(8,128)S(1)}, u32[]{:S(2)}, u32[]{:S(2)}) collective-permute-start(f32[192,128]{1,0:T(8,128)} %get-tuple-element.7), channel_id=1, source_target_pairs={{0,64},{16,80},{32,96},{48,112},{1,65},{17,81},{33,97},{49,113},{2... | collective-permute-start | bytes 294920 | tf_op jit(solution)/shard_map/ppermute | solution.py:212
  68.6 2.5 %collective-permute-done = f32[192,128]{1,0:T(8,128)S(1)} collective-permute-done((f32[192,128]{1,0:T(8,128)}, f32[192,128]{1,0:T(8,128)S(1)}, u32[]{:S(2)}, u32[]{:S(2)}) %collective-permute-start) | collective-permute-done | bytes 98336 | tf_op jit(solution)/shard_map/ppermute | solution.py:212
  71.1 2.7 %fusion.13 = f32[768,128]{1,0:T(8,128)} fusion(f32[768,192]{1,0:T(8,128)} %get-tuple-element.8, f32[192,128]{1,0:T(8,128)S(1)} %collective-permute-done), kind=kOutput, calls=%fused_computation.27 | convolution fusion | flops 226492416 | bytes 1081344 | tf_op jit(solution)/shard_map/dot_general | solution.py:20
  73.7 3.7 %all-to-all-start.2 = ((f32[4,192,128]{2,1,0:T(8,128)}), f32[4,192,128]{2,1,0:T(8,128)S(1)}, u32[]{:S(2)}, u32[]{:S(2)}) async-start(f32[4,192,128]{2,1,0:T(8,128)} %bitcast.2), calls=%async_computation.2 | async-start | bytes 786432 | tf_op jit(solution)/shard_map/all_to_all | solution.py:216
  77.4 4.2 %shard_map.61 = f32[4,192,384]{2,1,0:T(8,128)} custom-call(s32[2]{0:T(128)} %pad_add_fusion.where_ref, f32[192,192]{1,0:T(8,128)} %get-tuple-element.9.d_ref, f32[192,3072]{1,0:T(8,128)} %three_ref.1, f32[192,3072]{1,0:T(8,128)} %three_ref.1), custom_call_target="tpu_custom_call" | custom-call | tf_op jit(solution)/shard_map/pallas_call | solution.py:113
  81.6 1.7 all-to-all-done.2
  83.3 3.5 %all-to-all-start.1 = ((f32[4,192,384]{2,1,0:T(8,128)}), f32[4,192,384]{2,1,0:T(8,128)S(1)}, u32[]{:S(2)}, u32[]{:S(2)}) async-start(f32[4,192,384]{2,1,0:T(8,128)} %shard_map.61), calls=%async_computation.1 | async-start | bytes 2359296 | tf_op jit(solution)/shard_map/all_to_all | solution.py:202
  86.9 3.0 %collective-permute-start.2 = (f32[192,128]{1,0:T(8,128)S(1)}, f32[192,128]{1,0:T(8,128)S(1)}, u32[]{:S(2)}, u32[]{:S(2)}) collective-permute-start(f32[192,128]{1,0:T(8,128)S(1)} %sub.46), channel_id=1, source_target_pairs={{64,128},{80,144},{96,160},{112,176},{0,192},{16,208},{32,224},{48... | collective-permute-start | bytes 294920 | tf_op jit(solution)/shard_map/ppermute | solution.py:212
  89.9 2.7 %collective-permute-start.1 = (f32[192,128]{1,0:T(8,128)S(1)}, f32[192,128]{1,0:T(8,128)S(1)}, u32[]{:S(2)}, u32[]{:S(2)}) collective-permute-start(f32[192,128]{1,0:T(8,128)S(1)} %copy-done.3), channel_id=1, source_target_pairs={{0,128},{16,144},{32,160},{48,176},{1,129},{17,145},{33,161},{49,1... | collective-permute-start | bytes 294920 | tf_op jit(solution)/shard_map/ppermute | solution.py:212
  92.6 8.9 %all-to-all-done.1.more_ref = f32[4,192,384]{2,1,0:T(8,128)S(1)} async-done(((f32[4,192,384]{2,1,0:T(8,128)}), f32[4,192,384]{2,1,0:T(8,128)S(1)}, u32[]{:S(2)}, u32[]{:S(2)}) %all-to-all-start.1) | async-done | bytes 1179680 | tf_op jit(solution)/shard_map/all_to_all | solution.py:202
  101.5 1.0 copy-done.2
  102.5 5.2 %shard_map.62 = f32[768,384]{1,0:T(8,128)} custom-call(f32[4,192,896]{2,1,0:T(8,128)} %all_to_all.35.got_ref, f32[4,192,384]{2,1,0:T(8,128)} %copy-done.2), custom_call_target="tpu_custom_call" | custom-call | tf_op jit(solution)/shard_map/pallas_call | solution.py:177
  107.7 2.1 %fusion.2 = f32[768,128]{1,0:T(8,128)S(1)} fusion(f32[192,128]{1,0:T(8,128)S(1)} %collective-permute-done.2, f32[768,192]{1,0:T(8,128)S(1)} %copy-done.1, f32[768,384]{1,0:T(8,128)} %shard_map.62, pred[]{:T(512)S(6)} %eq.5), kind=kOutput, calls=%fused_computation.8 | convolution fusion | flops 226639872 | bytes 1867777 | tf_op jit(solution)/shard_map/dot_general | solution.py:20
  109.8 1.8 fusion.1
  111.6 9.0 %all_to_all.36 = f32[4,192,128]{2,1,0:T(8,128)S(1)} all-to-all(f32[4,192,128]{2,1,0:T(8,128)S(1)} %bitcast.26), channel_id=1, replica_groups={{0,16,32,48},{64,80,96,112},{128,144,160,176},{192,208,224,240},{1,17,3..., dimensions={0} | all-to-all | bytes 786432 | tf_op jit(solution)/shard_map/all_to_all | solution.py:216
  123.6 9.3 %all_to_all.37 = f32[4,192,128]{2,1,0:T(8,128)S(1)} all-to-all(f32[4,192,128]{2,1,0:T(8,128)S(1)} %bitcast.27), channel_id=1, replica_groups={{0,16,32,48},{64,80,96,112},{128,144,160,176},{192,208,224,240},{1,17,3..., dimensions={0} | all-to-all | bytes 786432 | tf_op jit(solution)/shard_map/all_to_all | solution.py:216
  132.9 5.0 %collective-permute-start.6 = (f32[192,128]{1,0:T(8,128)S(1)}, f32[192,128]{1,0:T(8,128)S(1)}, u32[]{:S(2)}, u32[]{:S(2)}) collective-permute-start(f32[192,128]{1,0:T(8,128)S(1)} %sub.48), channel_id=1, source_target_pairs={{0,0},{4,1},{8,2},{12,3},{16,4},{20,5},{24,6},{28,7},{32,8},{36,9}... | collective-permute-start | bytes 294920 | tf_op jit(solution)/shard_map/ppermute | solution.py:236
  137.9 4.2 %collective-permute-done.6 = f32[192,128]{1,0:T(8,128)S(1)} collective-permute-done((f32[192,128]{1,0:T(8,128)S(1)}, f32[192,128]{1,0:T(8,128)S(1)}, u32[]{:S(2)}, u32[]{:S(2)}) %collective-permute-start.6) | collective-permute-done | bytes 98336 | tf_op jit(solution)/shard_map/ppermute | solution.py:236
  142.0 1.3 broadcast_in_dim.2
  143.3 8.4 %all-to-all-start.5 = ((f32[16,192,128]{2,1,0:T(8,128)}), f32[16,192,128]{2,1,0:T(8,128)S(1)}, u32[]{:S(2)}, u32[]{:S(2)}) async-start(f32[16,192,128]{2,1,0:T(8,128)} %broadcast_in_dim.2), calls=%async_computation.5 | async-start | bytes 3145728 | tf_op jit(solution)/shard_map/all_to_all | solution.py:242
  152.1 1.9 collective-permute-start.8
  154.0 1.2 collective-permute-start.7
  155.2 7.6 %collective-permute-done.9 = f32[192,128]{1,0:T(8,128)S(1)} collective-permute-done((f32[192,128]{1,0:T(8,128)S(1)}, f32[192,128]{1,0:T(8,128)S(1)}, u32[]{:S(2)}, u32[]{:S(2)}) %collective-permute-start.9) | collective-permute-done | bytes 98336 | tf_op jit(solution)/shard_map/ppermute | solution.py:240
  162.8 12.0 %collective-permute-done.7 = f32[192,128]{1,0:T(8,128)S(1)} collective-permute-done((f32[192,128]{1,0:T(8,128)S(1)}, f32[192,128]{1,0:T(8,128)S(1)}, u32[]{:S(2)}, u32[]{:S(2)}) %collective-permute-start.7) | collective-permute-done | bytes 98336 | tf_op jit(solution)/shard_map/ppermute | solution.py:240
  174.8 3.3 %convolution_bitcast_fusion = f32[4,128,128]{2,1,0:T(8,128)} fusion(f32[4,4,192,128]{3,2,1,0:T(8,128)S(1)} %bitcast.25, f32[1,192,128]{2,1,0:T(8,128)S(1)} %bitcast.29, f32[1,192,128]{2,1,0:T(8,128)S(1)} %bitcast.30, f32[1,192,128]{2,1,0:T(8,128)S(1)} %bitcast.31, f32[1,192,128]{2,1,0:T(8,128)S(1)} %bitcast.28), kind=kOutput, calls=%fused_computation.6 | convolution fusion | flops 604274688 | bytes 2228224 | tf_op jit(solution)/shard_map/jmra,jrb->mab/dot_general | solution.py:244
  178.1 13.6 %all-to-all-start.6 = ((f32[4,128,128]{2,1,0:T(8,128)}), f32[4,128,128]{2,1,0:T(8,128)S(1)}, u32[]{:S(2)}, u32[]{:S(2)}) async-start(f32[4,128,128]{2,1,0:T(8,128)} %convolution_bitcast_fusion), calls=%async_computation.6 | async-start | bytes 524288 | tf_op jit(solution)/shard_map/all_to_all | solution.py:247
  192.4 10.2 %all-to-all-done.6 = f32[4,128,128]{2,1,0:T(8,128)S(1)} async-done(((f32[4,128,128]{2,1,0:T(8,128)}), f32[4,128,128]{2,1,0:T(8,128)S(1)}, u32[]{:S(2)}, u32[]{:S(2)}) %all-to-all-start.6) | async-done | bytes 262176 | tf_op jit(solution)/shard_map/all_to_all | solution.py:247
  (35 shorter events, 9.2 us)
Async XLA Ops:
  0.6 6.7 %collective-permute-start.5 = (f32[32,128]{1,0:T(8,128)}, f32[32,128]{1,0:T(8,128)S(1)}, u32[]{:S(2)}, u32[]{:S(2)}) collective-permute-start(f32[32,128]{1,0:T(8,128)} %param.5), channel_id=1, source_target_pairs={{0,0},{1,16},{2,32},{3,48},{4,64},{5,80},{6,96},{7,112},{8,128},{9... | collective-permute-start | bytes 49160 | tf_op jit(solution)/shard_map/ppermute | solution.py:199
  61.3 9.7 %collective-permute-start = (f32[192,128]{1,0:T(8,128)}, f32[192,128]{1,0:T(8,128)S(1)}, u32[]{:S(2)}, u32[]{:S(2)}) collective-permute-start(f32[192,128]{1,0:T(8,128)} %get-tuple-element.7), channel_id=1, source_target_pairs={{0,64},{16,80},{32,96},{48,112},{1,65},{17,81},{33,97},{49,113},{2... | collective-permute-start | bytes 294920 | tf_op jit(solution)/shard_map/ppermute | solution.py:212
  73.7 9.6 %all-to-all-start.2 = ((f32[4,192,128]{2,1,0:T(8,128)}), f32[4,192,128]{2,1,0:T(8,128)S(1)}, u32[]{:S(2)}, u32[]{:S(2)}) async-start(f32[4,192,128]{2,1,0:T(8,128)} %bitcast.2), calls=%async_computation.2 | async-start | bytes 786432 | tf_op jit(solution)/shard_map/all_to_all | solution.py:216
  81.6 5.2 %copy-start.3 = (f32[192,128]{1,0:T(8,128)S(1)}, f32[192,128]{1,0:T(8,128)}, u32[]{:S(2)}) copy-start(f32[192,128]{1,0:T(8,128)} %get-tuple-element.7) | copy-start | bytes 294916
  83.3 18.2 %all-to-all-start.1 = ((f32[4,192,384]{2,1,0:T(8,128)}), f32[4,192,384]{2,1,0:T(8,128)S(1)}, u32[]{:S(2)}, u32[]{:S(2)}) async-start(f32[4,192,384]{2,1,0:T(8,128)} %shard_map.61), calls=%async_computation.1 | async-start | bytes 2359296 | tf_op jit(solution)/shard_map/all_to_all | solution.py:202
  86.9 20.8 %collective-permute-start.2 = (f32[192,128]{1,0:T(8,128)S(1)}, f32[192,128]{1,0:T(8,128)S(1)}, u32[]{:S(2)}, u32[]{:S(2)}) collective-permute-start(f32[192,128]{1,0:T(8,128)S(1)} %sub.46), channel_id=1, source_target_pairs={{64,128},{80,144},{96,160},{112,176},{0,192},{16,208},{32,224},{48... | collective-permute-start | bytes 294920 | tf_op jit(solution)/shard_map/ppermute | solution.py:212
  89.9 17.8 %copy-start.1 = (f32[768,192]{1,0:T(8,128)S(1)}, f32[768,192]{1,0:T(8,128)}, u32[]{:S(2)}) copy-start(f32[768,192]{1,0:T(8,128)} %get-tuple-element.8) | copy-start | bytes 1769476
  89.9 19.9 %collective-permute-start.1 = (f32[192,128]{1,0:T(8,128)S(1)}, f32[192,128]{1,0:T(8,128)S(1)}, u32[]{:S(2)}, u32[]{:S(2)}) collective-permute-start(f32[192,128]{1,0:T(8,128)S(1)} %copy-done.3), channel_id=1, source_target_pairs={{0,128},{16,144},{32,160},{48,176},{1,129},{17,145},{33,161},{49,1... | collective-permute-start | bytes 294920 | tf_op jit(solution)/shard_map/ppermute | solution.py:212
  101.5 1.0 copy-start.2
  107.7 2.1 %copy-start = (f32[768,384]{1,0:T(8,128)S(1)}, f32[768,384]{1,0:T(8,128)}, u32[]{:S(2)}) copy-start(f32[768,384]{1,0:T(8,128)} %shard_map.62) | copy-start | bytes 3538948
  120.6 1.4 collective-permute-start.4
  121.3 1.5 collective-permute-start.3
  132.9 41.9 %copy-start.4 = (f32[192,128]{1,0:T(8,128)}, f32[192,128]{1,0:T(8,128)S(1)}, u32[]{:S(2)}) copy-start(f32[192,128]{1,0:T(8,128)S(1)} %sub.48) | copy-start | bytes 294916
  132.9 9.1 %collective-permute-start.6 = (f32[192,128]{1,0:T(8,128)S(1)}, f32[192,128]{1,0:T(8,128)S(1)}, u32[]{:S(2)}, u32[]{:S(2)}) collective-permute-start(f32[192,128]{1,0:T(8,128)S(1)} %sub.48), channel_id=1, source_target_pairs={{0,0},{4,1},{8,2},{12,3},{16,4},{20,5},{24,6},{28,7},{32,8},{36,9}... | collective-permute-start | bytes 294920 | tf_op jit(solution)/shard_map/ppermute | solution.py:236
  143.3 31.4 %all-to-all-start.5 = ((f32[16,192,128]{2,1,0:T(8,128)}), f32[16,192,128]{2,1,0:T(8,128)S(1)}, u32[]{:S(2)}, u32[]{:S(2)}) async-start(f32[16,192,128]{2,1,0:T(8,128)} %broadcast_in_dim.2), calls=%async_computation.5 | async-start | bytes 3145728 | tf_op jit(solution)/shard_map/all_to_all | solution.py:242
  151.8 11.1 %collective-permute-start.9 = (f32[192,128]{1,0:T(8,128)S(1)}, f32[192,128]{1,0:T(8,128)S(1)}, u32[]{:S(2)}, u32[]{:S(2)}) collective-permute-start(f32[192,128]{1,0:T(8,128)S(1)} %sub.48), channel_id=1, source_target_pairs={{0,48},{16,32},{32,16},{48,0},{64,112},{80,96},{96,80},{112,64},{1... | collective-permute-start | bytes 294920 | tf_op jit(solution)/shard_map/ppermute | solution.py:240
  152.1 10.8 %collective-permute-start.8 = (f32[192,128]{1,0:T(8,128)S(1)}, f32[192,128]{1,0:T(8,128)S(1)}, u32[]{:S(2)}, u32[]{:S(2)}) collective-permute-start(f32[192,128]{1,0:T(8,128)S(1)} %sub.48), channel_id=1, source_target_pairs={{0,32},{16,48},{32,0},{48,16},{64,96},{80,112},{96,64},{112,80},{1... | collective-permute-start | bytes 294920 | tf_op jit(solution)/shard_map/ppermute | solution.py:240
  154.0 20.8 %collective-permute-start.7 = (f32[192,128]{1,0:T(8,128)S(1)}, f32[192,128]{1,0:T(8,128)S(1)}, u32[]{:S(2)}, u32[]{:S(2)}) collective-permute-start(f32[192,128]{1,0:T(8,128)S(1)} %sub.48), channel_id=1, source_target_pairs={{0,16},{16,0},{32,48},{48,32},{64,80},{80,64},{96,112},{112,96},{1... | collective-permute-start | bytes 294920 | tf_op jit(solution)/shard_map/ppermute | solution.py:240
  178.1 24.5 %all-to-all-start.6 = ((f32[4,128,128]{2,1,0:T(8,128)}), f32[4,128,128]{2,1,0:T(8,128)S(1)}, u32[]{:S(2)}, u32[]{:S(2)}) async-start(f32[4,128,128]{2,1,0:T(8,128)} %convolution_bitcast_fusion), calls=%async_computation.6 | async-start | bytes 524288 | tf_op jit(solution)/shard_map/all_to_all | solution.py:247

commit v3 on v1

v3 whole, which is shorter than its diff:
```python
import jax
import jax.numpy as jnp
from jax import lax
from jax.experimental import pallas as pl
from jax.experimental.pallas import tpu as pltpu
from jax.sharding import PartitionSpec as P

HIGH = lax.Precision.HIGHEST
BASE = 32
QUAD = 4


def matern(first_set, second_set):
    differ = first_set[:, :, None] - second_set[:, None, :]
    radius = jnp.sqrt(5.0 * jnp.sum(differ * differ, axis=0))
    return (1.0 + radius + radius * radius / 3.0) * jnp.exp(-radius)


def mm(a, b):
    return jnp.dot(a, b, precision=HIGH, preferred_element_type=jnp.float32)


def invert_into(l_ref, d_ref):
    size = l_ref.shape[0]
    count = size // BASE
    rows = lax.broadcasted_iota(jnp.int32, (BASE, BASE), 0)
    cols = lax.broadcasted_iota(jnp.int32, (BASE, BASE), 1)
    strict, solved = [], []
    for k in range(count):
        block = l_ref[k * BASE : (k + 1) * BASE, k * BASE : (k + 1) * BASE]
        diag = jnp.sum(jnp.where(rows == cols, block, 0.0), axis=1, keepdims=True)
        inv = 1.0 / diag
        strict.append(jnp.where(rows > cols, block * inv, 0.0))
        solved.append(jnp.where(rows == cols, inv, 0.0))
    for r in range(BASE - 1):
        for k in range(count):
            solved[k] = solved[k] - strict[k][:, r : r + 1] * solved[k][r : r + 1, :]
    d_ref[...] = jnp.zeros_like(d_ref)
    for k in range(count):
        d_ref[k * BASE : (k + 1) * BASE, k * BASE : (k + 1) * BASE] = solved[k]
    for k in range(0, count - 1, 2):
        a, b, c = k * BASE, (k + 1) * BASE, (k + 2) * BASE
        d_ref[b:c, a:b] = -mm(solved[k + 1], mm(l_ref[b:c, a:b], solved[k]))
    low = 2 * BASE
    while low < size:
        high = low + 2 * BASE
        d_ref[low:high, 0:low] = -mm(
            d_ref[low:high, low:high], mm(l_ref[low:high, 0:low], d_ref[0:low, 0:low])
        )
        low = high


def unpack(panel):
    half = panel.shape[1] // 2
    return jnp.concatenate([panel[:, 0:half], panel[:, half:]], axis=0)


def pack(tall):
    height = tall.shape[0] // 2
    return jnp.concatenate([tall[0:height], tall[height:]], axis=1)


def first_kernel(side_ref, own_ref, other_ref, cross_ref, d_ref, x_ref, e_ref, o_ref, i_ref):
    height = own_ref.shape[0]
    even = side_ref[0] == 0
    e_ref[...] = jnp.where(even, own_ref[:, 0:height], other_ref[:, 0:height])
    o_ref[...] = jnp.where(even, other_ref[:, height:], own_ref[:, height:])
    couple = jnp.where(even, other_ref[:, 0:height], own_ref[:, 0:height])
    d_ref[0:height, height:] = jnp.zeros((height, height), jnp.float32)
    invert_into(e_ref, i_ref)
    upper = i_ref[...]
    d_ref[0:height, 0:height] = upper
    invert_into(o_ref, e_ref)
    lower = e_ref[...]
    d_ref[height:, height:] = lower
    d_ref[height:, 0:height] = -mm(lower, mm(couple, upper))
    x_ref[...] = pack(mm(d_ref[...], unpack(cross_ref[...])))


def first(side, own, other, cross):
    height = own.shape[0]
    square = pltpu.VMEM((height, height), jnp.float32)
    return pl.pallas_call(
        first_kernel,
        in_specs=[pl.BlockSpec(memory_space=pltpu.SMEM)] + [pl.BlockSpec(memory_space=pltpu.VMEM)] * 3,
        out_shape=[
            jax.ShapeDtypeStruct((2 * height, 2 * height), jnp.float32),
            jax.ShapeDtypeStruct(cross.shape, jnp.float32),
        ],
        scratch_shapes=[square, square, square],
    )(side, own, other, cross)


def step_kernel(pick_ref, one_ref, two_ref, d_ref, rest_ref, near_ref, far_ref, left_ref, x_ref):
    near, far = near_ref[...], far_ref[...]
    swap = pick_ref[1] == 1
    lead = jnp.where(swap, near, far)
    tail = jnp.where(swap, far, near)
    panels = jnp.concatenate([unpack(lead), unpack(tail)], axis=0)

    rows = jnp.where(pick_ref[0] == 0, one_ref[...], two_ref[...])
    left = unpack(rest_ref[...]) - mm(rows, panels)
    left_ref[...] = pack(left)
    x_ref[...] = pack(mm(d_ref[...], left))


def step(pick, one, two, inverse, rest, near, far):
    shape = jax.ShapeDtypeStruct(rest.shape, jnp.float32)
    return pl.pallas_call(
        step_kernel,
        in_specs=[pl.BlockSpec(memory_space=pltpu.SMEM)] + [pl.BlockSpec(memory_space=pltpu.VMEM)] * 6,
        out_shape=[shape, shape],
    )(pick, one, two, inverse, rest, near, far)


def shards(archive_inputs, candidate_inputs, lengthscales, factor):
    height = factor.shape[0]
    width = candidate_inputs.shape[1]
    chain = lax.axis_size("chain")
    cand = lax.axis_size("cand")
    quads = chain // QUAD
    position = lax.axis_index("chain")
    inside = [[QUAD * g + i for i in range(QUAD)] for g in range(quads)]
    across = [[QUAD * g + i for g in range(quads)] for i in range(QUAD)]
    layers = chain // 2
    layer, side = position // 2, position % 2
    odd = layer % 2
    side_word = jnp.full((1,), side, jnp.int32)
    pair_all = [(p, p ^ 1) for p in range(chain)]
    scaling = 1.0 / lengthscales
    scaled_archive = archive_inputs * scaling[:, None]
    scaled_candidates = candidate_inputs * scaling[:, None]

    def halves(own, other):
        half = width // 2
        even = jnp.concatenate([own[:, :half], other[:, :half]], axis=1)
        return jnp.where(side == 0, even, jnp.concatenate([other[:, half:], own[:, half:]], axis=1))

    own_diagonal = lax.dynamic_slice_in_dim(factor, layer * 2 * height, 2 * height, 1)
    other_diagonal = lax.ppermute(own_diagonal, "chain", pair_all)
    cross = matern(scaled_archive, scaled_candidates)
    rest = halves(cross, lax.ppermute(cross, "chain", pair_all))

    slabs = []
    for s in range(layers // 2):
        start = jnp.maximum(2 * s - odd, 0) * 2 * height
        mine = lax.dynamic_slice_in_dim(factor, start, 4 * height, 1)
        pairs = [(p, p ^ 1) for p in range(chain) if p // 2 >= 2 * s + 1]
        yours = lax.ppermute(mine, "chain", pairs)
        upper = jnp.where(side == 0, mine, yours)
        lower = jnp.where(side == 0, yours, mine)
        slabs.append(jnp.concatenate([upper, lower], axis=0))

    def hop(value, pairs):
        return lax.ppermute(value, "chain", [(2 * a + i, 2 * b + i) for a, b in pairs for i in range(2)])

    inverse, solved = first(side_word, own_diagonal, other_diagonal, rest)
    far = jnp.zeros_like(rest)
    for t in range(layers - 1):
        near = hop(solved, [(t - k, t + 1 + k) for k in range(layers) if t - k >= 0 and t + 1 + k < layers])
        pairs = [(t - k, t + 2 + k) for k in range(layers) if t - k >= 0 and t + 2 + k < layers]
        ahead = hop(solved, pairs) if pairs else None
        users = sorted({t - z // 2 for z in range(t + 1, min(2 * t + 1, layers - 1) + 1)})
        turn_of = t - layer // 2
        choice = (turn_of == users[-1]).astype(jnp.int32) if len(users) > 1 else jnp.int32(0)
        flip = jnp.logical_and(turn_of == 0, odd == 1).astype(jnp.int32)
        pick = jnp.stack([choice, flip])
        rest, solved = step(pick, slabs[users[0]], slabs[users[-1]], inverse, rest, near, far)
        far = ahead
    rows = halves(solved, lax.ppermute(solved, "chain", pair_all))
    swap = [(a * cand + b, b * cand + a) for a in range(chain) for b in range(cand)]
    chosen = lax.ppermute(candidate_inputs, ("chain", "cand"), swap)

    turn = [
        ((QUAD * g + (i ^ j)) * cand + QUAD * m + i, (QUAD * g + i) * cand + QUAD * j + m)
        for g in range(quads)
        for i in range(QUAD)
        for j in range(QUAD)
        for m in range(cand // QUAD)
    ]
    turned = lax.ppermute(rows, ("chain", "cand"), turn)
    mine = [rows]
    for r in range(1, QUAD):
        pairs = [(QUAD * g + i, QUAD * g + (i ^ r)) for g in range(quads) for i in range(QUAD)]
        mine.append(lax.ppermute(rows, "chain", pairs))
    copies = jnp.broadcast_to(turned[None], (cand,) + turned.shape)
    others = lax.all_to_all(copies, "cand", 0, 0, tiled=True)
    others = others.reshape(QUAD, cand // QUAD, height, width)
    shares = jnp.einsum(
        "jmra,jrb->mab", others, jnp.stack(mine), precision=HIGH, preferred_element_type=jnp.float32
    )
    shared = lax.all_to_all(shares, "chain", 0, 0, axis_index_groups=across, tiled=True).sum(axis=0)
    prior_cov = matern(chosen * scaling[:, None], scaled_candidates)
    return (rows, prior_cov - shared)


def solution(mesh):
    return jax.shard_map(
        shards,
        mesh=mesh,
        in_specs=(P(None, "chain"), P(None, "cand"), P(), P("chain", None)),
        out_specs=(P("chain", "cand"), P("chain", "cand")),
        check_vma=False,
    )
```

time: 230 us -> 223 us (0.970)
  Pallas kernels: 10.1 us -> 44.4 us
  blocking collectives: 28.4 us -> 0 us
  starting transfers between devices: 120 us -> 98.1 us
  matrix products: 22.1 us -> 3.31 us
  waiting for transfers between devices: 37 us -> 49.3 us
  other arithmetic: 5.24 us -> 16.5 us
  local copies, waits for them, and re-layouts: 2.71 us -> 9.32 us
    all_to_all x1, starting transfers between devices: 56.6 us -> 21.9 us  [shards(): lax.all_to_all(shares, 'chain', 0, 0, axis_index_groups=across, tiled=True)]
    pallas_call x2 -> x8, Pallas kernels: 10.1 us -> 44.4 us  [the longest x7 36.5 us: step(): pl.pallas_call(step_kernel, in_specs=[pl.BlockSpec(memory_space=pltpu.SME...]
    ppermute x29 -> x23, starting transfers between devices: 30.7 us -> 60.5 us  [the longest x13 48.3 us: hop(): lax.ppermute(value, 'chain', [(2 * a + i, 2 * b + i) for a, b in pairs fo...]
    all_to_all x1 -> x0, blocking collectives: 28.4 us -> none  [spread(): lax.all_to_all(copies, axis, 0, 0, axis_index_groups=groups, tiled=True)]
    all_to_all x1, starting transfers between devices: 27 us -> 7.74 us  [shards(): others = lax.all_to_all(copies, 'cand', 0, 0, tiled=True)]
    dot_general x31 -> x1, matrix products: 22.1 us -> 3.31 us  [shards(): jnp.einsum('jmra,jrb->mab', others, jnp.stack(mine), precision=HIGH, pref...]
    ppermute x29 -> x23, waiting for transfers between devices: 17.1 us -> 32.2 us  [the longest x3 19.9 us: shards(): mine.append(lax.ppermute(rows, 'chain', pairs))]
    concatenate x0 -> x4, other arithmetic: none -> 4.54 us  [shards(): slabs.append(jnp.concatenate([upper, lower], axis=0))]
  transfers between devices with their start and end apart: 33 -> 27, of which waited for: 15 -> 7; matrix products, arithmetic and copies ran while one was open for 5% -> 8% of each run, Pallas kernels for 4% -> 18%
where the time goes in v3:
time: 223 us; the launch traced here: 222 us
  starting transfers between devices  98.1 us (44%)
  waiting for transfers between devices  49.3 us (22%)
  Pallas kernels  44.4 us (20%)
  other arithmetic  16.5 us (7%)
  local copies, waits for them, and re-layouts  9.32 us (4%)
  matrix products  3.31 us (1%)
    ppermute x13, starting transfers between devices, hop(): lax.ppermute(value, 'chain', [(2 * a + i, 2 * b + i) for a, b in pairs fo...  48.3 us
    pallas_call x7, Pallas kernels, step(): pl.pallas_call(step_kernel, in_specs=[pl.BlockSpec(memory_space=pltpu.SME...  36.5 us
    all_to_all x1, starting transfers between devices, shards(): lax.all_to_all(shares, 'chain', 0, 0, axis_index_groups=across, tiled=True)  21.9 us
    ppermute x3, waiting for transfers between devices, shards(): mine.append(lax.ppermute(rows, 'chain', pairs))  19.9 us
    all_to_all x1, waiting for transfers between devices, shards(): lax.all_to_all(shares, 'chain', 0, 0, axis_index_groups=across, tiled=True)  10.5 us
    pallas_call x1, Pallas kernels, first(): pl.pallas_call(first_kernel, in_specs=[pl.BlockSpec(memory_space=pltpu.SM...  7.86 us
    all_to_all x1, starting transfers between devices, shards(): others = lax.all_to_all(copies, 'cand', 0, 0, tiled=True)  7.74 us
    ppermute x1, waiting for transfers between devices, shards(): turned = lax.ppermute(rows, ('chain', 'cand'), turn)  6.62 us
  transfers between devices with their start and end apart: 27, of which 7 were waited for; matrix products, arithmetic and copies ran while one was open for 8% of the time, Pallas kernels for 18%

profile of v3, /device:TPU:2, one launch (start us, length us, event | category | flops | bytes accessed | tf_op | source)
XLA Modules:
  0.0 222.1 jit_solution(10033734590240947062)
XLA Ops:
  0.7 1.8 constant_dynamic-slice_fusion
  2.5 1.5 collective-permute-start.5
  5.0 1.7 collective-permute-start.1
  6.6 4.7 %collective-permute-start.20 = (f32[32,128]{1,0:T(8,128)S(1)}, f32[32,128]{1,0:T(8,128)S(1)}, u32[]{:S(2)}, u32[]{:S(2)}) collective-permute-start(f32[32,128]{1,0:T(8,128)S(1)} %copy-done.14), channel_id=1, source_target_pairs={{0,0},{1,16},{2,32},{3,48},{4,64},{5,80},{6,96},{7,112},{8,128},{9... | collective-permute-start | bytes 49160 | tf_op jit(solution)/shard_map/ppermute | solution.py:172
  11.3 1.5 collective-permute-start.4
  20.1 5.1 %collective-permute-done.2 = f32[192,128]{1,0:T(8,128)S(1)} collective-permute-done((f32[192,128]{1,0:T(8,128)S(1)}, f32[192,128]{1,0:T(8,128)S(1)}, u32[]{:S(2)}, u32[]{:S(2)}) %collective-permute-start.2) | collective-permute-done | bytes 98336 | tf_op jit(solution)/shard_map/ppermute | solution.py:142
  25.2 1.5 collective-permute-start
  27.6 7.9 %shard_map.59 = (f32[384,384]{1,0:T(8,128)}, f32[192,128]{1,0:T(8,128)}) custom-call(s32[1]{0:T(128)} %bitcast.1.side_ref, f32[192,384]{1,0:T(8,128)} %copy-done, f32[192,384]{1,0:T(8,128)} %collective-permute-done.1.other_ref, f32[192,128]{1,0:T(8,128)} %maximum_select_fusion.cross_ref.rest_ref), custom_call_target="tpu_custom_call" | custom-call | tf_op jit(solution)/shard_map/pallas_call | solution.py:83
  35.4 10.3 %collective-permute-start.6 = (f32[192,128]{1,0:T(8,128)}, f32[192,128]{1,0:T(8,128)S(1)}, u32[]{:S(2)}, u32[]{:S(2)}) collective-permute-start(f32[192,128]{1,0:T(8,128)} %get-tuple-element.18), channel_id=1, source_target_pairs={{0,32},{16,48},{1,33},{17,49},{2,34},{18,50},{3,35},{19,51},{4,36}... | collective-permute-start | bytes 294920 | tf_op jit(solution)/shard_map/ppermute | solution.py:155
  45.7 1.9 collective-permute-start.8
  50.6 5.3 %shard_map.60 = (f32[192,128]{1,0:T(8,128)}, f32[192,128]{1,0:T(8,128)}) custom-call(s32[2]{0:T(128)} %fusion.9.pick_ref, f32[384,768]{1,0:T(8,128)} %pad_maximum_fusion.3.one_ref.two_ref, f32[384,768]{1,0:T(8,128)} %pad_maximum_fusion.3.one_ref.two_ref, f32[384,384]{1,0:T(8,128)} %get-tuple-element.17.d_ref, ...), custom_call_target="tpu_custom_call" | custom-call | tf_op jit(solution)/shard_map/pallas_call | solution.py:109
  56.0 12.5 %collective-permute-start.7 = (f32[192,128]{1,0:T(8,128)}, f32[192,128]{1,0:T(8,128)}, u32[]{:S(2)}, u32[]{:S(2)}) collective-permute-start(f32[192,128]{1,0:T(8,128)} %get-tuple-element.20), channel_id=1, source_target_pairs={{32,64},{48,80},{0,96},{16,112},{33,65},{49,81},{1,97},{17,113},{3... | collective-permute-start | bytes 294920 | tf_op jit(solution)/shard_map/ppermute | solution.py:155
  68.5 3.5 %collective-permute-start.10 = (f32[192,128]{1,0:T(8,128)}, f32[192,128]{1,0:T(8,128)}, u32[]{:S(2)}, u32[]{:S(2)}) collective-permute-start(f32[192,128]{1,0:T(8,128)} %get-tuple-element.20), channel_id=1, source_target_pairs={{32,96},{48,112},{0,128},{16,144},{33,97},{49,113},{1,129},{17,145... | collective-permute-start | bytes 294920 | tf_op jit(solution)/shard_map/ppermute | solution.py:155
  73.2 5.3 %shard_map.61 = (f32[192,128]{1,0:T(8,128)}, f32[192,128]{1,0:T(8,128)}) custom-call(s32[2]{0:T(128)} %fusion.8.pick_ref, f32[384,768]{1,0:T(8,128)} %pad_maximum_fusion.3.one_ref.two_ref, f32[384,768]{1,0:T(8,128)} %pad_maximum_fusion.3.one_ref.two_ref, f32[384,384]{1,0:T(8,128)} %get-tuple-element.17.d_ref, f32[192,128]{1,0:T(8,128)} %get-tuple-element.19.rest_ref, ...), custom_call_target="tpu_custom_call" | custom-call | tf_op jit(solution)/shard_map/pallas_call | solution.py:109
  78.5 12.8 %collective-permute-start.9 = (f32[192,128]{1,0:T(8,128)}, f32[192,128]{1,0:T(8,128)S(1)}, u32[]{:S(2)}, u32[]{:S(2)}) collective-permute-start(f32[192,128]{1,0:T(8,128)} %get-tuple-element.22), channel_id=1, source_target_pairs={{64,96},{80,112},{32,128},{48,144},{0,160},{16,176},{65,97},{81,11... | collective-permute-start | bytes 294920 | tf_op jit(solution)/shard_map/ppermute | solution.py:155
  94.9 5.2 %shard_map.62 = (f32[192,128]{1,0:T(8,128)}, f32[192,128]{1,0:T(8,128)}) custom-call(s32[2]{0:T(128)} %add_convert_fusion.2.pick_ref, f32[384,768]{1,0:T(8,128)} %pad_maximum_fusion.3.one_ref.two_ref, f32[384,768]{1,0:T(8,128)} %pad_maximum_fusion.2.two_ref.one_ref, f32[384,384]{1,0:T(8,128)} %get-tuple-element.17.d_ref, ...), custom_call_target="tpu_custom_call" | custom-call | tf_op jit(solution)/shard_map/pallas_call | solution.py:109
  100.1 1.4 collective-permute-start.11
  102.3 4.4 %collective-permute-done.11.near_ref = f32[192,128]{1,0:T(8,128)S(1)} collective-permute-done((f32[192,128]{1,0:T(8,128)}, f32[192,128]{1,0:T(8,128)S(1)}, u32[]{:S(2)}, u32[]{:S(2)}) %collective-permute-start.11) | collective-permute-done | bytes 98336 | tf_op jit(solution)/shard_map/ppermute | solution.py:155
  107.3 5.2 %shard_map.63 = (f32[192,128]{1,0:T(8,128)}, f32[192,128]{1,0:T(8,128)}) custom-call(s32[2]{0:T(128)} %add_convert_fusion.1.pick_ref, f32[384,768]{1,0:T(8,128)} %pad_maximum_fusion.3.one_ref.two_ref, f32[384,768]{1,0:T(8,128)} %pad_maximum_fusion.2.two_ref.one_ref, f32[384,384]{1,0:T(8,128)} %get-tuple-element.17.d_ref, ...), custom_call_target="tpu_custom_call" | custom-call | tf_op jit(solution)/shard_map/pallas_call | solution.py:109
  115.8 5.2 %shard_map.64 = (f32[192,128]{1,0:T(8,128)}, f32[192,128]{1,0:T(8,128)}) custom-call(s32[2]{0:T(128)} %add_convert_fusion.pick_ref, f32[384,768]{1,0:T(8,128)} %pad_maximum_fusion.2.two_ref.one_ref, f32[384,768]{1,0:T(8,128)} %pad_maximum_fusion.1.two_ref.one_ref, f32[384,384]{1,0:T(8,128)} %get-tuple-element.17.d_ref, ...), custom_call_target="tpu_custom_call" | custom-call | tf_op jit(solution)/shard_map/pallas_call | solution.py:109
  124.3 5.2 %shard_map.65 = (f32[192,128]{1,0:T(8,128)}, f32[192,128]{1,0:T(8,128)}) custom-call(s32[2]{0:T(128)} %fusion.7.pick_ref, f32[384,768]{1,0:T(8,128)} %pad_maximum_fusion.1.two_ref.one_ref, f32[384,768]{1,0:T(8,128)} %pad_maximum_fusion.1.two_ref.one_ref, f32[384,384]{1,0:T(8,128)} %get-tuple-element.17.d_ref, f32[192,128]{1,0:T(8,128)} %get-tuple-element.27.rest_ref, ...), custom_call_target="tpu_custom_call" | custom-call | tf_op jit(solution)/shard_map/pallas_call | solution.py:109
  132.2 5.2 %shard_map.66 = (f32[192,128]{1,0:T(8,128)}, f32[192,128]{1,0:T(8,128)}) custom-call(s32[2]{0:T(128)} %fusion.6.pick_ref, f32[384,768]{1,0:T(8,128)} %pad_maximum_fusion.one_ref.two_ref, f32[384,768]{1,0:T(8,128)} %pad_maximum_fusion.one_ref.two_ref, f32[384,384]{1,0:T(8,128)} %get-tuple-element.17.d_ref, f32[192,128]{1,0:T(8,128)} %get-tuple-element.29.rest_ref, ...), custom_call_target="tpu_custom_call" | custom-call | tf_op jit(solution)/shard_map/pallas_call | solution.py:109
  137.4 1.6 collective-permute-start.19
  140.1 2.2 collective-permute-done.19
  142.5 3.3 %collective-permute-start.21 = (f32[192,128]{1,0:T(8,128)S(1)}, f32[192,128]{1,0:T(8,128)S(1)}, u32[]{:S(2)}, u32[]{:S(2)}) collective-permute-start(f32[192,128]{1,0:T(8,128)S(1)} %maximum_select_fusion.1), channel_id=1, source_target_pairs={{0,0},{4,1},{8,2},{12,3},{16,4},{20,5},{24,6},{28,7},{32,8},{36,9}... | collective-permute-start | bytes 294920 | tf_op jit(solution)/shard_map/ppermute | solution.py:181
  145.8 6.6 %collective-permute-done.21 = f32[192,128]{1,0:T(8,128)S(1)} collective-permute-done((f32[192,128]{1,0:T(8,128)S(1)}, f32[192,128]{1,0:T(8,128)S(1)}, u32[]{:S(2)}, u32[]{:S(2)}) %collective-permute-start.21) | collective-permute-done | bytes 98336 | tf_op jit(solution)/shard_map/ppermute | solution.py:181
  153.7 7.7 %all-to-all-start = ((f32[16,192,128]{2,1,0:T(8,128)}), f32[16,192,128]{2,1,0:T(8,128)S(1)}, u32[]{:S(2)}, u32[]{:S(2)}) async-start(f32[16,192,128]{2,1,0:T(8,128)} %broadcast_in_dim.8), calls=%async_computation | async-start | bytes 3145728 | tf_op jit(solution)/shard_map/all_to_all | solution.py:187
  162.8 2.2 collective-permute-start.24
  165.1 19.9 %collective-permute-done.22 = f32[192,128]{1,0:T(8,128)S(1)} collective-permute-done((f32[192,128]{1,0:T(8,128)S(1)}, f32[192,128]{1,0:T(8,128)S(1)}, u32[]{:S(2)}, u32[]{:S(2)}) %collective-permute-start.22) | collective-permute-done | bytes 98336 | tf_op jit(solution)/shard_map/ppermute | solution.py:185
  185.0 3.3 %convolution_bitcast_fusion = f32[4,128,128]{2,1,0:T(8,128)} fusion(f32[4,4,192,128]{3,2,1,0:T(8,128)S(1)} %bitcast.31, f32[1,192,128]{2,1,0:T(8,128)S(1)} %bitcast.34, f32[1,192,128]{2,1,0:T(8,128)S(1)} %bitcast.33, f32[1,192,128]{2,1,0:T(8,128)S(1)} %bitcast.32, f32[1,192,128]{2,1,0:T(8,128)S(1)} %maximum_select_fusion.2), kind=kOutput, calls=%fused_computation.6 | convolution fusion | flops 604274688 | bytes 2228224 | tf_op jit(solution)/shard_map/jmra,jrb->mab/dot_general | solution.py:189
  188.3 21.9 %all-to-all-start.1 = ((f32[4,128,128]{2,1,0:T(8,128)}), f32[4,128,128]{2,1,0:T(8,128)S(1)}, u32[]{:S(2)}, u32[]{:S(2)}) async-start(f32[4,128,128]{2,1,0:T(8,128)} %convolution_bitcast_fusion), calls=%async_computation.1 | async-start | bytes 524288 | tf_op jit(solution)/shard_map/all_to_all | solution.py:192
  210.9 10.5 %all-to-all-done.1 = f32[4,128,128]{2,1,0:T(8,128)S(1)} async-done(((f32[4,128,128]{2,1,0:T(8,128)}), f32[4,128,128]{2,1,0:T(8,128)S(1)}, u32[]{:S(2)}, u32[]{:S(2)}) %all-to-all-start.1) | async-done | bytes 262176 | tf_op jit(solution)/shard_map/all_to_all | solution.py:192
  (103 shorter events, 32.8 us)
Async XLA Ops:
  0.7 12.9 %copy-start.18 = (f32[32]{0:T(128)S(1)}, f32[32]{0:T(128)}, u32[]{:S(2)}) copy-start(f32[32]{0:T(128)} %param.6) | copy-start | bytes 388
  0.7 15.3 %copy-start.13 = (f32[32,192]{1,0:T(8,128)S(1)}, f32[32,192]{1,0:T(8,128)}, u32[]{:S(2)}) copy-start(f32[32,192]{1,0:T(8,128)} %param.4) | copy-start | bytes 73732
  2.5 43.3 %collective-permute-start.5 = (f32[192,768]{1,0:T(8,128)S(1)}, f32[192,768]{1,0:T(8,128)}, u32[]{:S(2)}, u32[]{:S(2)}) collective-permute-start(f32[192,768]{1,0:T(8,128)S(1)} %get-tuple-element.32), channel_id=1, source_target_pairs={{32,48},{48,32},{64,80},{80,64},{96,112},{112,96},{128,144},{144,1... | collective-permute-start | bytes 1769480 | tf_op jit(solution)/shard_map/ppermute | solution.py:149
  5.0 22.6 %copy-start = (f32[192,384]{1,0:T(8,128)}, f32[192,384]{1,0:T(8,128)S(1)}, u32[]{:S(2)}) copy-start(f32[192,384]{1,0:T(8,128)S(1)} %constant_dynamic-slice_fusion.3.own_ref) | copy-start | bytes 884740
  5.0 22.6 %collective-permute-start.1 = (f32[192,384]{1,0:T(8,128)S(1)}, f32[192,384]{1,0:T(8,128)}, u32[]{:S(2)}, u32[]{:S(2)}) collective-permute-start(f32[192,384]{1,0:T(8,128)S(1)} %constant_dynamic-slice_fusion.3.own_ref), channel_id=1, source_target_pairs={{0,16},{16,0},{32,48},{48,32},{64,80},{80,64},{96,112},{112,96},{1... | collective-permute-start | bytes 884744 | tf_op jit(solution)/shard_map/ppermute | solution.py:140
  6.6 11.3 %collective-permute-start.20 = (f32[32,128]{1,0:T(8,128)S(1)}, f32[32,128]{1,0:T(8,128)S(1)}, u32[]{:S(2)}, u32[]{:S(2)}) collective-permute-start(f32[32,128]{1,0:T(8,128)S(1)} %copy-done.14), channel_id=1, source_target_pairs={{0,0},{1,16},{2,32},{3,48},{4,64},{5,80},{6,96},{7,112},{8,128},{9... | collective-permute-start | bytes 49160 | tf_op jit(solution)/shard_map/ppermute | solution.py:172
  11.3 57.2 %collective-permute-start.4 = (f32[192,768]{1,0:T(8,128)S(1)}, f32[192,768]{1,0:T(8,128)}, u32[]{:S(2)}, u32[]{:S(2)}) collective-permute-start(f32[192,768]{1,0:T(8,128)S(1)} %get-tuple-element.35), channel_id=1, source_target_pairs={{96,112},{112,96},{128,144},{144,128},{160,176},{176,160},{192,208... | collective-permute-start | bytes 1769480 | tf_op jit(solution)/shard_map/ppermute | solution.py:149
  12.8 88.7 %collective-permute-start.3 = (f32[192,768]{1,0:T(8,128)S(1)}, f32[192,768]{1,0:T(8,128)S(1)}, u32[]{:S(2)}, u32[]{:S(2)}) collective-permute-start(f32[192,768]{1,0:T(8,128)S(1)} %get-tuple-element.33), channel_id=1, source_target_pairs={{160,176},{176,160},{192,208},{208,192},{224,240},{240,224},{161,1... | collective-permute-start | bytes 1769480 | tf_op jit(solution)/shard_map/ppermute | solution.py:149
  19.6 5.6 %collective-permute-start.2 = (f32[192,128]{1,0:T(8,128)S(1)}, f32[192,128]{1,0:T(8,128)S(1)}, u32[]{:S(2)}, u32[]{:S(2)}) collective-permute-start(f32[192,128]{1,0:T(8,128)S(1)} %exponential_multiply_fusion), channel_id=1, source_target_pairs={{0,16},{16,0},{32,48},{48,32},{64,80},{80,64},{96,112},{112,96},{1... | collective-permute-start | bytes 294920 | tf_op jit(solution)/shard_map/ppermute | solution.py:142
  25.2 96.5 %collective-permute-start = (f32[192,768]{1,0:T(8,128)S(1)}, f32[192,768]{1,0:T(8,128)}, u32[]{:S(2)}, u32[]{:S(2)}) collective-permute-start(f32[192,768]{1,0:T(8,128)S(1)} %get-tuple-element.34), channel_id=1, source_target_pairs={{224,240},{240,224},{225,241},{241,225},{226,242},{242,226},{227,2... | collective-permute-start | bytes 1769480 | tf_op jit(solution)/shard_map/ppermute | solution.py:149
  35.4 14.5 %collective-permute-start.6 = (f32[192,128]{1,0:T(8,128)}, f32[192,128]{1,0:T(8,128)S(1)}, u32[]{:S(2)}, u32[]{:S(2)}) collective-permute-start(f32[192,128]{1,0:T(8,128)} %get-tuple-element.18), channel_id=1, source_target_pairs={{0,32},{16,48},{1,33},{17,49},{2,34},{18,50},{3,35},{19,51},{4,36}... | collective-permute-start | bytes 294920 | tf_op jit(solution)/shard_map/ppermute | solution.py:155
  45.7 27.4 %collective-permute-start.8 = (f32[192,128]{1,0:T(8,128)}, f32[192,128]{1,0:T(8,128)}, u32[]{:S(2)}, u32[]{:S(2)}) collective-permute-start(f32[192,128]{1,0:T(8,128)} %get-tuple-element.18), channel_id=1, source_target_pairs={{0,64},{16,80},{1,65},{17,81},{2,66},{18,82},{3,67},{19,83},{4,68}... | collective-permute-start | bytes 294920 | tf_op jit(solution)/shard_map/ppermute | solution.py:155
  56.0 17.2 %collective-permute-start.7 = (f32[192,128]{1,0:T(8,128)}, f32[192,128]{1,0:T(8,128)}, u32[]{:S(2)}, u32[]{:S(2)}) collective-permute-start(f32[192,128]{1,0:T(8,128)} %get-tuple-element.20), channel_id=1, source_target_pairs={{32,64},{48,80},{0,96},{16,112},{33,65},{49,81},{1,97},{17,113},{3... | collective-permute-start | bytes 294920 | tf_op jit(solution)/shard_map/ppermute | solution.py:155
  68.5 25.2 %collective-permute-start.10 = (f32[192,128]{1,0:T(8,128)}, f32[192,128]{1,0:T(8,128)}, u32[]{:S(2)}, u32[]{:S(2)}) collective-permute-start(f32[192,128]{1,0:T(8,128)} %get-tuple-element.20), channel_id=1, source_target_pairs={{32,96},{48,112},{0,128},{16,144},{33,97},{49,113},{1,129},{17,145... | collective-permute-start | bytes 294920 | tf_op jit(solution)/shard_map/ppermute | solution.py:155
  78.5 15.8 %collective-permute-start.9 = (f32[192,128]{1,0:T(8,128)}, f32[192,128]{1,0:T(8,128)S(1)}, u32[]{:S(2)}, u32[]{:S(2)}) collective-permute-start(f32[192,128]{1,0:T(8,128)} %get-tuple-element.22), channel_id=1, source_target_pairs={{64,96},{80,112},{32,128},{48,144},{0,160},{16,176},{65,97},{81,11... | collective-permute-start | bytes 294920 | tf_op jit(solution)/shard_map/ppermute | solution.py:155
  92.4 9.8 %collective-permute-start.12 = (f32[192,128]{1,0:T(8,128)}, f32[192,128]{1,0:T(8,128)S(1)}, u32[]{:S(2)}, u32[]{:S(2)}) collective-permute-start(f32[192,128]{1,0:T(8,128)} %get-tuple-element.22), channel_id=1, source_target_pairs={{64,128},{80,144},{32,160},{48,176},{0,192},{16,208},{65,129},{81,... | collective-permute-start | bytes 294920 | tf_op jit(solution)/shard_map/ppermute | solution.py:155
  100.1 6.6 %collective-permute-start.11 = (f32[192,128]{1,0:T(8,128)}, f32[192,128]{1,0:T(8,128)S(1)}, u32[]{:S(2)}, u32[]{:S(2)}) collective-permute-start(f32[192,128]{1,0:T(8,128)} %get-tuple-element.24), channel_id=1, source_target_pairs={{96,128},{112,144},{64,160},{80,176},{32,192},{48,208},{0,224},{16... | collective-permute-start | bytes 294920 | tf_op jit(solution)/shard_map/ppermute | solution.py:155
  101.6 13.5 %collective-permute-start.14 = (f32[192,128]{1,0:T(8,128)S(1)}, f32[192,128]{1,0:T(8,128)S(1)}, u32[]{:S(2)}, u32[]{:S(2)}) collective-permute-start(f32[192,128]{1,0:T(8,128)S(1)} %copy-done.16), channel_id=1, source_target_pairs={{96,160},{112,176},{64,192},{80,208},{32,224},{48,240},{97,161},{1... | collective-permute-start | bytes 294920 | tf_op jit(solution)/shard_map/ppermute | solution.py:155
  112.5 2.6 %collective-permute-start.13 = (f32[192,128]{1,0:T(8,128)}, f32[192,128]{1,0:T(8,128)S(1)}, u32[]{:S(2)}, u32[]{:S(2)}) collective-permute-start(f32[192,128]{1,0:T(8,128)} %get-tuple-element.26), channel_id=1, source_target_pairs={{128,160},{144,176},{96,192},{112,208},{64,224},{80,240},{129,161}... | collective-permute-start | bytes 294920 | tf_op jit(solution)/shard_map/ppermute | solution.py:155
  114.4 9.1 %collective-permute-start.16 = (f32[192,128]{1,0:T(8,128)S(1)}, f32[192,128]{1,0:T(8,128)S(1)}, u32[]{:S(2)}, u32[]{:S(2)}) collective-permute-start(f32[192,128]{1,0:T(8,128)S(1)} %copy-done.15), channel_id=1, source_target_pairs={{128,192},{144,208},{96,224},{112,240},{129,193},{145,209},{97,225... | collective-permute-start | bytes 294920 | tf_op jit(solution)/shard_map/ppermute | solution.py:155
  120.9 2.7 %collective-permute-start.15 = (f32[192,128]{1,0:T(8,128)}, f32[192,128]{1,0:T(8,128)S(1)}, u32[]{:S(2)}, u32[]{:S(2)}) collective-permute-start(f32[192,128]{1,0:T(8,128)} %get-tuple-element.28), channel_id=1, source_target_pairs={{160,192},{176,208},{128,224},{144,240},{161,193},{177,209},{129,2... | collective-permute-start | bytes 294920 | tf_op jit(solution)/shard_map/ppermute | solution.py:155
  122.9 8.6 %collective-permute-start.18 = (f32[192,128]{1,0:T(8,128)S(1)}, f32[192,128]{1,0:T(8,128)S(1)}, u32[]{:S(2)}, u32[]{:S(2)}) collective-permute-start(f32[192,128]{1,0:T(8,128)S(1)} %copy-done.17), channel_id=1, source_target_pairs={{160,224},{176,240},{161,225},{177,241},{162,226},{178,242},{163,2... | collective-permute-start | bytes 294920 | tf_op jit(solution)/shard_map/ppermute | solution.py:155
  129.5 2.0 collective-permute-start.17
  137.4 4.8 %collective-permute-start.19 = (f32[192,128]{1,0:T(8,128)}, f32[192,128]{1,0:T(8,128)S(1)}, u32[]{:S(2)}, u32[]{:S(2)}) collective-permute-start(f32[192,128]{1,0:T(8,128)} %get-tuple-element.31), channel_id=1, source_target_pairs={{0,16},{16,0},{32,48},{48,32},{64,80},{80,64},{96,112},{112,96},{1... | collective-permute-start | bytes 294920 | tf_op jit(solution)/shard_map/ppermute | solution.py:170
  142.5 20.3 %copy-start.11 = (f32[192,128]{1,0:T(8,128)}, f32[192,128]{1,0:T(8,128)S(1)}, u32[]{:S(2)}) copy-start(f32[192,128]{1,0:T(8,128)S(1)} %maximum_select_fusion.1) | copy-start | bytes 294916
  142.5 9.9 %collective-permute-start.21 = (f32[192,128]{1,0:T(8,128)S(1)}, f32[192,128]{1,0:T(8,128)S(1)}, u32[]{:S(2)}, u32[]{:S(2)}) collective-permute-start(f32[192,128]{1,0:T(8,128)S(1)} %maximum_select_fusion.1), channel_id=1, source_target_pairs={{0,0},{4,1},{8,2},{12,3},{16,4},{20,5},{24,6},{28,7},{32,8},{36,9}... | collective-permute-start | bytes 294920 | tf_op jit(solution)/shard_map/ppermute | solution.py:181
  153.7 31.3 %all-to-all-start = ((f32[16,192,128]{2,1,0:T(8,128)}), f32[16,192,128]{2,1,0:T(8,128)S(1)}, u32[]{:S(2)}, u32[]{:S(2)}) async-start(f32[16,192,128]{2,1,0:T(8,128)} %broadcast_in_dim.8), calls=%async_computation | async-start | bytes 3145728 | tf_op jit(solution)/shard_map/all_to_all | solution.py:187
  161.5 23.5 %collective-permute-start.22 = (f32[192,128]{1,0:T(8,128)S(1)}, f32[192,128]{1,0:T(8,128)S(1)}, u32[]{:S(2)}, u32[]{:S(2)}) collective-permute-start(f32[192,128]{1,0:T(8,128)S(1)} %maximum_select_fusion.1), channel_id=1, source_target_pairs={{0,16},{16,0},{32,48},{48,32},{64,80},{80,64},{96,112},{112,96},{1... | collective-permute-start | bytes 294920 | tf_op jit(solution)/shard_map/ppermute | solution.py:185
  162.8 22.2 %collective-permute-start.23 = (f32[192,128]{1,0:T(8,128)S(1)}, f32[192,128]{1,0:T(8,128)S(1)}, u32[]{:S(2)}, u32[]{:S(2)}) collective-permute-start(f32[192,128]{1,0:T(8,128)S(1)} %maximum_select_fusion.1), channel_id=1, source_target_pairs={{0,32},{16,48},{32,0},{48,16},{64,96},{80,112},{96,64},{112,80},{1... | collective-permute-start | bytes 294920 | tf_op jit(solution)/shard_map/ppermute | solution.py:185
  162.8 22.2 %collective-permute-start.24 = (f32[192,128]{1,0:T(8,128)S(1)}, f32[192,128]{1,0:T(8,128)S(1)}, u32[]{:S(2)}, u32[]{:S(2)}) collective-permute-start(f32[192,128]{1,0:T(8,128)S(1)} %maximum_select_fusion.1), channel_id=1, source_target_pairs={{0,48},{16,32},{32,16},{48,0},{64,112},{80,96},{96,80},{112,64},{1... | collective-permute-start | bytes 294920 | tf_op jit(solution)/shard_map/ppermute | solution.py:185
  165.0 45.3 %copy-start.12 = (f32[32,128]{1,0:T(8,128)S(1)}, f32[32,128]{1,0:T(8,128)}, u32[]{:S(2)}) copy-start(f32[32,128]{1,0:T(8,128)} %get-tuple-element.56) | copy-start | bytes 49156
  188.3 33.1 %all-to-all-start.1 = ((f32[4,128,128]{2,1,0:T(8,128)}), f32[4,128,128]{2,1,0:T(8,128)S(1)}, u32[]{:S(2)}, u32[]{:S(2)}) async-start(f32[4,128,128]{2,1,0:T(8,128)} %convolution_bitcast_fusion), calls=%async_computation.1 | async-start | bytes 524288 | tf_op jit(solution)/shard_map/all_to_all | solution.py:192
  (14 other events, 21.6 us)

commit v4 on v3

v4 whole, which is shorter than its diff:
```python
import jax
import jax.numpy as jnp
from jax import lax
from jax.experimental import pallas as pl
from jax.experimental.pallas import tpu as pltpu
from jax.sharding import PartitionSpec as P

HIGH = lax.Precision.HIGHEST
BASE = 32
QUAD = 4


def matern(first_set, second_set):
    differ = first_set[:, :, None] - second_set[:, None, :]
    radius = jnp.sqrt(5.0 * jnp.sum(differ * differ, axis=0))
    return (1.0 + radius + radius * radius / 3.0) * jnp.exp(-radius)


def mm(a, b):
    return jnp.dot(a, b, precision=HIGH, preferred_element_type=jnp.float32)


def invert_into(l_ref, d_ref):
    size = l_ref.shape[0]
    count = size // BASE
    rows = lax.broadcasted_iota(jnp.int32, (BASE, BASE), 0)
    cols = lax.broadcasted_iota(jnp.int32, (BASE, BASE), 1)
    strict, solved = [], []
    for k in range(count):
        block = l_ref[k * BASE : (k + 1) * BASE, k * BASE : (k + 1) * BASE]
        diag = jnp.sum(jnp.where(rows == cols, block, 0.0), axis=1, keepdims=True)
        inv = 1.0 / diag
        strict.append(jnp.where(rows > cols, block * inv, 0.0))
        solved.append(jnp.where(rows == cols, inv, 0.0))
    for r in range(BASE - 1):
        for k in range(count):
            solved[k] = solved[k] - strict[k][:, r : r + 1] * solved[k][r : r + 1, :]
    d_ref[...] = jnp.zeros_like(d_ref)
    for k in range(count):
        d_ref[k * BASE : (k + 1) * BASE, k * BASE : (k + 1) * BASE] = solved[k]
    for k in range(0, count - 1, 2):
        a, b, c = k * BASE, (k + 1) * BASE, (k + 2) * BASE
        d_ref[b:c, a:b] = -mm(solved[k + 1], mm(l_ref[b:c, a:b], solved[k]))
    low = 2 * BASE
    while low < size:
        high = low + 2 * BASE
        d_ref[low:high, 0:low] = -mm(
            d_ref[low:high, low:high], mm(l_ref[low:high, 0:low], d_ref[0:low, 0:low])
        )
        low = high


def across_rows(a, b):
    return lax.dot_general(
        a, b, (((1,), (1,)), ((), ())), precision=HIGH, preferred_element_type=jnp.float32
    )


def own_kernel(side_ref, own_ref, out_ref, l_ref, d_ref):
    height = own_ref.shape[0]
    even = side_ref[0] == 0
    left, right = own_ref[:, 0:height], own_ref[:, height:]
    l_ref[...] = jnp.where(even, left, right)
    invert_into(l_ref, d_ref)
    out_ref[:, 0:height] = jnp.where(even, d_ref[...], left)
    out_ref[:, height:] = jnp.where(even, 0.0, d_ref[...])


def own_inverse(side, own):
    height = own.shape[0]
    square = pltpu.VMEM((height, height), jnp.float32)
    return pl.pallas_call(
        own_kernel,
        in_specs=[pl.BlockSpec(memory_space=pltpu.SMEM), pl.BlockSpec(memory_space=pltpu.VMEM)],
        out_shape=jax.ShapeDtypeStruct(own.shape, jnp.float32),
        scratch_shapes=[square, square],
    )(side, own)


def join_kernel(side_ref, own_ref, other_ref, cross_ref, mine_ref, yours_ref, x_ref, d_ref):
    height = own_ref.shape[0]
    even = side_ref[0] == 0
    own, other = own_ref[...], other_ref[...]
    upper = jnp.where(even, own[:, 0:height], other[:, 0:height])
    lower = jnp.where(even, other, own)
    d_ref[0:height, 0:height] = upper
    d_ref[0:height, height:] = jnp.zeros((height, height), jnp.float32)
    d_ref[height:, height:] = lower[:, height:]
    d_ref[height:, 0:height] = -mm(lower[:, height:], mm(lower[:, 0:height], upper))
    left, right = d_ref[:, 0:height], d_ref[:, height:]
    mine_ref[...] = jnp.where(even, left, right)
    yours_ref[...] = jnp.where(even, right, left)
    x_ref[...] = across_rows(cross_ref[...], d_ref[...])


def join(side, own, other, cross):
    height = own.shape[0]
    tall = jax.ShapeDtypeStruct((2 * height, height), jnp.float32)
    return pl.pallas_call(
        join_kernel,
        in_specs=[pl.BlockSpec(memory_space=pltpu.SMEM)] + [pl.BlockSpec(memory_space=pltpu.VMEM)] * 3,
        out_shape=[tall, tall, jax.ShapeDtypeStruct(cross.shape, jnp.float32)],
        scratch_shapes=[pltpu.VMEM((2 * height, 2 * height), jnp.float32)],
    )(side, own, other, cross)


def shards(archive_inputs, candidate_inputs, lengthscales, factor):
    height = factor.shape[0]
    width = candidate_inputs.shape[1]
    chain = lax.axis_size("chain")
    cand = lax.axis_size("cand")
    quads = chain // QUAD
    position = lax.axis_index("chain")
    inside = [[QUAD * g + i for i in range(QUAD)] for g in range(quads)]
    across = [[QUAD * g + i for g in range(quads)] for i in range(QUAD)]
    layers = chain // 2
    layer, side = position // 2, position % 2
    odd = layer % 2
    side_word = jnp.full((1,), side, jnp.int32)
    pair_all = [(p, p ^ 1) for p in range(chain)]
    scaling = 1.0 / lengthscales
    scaled_candidates = candidate_inputs * scaling[:, None]

    def both(own, other, axis):
        return jnp.where(
            side == 0,
            jnp.concatenate([own, other], axis=axis),
            jnp.concatenate([other, own], axis=axis),
        )

    def after(value, *events):
        return lax.optimization_barrier((value, *events))[0]

    other_archive = lax.ppermute(archive_inputs, "chain", pair_all)
    own_diagonal = lax.dynamic_slice_in_dim(factor, layer * 2 * height, 2 * height, 1)
    own_part = own_inverse(side_word, own_diagonal)
    other_part = lax.ppermute(own_part, "chain", pair_all)
    half = width // 2
    columns = lax.dynamic_slice_in_dim(scaled_candidates, side * half, half, 1)
    cross = matern(columns, both(archive_inputs, other_archive, 1) * scaling[:, None])
    for_mine, for_yours, solved = join(side_word, own_part, other_part, cross)

    def hop(value, pairs):
        return lax.ppermute(value, "chain", [(2 * a + i, 2 * b + i) for a, b in pairs for i in range(2)])

    span = 2 * height
    core = lax.axis_index("cand") % 2
    chunks = [factor[:, k * span : (k + 1) * span] for k in range(layers)]
    lefts, rights = [], []
    for s in range(layers // 2):
        left = jnp.where(odd == 1, chunks[max(2 * s - 1, 0)], chunks[2 * s])
        right = jnp.where(odd == 1, chunks[2 * s], chunks[2 * s + 1])
        sent = after(jnp.where(core == 0, left, right), other_part if s == 0 else solved)
        got = lax.ppermute(sent, "chain", [(p, p ^ 1) for p in range(chain) if p // 2 >= 2 * s + 1])
        users = [p for p in range(chain) if p // 2 >= 2 * s + 1]
        twins = [(p * cand + c, p * cand + (c ^ 1)) for p in users for c in range(cand)]
        twin = lax.ppermute(got, ("chain", "cand"), twins)
        yours_left = jnp.where(core == 0, got, twin)
        yours_right = jnp.where(core == 0, twin, got)
        mine = jnp.concatenate([left, right], axis=1)
        yours = jnp.concatenate([yours_left, yours_right], axis=1)
        slab = mm(for_mine, mine) + mm(for_yours, yours)
        lefts.append(after(slab[:, :span]))
        rights.append(after(slab[:, span:]))

    far = None
    for t in range(layers - 1):
        near = hop(solved, [(t - k, t + 1 + k) for k in range(layers) if t - k >= 0 and t + 1 + k < layers])
        pairs = [(t - k, t + 2 + k) for k in range(layers) if t - k >= 0 and t + 2 + k < layers]
        ahead = hop(solved, pairs) if pairs else None
        users = sorted({t - z // 2 for z in range(t + 1, min(2 * t + 1, layers - 1) + 1)})
        left, right = lefts[users[0]], rights[users[0]]
        if len(users) > 1:
            second = t - layer // 2 == users[1]
            left = after(jnp.where(second, lefts[users[1]], left))
            right = after(jnp.where(second, rights[users[1]], right))
        if far is not None:
            solved = after(solved - across_rows(far, left))
        solved = solved - across_rows(near, right)
        far = ahead
    other = lax.ppermute(solved, "chain", pair_all)
    rows = jnp.where(
        side == 0,
        jnp.concatenate([solved[:, :height], other[:, :height]], axis=0),
        jnp.concatenate([other[:, height:], solved[:, height:]], axis=0),
    ).T
    swap = [(a * cand + b, b * cand + a) for a in range(chain) for b in range(cand)]
    chosen = lax.ppermute(candidate_inputs, ("chain", "cand"), swap)

    turn = [
        ((QUAD * g + (i ^ j)) * cand + QUAD * m + i, (QUAD * g + i) * cand + QUAD * j + m)
        for g in range(quads)
        for i in range(QUAD)
        for j in range(QUAD)
        for m in range(cand // QUAD)
    ]
    turned = lax.ppermute(rows, ("chain", "cand"), turn)
    mine = [rows]
    for r in range(1, QUAD):
        pairs = [(QUAD * g + i, QUAD * g + (i ^ r)) for g in range(quads) for i in range(QUAD)]
        mine.append(lax.ppermute(rows, "chain", pairs))
    copies = jnp.broadcast_to(turned[None], (cand,) + turned.shape)
    others = lax.all_to_all(copies, "cand", 0, 0, tiled=True)
    others = others.reshape(QUAD, cand // QUAD, height, width)
    shares = jnp.einsum(
        "jmra,jrb->mab", others, jnp.stack(mine), precision=HIGH, preferred_element_type=jnp.float32
    )
    shared = lax.all_to_all(shares, "chain", 0, 0, axis_index_groups=across, tiled=True).sum(axis=0)
    prior_cov = matern(chosen * scaling[:, None], scaled_candidates)
    return (rows, prior_cov - shared)


def solution(mesh):
    return jax.shard_map(
        shards,
        mesh=mesh,
        in_specs=(P(None, "chain"), P(None, "cand"), P(), P("chain", None)),
        out_specs=(P("chain", "cand"), P("chain", "cand")),
        check_vma=False,
    )
```

time: 223 us -> 181 us (0.81)
  Pallas kernels: 44.4 us -> 7.42 us
  matrix products: 3.31 us -> 22.9 us
  other arithmetic: 16.5 us -> 7.91 us
  starting transfers between devices: 98.1 us -> 91.1 us
  local copies, waits for them, and re-layouts: 9.32 us -> 3.53 us
  waiting for transfers between devices: 49.3 us -> 45.7 us
    pallas_call x8 -> x2, Pallas kernels: 44.4 us -> 7.42 us  [the longest x1 4.16 us: own_inverse(): pl.pallas_call(own_kernel, in_specs=[pl.BlockSpec(memory_space=pltpu.SMEM...]
    dot_general x0 -> x21, matrix products: none -> 18.6 us  [the longest x13 9.62 us: across_rows(): lax.dot_general(a, b, (((1,), (1,)), ((), ())), precision=HIGH, preferred...]
    ppermute x13, starting transfers between devices: 48.3 us -> 40.3 us  [hop(): lax.ppermute(value, 'chain', [(2 * a + i, 2 * b + i) for a, b in pairs fo...]
    concatenate x4 -> x0, other arithmetic: 4.54 us -> none  [shards(): slabs.append(jnp.concatenate([upper, lower], axis=0))]
    another operation x7 -> x1, other arithmetic: 4.26 us -> 0.02 us  [shards(): jnp.stack(mine)]
    ppermute x13, waiting for transfers between devices: 4.97 us -> 1.78 us  [hop(): lax.ppermute(value, 'chain', [(2 * a + i, 2 * b + i) for a, b in pairs fo...]
    all_to_all x1, starting transfers between devices: 7.74 us -> 4.68 us  [shards(): others = lax.all_to_all(copies, 'cand', 0, 0, tiled=True)]
    dynamic_slice x2 -> x1, local copies, waits for them, and re-layouts: 2.75 us -> 0.07 us  [shards(): columns = lax.dynamic_slice_in_dim(scaled_candidates, side * half, half, 1)]
  transfers between devices with their start and end apart: 27 -> 31, of which waited for: 7 -> 8; matrix products, arithmetic and copies ran while one was open for 8% -> 13% of each run, Pallas kernels for 18% -> 2%
where the time goes in v4:
time: 181 us; the launch traced here: 180 us
  starting transfers between devices  91.1 us (50%)
  waiting for transfers between devices  45.7 us (25%)
  matrix products  22.9 us (13%)
  other arithmetic  7.91 us (4%)
  Pallas kernels  7.42 us (4%)
  local copies, waits for them, and re-layouts  3.53 us (2%)
    ppermute x13, starting transfers between devices, hop(): lax.ppermute(value, 'chain', [(2 * a + i, 2 * b + i) for a, b in pairs fo...  40.3 us
    all_to_all x1, starting transfers between devices, shards(): lax.all_to_all(shares, 'chain', 0, 0, axis_index_groups=across, tiled=True)  24 us
    ppermute x3, waiting for transfers between devices, shards(): mine.append(lax.ppermute(rows, 'chain', pairs))  20.4 us
    all_to_all x1, waiting for transfers between devices, shards(): lax.all_to_all(shares, 'chain', 0, 0, axis_index_groups=across, tiled=True)  10.4 us
    dot_general x13, matrix products, across_rows(): lax.dot_general(a, b, (((1,), (1,)), ((), ())), precision=HIGH, preferred...  9.62 us
    dot_general x8, matrix products, mm(): return jnp.dot(a, b, precision=HIGH, preferred_element_type=jnp.float32)  9.02 us
    ppermute x1, waiting for transfers between devices, shards(): turned = lax.ppermute(rows, ('chain', 'cand'), turn)  6.14 us
    all_to_all x1, starting transfers between devices, shards(): others = lax.all_to_all(copies, 'cand', 0, 0, tiled=True)  4.68 us
  transfers between devices with their start and end apart: 31, of which 8 were waited for; matrix products, arithmetic and copies ran while one was open for 13% of the time, Pallas kernels for 2%

profile of v4, /device:TPU:2, one launch (start us, length us, event | category | flops | bytes accessed | tf_op | source)
XLA Modules:
  0.0 179.9 jit_solution(16867760301072967383)
XLA Ops:
  0.7 2.9 %broadcast_select_fusion.8 = (f32[192,384]{1,0:T(8,128)S(1)}, f32[192,384]{1,0:T(8,128)S(1)}, f32[192,384]{1,0:T(8,128)S(1)}, f32[192,384]{1,0:T(8,128)S(1)}, f3...) fusion(pred[]{:T(512)S(6)} %eq.18, ...), kind=kLoop, calls=%fused_computation.64 | loop fusion | flops 811008 | bytes 6488070 | tf_op jit(solution)/shard_map/jit(_where)/select_n | solution.py:153
  3.6 4.2 %shard_map.59.own_ref = f32[192,384]{1,0:T(8,128)} custom-call(s32[1]{0:T(128)} %bitcast.side_ref, f32[192,384]{1,0:T(8,128)} %get-tuple-element.34.own_ref), custom_call_target="tpu_custom_call" | custom-call | tf_op jit(solution)/shard_map/pallas_call | solution.py:72
  7.8 1.6 collective-permute-start
  9.3 3.7 %collective-permute-start.24 = (f32[32,128]{1,0:T(8,128)S(1)}, f32[32,128]{1,0:T(8,128)S(1)}, u32[]{:S(2)}, u32[]{:S(2)}) collective-permute-start(f32[32,128]{1,0:T(8,128)S(1)} %copy-done.6), channel_id=1, source_target_pairs={{0,0},{1,16},{2,32},{3,48},{4,64},{5,80},{6,96},{7,112},{8,128},{9... | collective-permute-start | bytes 49160 | tf_op jit(solution)/shard_map/ppermute | solution.py:188
  13.8 2.0 %collective-permute-done.24 = f32[32,128]{1,0:T(8,128)S(1)} collective-permute-done((f32[32,128]{1,0:T(8,128)S(1)}, f32[32,128]{1,0:T(8,128)S(1)}, u32[]{:S(2)}, u32[]{:S(2)}) %collective-permute-start.24) | collective-permute-done | bytes 16416 | tf_op jit(solution)/shard_map/ppermute | solution.py:188
  18.8 1.4 collective-permute-start.3
  20.2 3.3 %shard_map.60 = (f32[384,192]{1,0:T(8,128)}, f32[384,192]{1,0:T(8,128)}, f32[64,384]{1,0:T(8,128)}) custom-call(s32[1]{0:T(128)} %bitcast.side_ref, f32[192,384]{1,0:T(8,128)} %shard_map.59.own_ref, f32[192,384]{1,0:T(8,128)} %copy-done.2, f32[64,384]{1,0:T(8,128)} %exponential_multiply_fusion.cross_ref), custom_call_target="tpu_custom_call" | custom-call | tf_op jit(solution)/shard_map/pallas_call | solution.py:99
  23.5 1.4 collective-permute-start.8
  26.2 1.4 collective-permute-start.4
  27.6 1.4 collective-permute-start.9
  29.0 8.5 %collective-permute-start.2 = (f32[64,384]{1,0:T(8,128)}, f32[64,384]{1,0:T(8,128)S(1)}, u32[]{:S(2)}, u32[]{:S(2)}) collective-permute-start(f32[64,384]{1,0:T(8,128)} %get-tuple-element.9), channel_id=1, source_target_pairs={{0,32},{16,48},{1,33},{17,49},{2,34},{18,50},{3,35},{19,51},{4,36}... | collective-permute-start | bytes 294920 | tf_op jit(solution)/shard_map/ppermute | solution.py:144
  37.5 1.3 collective-permute-start.5
  40.2 1.3 broadcast_select_fusion.13
  42.7 1.1 convolution_add_fusion.3
  45.4 8.8 %collective-permute-start.6 = (f32[64,384]{1,0:T(8,128)S(1)}, f32[64,384]{1,0:T(8,128)S(1)}, u32[]{:S(2)}, u32[]{:S(2)}) collective-permute-start(f32[64,384]{1,0:T(8,128)S(1)} %convolution_subtract_fusion.6), channel_id=1, source_target_pairs={{32,64},{48,80},{0,96},{16,112},{33,65},{49,81},{1,97},{17,113},{3... | collective-permute-start | bytes 294920 | tf_op jit(solution)/shard_map/ppermute | solution.py:144
  54.3 5.3 %collective-permute-start.7 = (f32[64,384]{1,0:T(8,128)S(1)}, f32[64,384]{1,0:T(8,128)S(1)}, u32[]{:S(2)}, u32[]{:S(2)}) collective-permute-start(f32[64,384]{1,0:T(8,128)S(1)} %convolution_subtract_fusion.6), channel_id=1, source_target_pairs={{32,96},{48,112},{0,128},{16,144},{33,97},{49,113},{1,129},{17,145... | collective-permute-start | bytes 294920 | tf_op jit(solution)/shard_map/ppermute | solution.py:144
  63.2 1.1 convolution_add_fusion.2
  65.6 1.1 convolution_add_fusion
  68.6 4.7 %collective-permute-start.10 = (f32[64,384]{1,0:T(8,128)S(1)}, f32[64,384]{1,0:T(8,128)S(1)}, u32[]{:S(2)}, u32[]{:S(2)}) collective-permute-start(f32[64,384]{1,0:T(8,128)S(1)} %sub.92), channel_id=1, source_target_pairs={{64,96},{80,112},{32,128},{48,144},{0,160},{16,176},{65,97},{81,11... | collective-permute-start | bytes 294920 | tf_op jit(solution)/shard_map/ppermute | solution.py:144
  73.3 1.3 collective-permute-start.11
  77.1 6.1 %collective-permute-start.12 = (f32[64,384]{1,0:T(8,128)S(1)}, f32[64,384]{1,0:T(8,128)S(1)}, u32[]{:S(2)}, u32[]{:S(2)}) collective-permute-start(f32[64,384]{1,0:T(8,128)S(1)} %sub.96), channel_id=1, source_target_pairs={{96,128},{112,144},{64,160},{80,176},{32,192},{48,208},{0,224},{16... | collective-permute-start | bytes 294920 | tf_op jit(solution)/shard_map/ppermute | solution.py:144
  95.2 3.9 %collective-permute-done.23 = f32[64,384]{1,0:T(8,128)S(1)} collective-permute-done((f32[64,384]{1,0:T(8,128)S(1)}, f32[64,384]{1,0:T(8,128)S(1)}, u32[]{:S(2)}, u32[]{:S(2)}) %collective-permute-start.23) | collective-permute-done | bytes 98336 | tf_op jit(solution)/shard_map/ppermute | solution.py:181
  99.2 3.7 %collective-permute-start.25 = (f32[192,128]{0,1:T(8,128)S(1)}, f32[192,128]{0,1:T(8,128)S(1)}, u32[]{:S(2)}, u32[]{:S(2)}) collective-permute-start(f32[192,128]{0,1:T(8,128)S(1)} %get-tuple-element.66), channel_id=1, source_target_pairs={{0,0},{4,1},{8,2},{12,3},{16,4},{20,5},{24,6},{28,7},{32,8},{36,9}... | collective-permute-start | bytes 294920 | tf_op jit(solution)/shard_map/ppermute | solution.py:197
  103.0 6.1 %collective-permute-done.25 = f32[192,128]{0,1:T(8,128)S(1)} collective-permute-done((f32[192,128]{0,1:T(8,128)S(1)}, f32[192,128]{0,1:T(8,128)S(1)}, u32[]{:S(2)}, u32[]{:S(2)}) %collective-permute-start.25) | collective-permute-done | bytes 98336 | tf_op jit(solution)/shard_map/ppermute | solution.py:197
  109.2 1.3 broadcast_in_dim.5
  110.5 4.7 %all-to-all-start = ((f32[16,192,128]{2,1,0:T(8,128)}), f32[16,192,128]{2,1,0:T(8,128)S(1)}, u32[]{:S(2)}, u32[]{:S(2)}) async-start(f32[16,192,128]{2,1,0:T(8,128)} %broadcast_in_dim.5), calls=%async_computation | async-start | bytes 3145728 | tf_op jit(solution)/shard_map/all_to_all | solution.py:203
  115.4 1.3 collective-permute-start.27
  116.8 1.9 %collective-permute-start.28 = (f32[192,128]{0,1:T(8,128)S(1)}, f32[192,128]{0,1:T(8,128)S(1)}, u32[]{:S(2)}, u32[]{:S(2)}) collective-permute-start(f32[192,128]{0,1:T(8,128)S(1)} %get-tuple-element.66), channel_id=1, source_target_pairs={{0,48},{16,32},{32,16},{48,0},{64,112},{80,96},{96,80},{112,64},{1... | collective-permute-start | bytes 294920 | tf_op jit(solution)/shard_map/ppermute | solution.py:201
  118.7 20.4 %collective-permute-done.26 = f32[192,128]{0,1:T(8,128)S(1)} collective-permute-done((f32[192,128]{0,1:T(8,128)S(1)}, f32[192,128]{0,1:T(8,128)S(1)}, u32[]{:S(2)}, u32[]{:S(2)}) %collective-permute-start.26) | collective-permute-done | bytes 98336 | tf_op jit(solution)/shard_map/ppermute | solution.py:201
  139.1 4.3 %convolution_bitcast_fusion = f32[4,128,128]{2,1,0:T(8,128)} fusion(f32[4,4,192,128]{3,2,1,0:T(8,128)S(1)} %bitcast.52, f32[1,192,128]{1,2,0:T(8,128)S(1)} %bitcast.55, f32[1,192,128]{1,2,0:T(8,128)S(1)} %bitcast.54, f32[1,192,128]{1,2,0:T(8,128)S(1)} %bitcast.53, f32[1,192,128]{1,2,0:T(8,128)S(1)} %get-tuple-element.65), kind=kOutput, calls=%fused_computation.6 | convolution fusion | flops 604274688 | bytes 2228224 | tf_op jit(solution)/shard_map/jmra,jrb->mab/dot_general | solution.py:205
  143.3 24.0 %all-to-all-start.1 = ((f32[4,128,128]{2,1,0:T(8,128)}), f32[4,128,128]{2,1,0:T(8,128)S(1)}, u32[]{:S(2)}, u32[]{:S(2)}) async-start(f32[4,128,128]{2,1,0:T(8,128)} %convolution_bitcast_fusion), calls=%async_computation.1 | async-start | bytes 524288 | tf_op jit(solution)/shard_map/all_to_all | solution.py:208
  168.8 10.4 %all-to-all-done.1 = f32[4,128,128]{2,1,0:T(8,128)S(1)} async-done(((f32[4,128,128]{2,1,0:T(8,128)}), f32[4,128,128]{2,1,0:T(8,128)S(1)}, u32[]{:S(2)}, u32[]{:S(2)}) %all-to-all-start.1) | async-done | bytes 262176 | tf_op jit(solution)/shard_map/all_to_all | solution.py:208
  (100 shorter events, 32.4 us)
Async XLA Ops:
  7.8 11.0 %collective-permute-start = (f32[192,384]{1,0:T(8,128)}, f32[192,384]{1,0:T(8,128)S(1)}, u32[]{:S(2)}, u32[]{:S(2)}) collective-permute-start(f32[192,384]{1,0:T(8,128)} %shard_map.59.own_ref), channel_id=1, source_target_pairs={{0,16},{16,0},{32,48},{48,32},{64,80},{80,64},{96,112},{112,96},{1... | collective-permute-start | bytes 884744 | tf_op jit(solution)/shard_map/ppermute | solution.py:137
  9.3 6.5 %collective-permute-start.24 = (f32[32,128]{1,0:T(8,128)S(1)}, f32[32,128]{1,0:T(8,128)S(1)}, u32[]{:S(2)}, u32[]{:S(2)}) collective-permute-start(f32[32,128]{1,0:T(8,128)S(1)} %copy-done.6), channel_id=1, source_target_pairs={{0,0},{1,16},{2,32},{3,48},{4,64},{5,80},{6,96},{7,112},{8,128},{9... | collective-permute-start | bytes 49160 | tf_op jit(solution)/shard_map/ppermute | solution.py:188
  13.1 4.5 %collective-permute-start.1 = (f32[32,192]{1,0:T(8,128)S(1)}, f32[32,192]{1,0:T(8,128)S(1)}, u32[]{:S(2)}, u32[]{:S(2)}) collective-permute-start(f32[32,192]{1,0:T(8,128)S(1)} %copy-done.5), channel_id=1, source_target_pairs={{0,16},{16,0},{32,48},{48,32},{64,80},{80,64},{96,112},{112,96},{1... | collective-permute-start | bytes 73736 | tf_op jit(solution)/shard_map/ppermute | solution.py:134
  18.8 7.4 %collective-permute-start.3 = (f32[192,384]{1,0:T(8,128)}, f32[192,384]{1,0:T(8,128)}, u32[]{:S(2)}, u32[]{:S(2)}) collective-permute-start(f32[192,384]{1,0:T(8,128)} %get-tuple-element.12), channel_id=1, source_target_pairs={{32,48},{48,32},{64,80},{80,64},{96,112},{112,96},{128,144},{144,1... | collective-permute-start | bytes 884744 | tf_op jit(solution)/shard_map/ppermute | solution.py:154
  23.5 4.1 %collective-permute-start.8 = (f32[192,384]{1,0:T(8,128)}, f32[192,384]{1,0:T(8,128)}, u32[]{:S(2)}, u32[]{:S(2)}) collective-permute-start(f32[192,384]{1,0:T(8,128)} %get-tuple-element.13), channel_id=1, source_target_pairs={{96,112},{112,96},{128,144},{144,128},{160,176},{176,160},{192,208... | collective-permute-start | bytes 884744 | tf_op jit(solution)/shard_map/ppermute | solution.py:154
  24.8 12.6 %collective-permute-start.14 = (f32[192,384]{1,0:T(8,128)S(1)}, f32[192,384]{1,0:T(8,128)S(1)}, u32[]{:S(2)}, u32[]{:S(2)}) collective-permute-start(f32[192,384]{1,0:T(8,128)S(1)} %get-tuple-element.14), channel_id=1, source_target_pairs={{160,176},{176,160},{192,208},{208,192},{224,240},{240,224},{161,1... | collective-permute-start | bytes 884744 | tf_op jit(solution)/shard_map/ppermute | solution.py:154
  25.5 13.3 %collective-permute-start.20 = (f32[192,384]{1,0:T(8,128)S(1)}, f32[192,384]{1,0:T(8,128)S(1)}, u32[]{:S(2)}, u32[]{:S(2)}) collective-permute-start(f32[192,384]{1,0:T(8,128)S(1)} %get-tuple-element.15), channel_id=1, source_target_pairs={{224,240},{240,224},{225,241},{241,225},{226,242},{242,226},{227,2... | collective-permute-start | bytes 884744 | tf_op jit(solution)/shard_map/ppermute | solution.py:154
  26.2 13.3 %collective-permute-start.4 = (f32[192,384]{1,0:T(8,128)}, f32[192,384]{1,0:T(8,128)}, u32[]{:S(2)}, u32[]{:S(2)}) collective-permute-start(f32[192,384]{1,0:T(8,128)} %collective-permute-done.3), channel_id=1, source_target_pairs={{32,33},{33,32},{34,35},{35,34},{36,37},{37,36},{38,39},{39,38},{4... | collective-permute-start | bytes 884744 | tf_op jit(solution)/shard_map/ppermute | solution.py:157
  27.6 12.6 %collective-permute-start.9 = (f32[192,384]{1,0:T(8,128)}, f32[192,384]{1,0:T(8,128)}, u32[]{:S(2)}, u32[]{:S(2)}) collective-permute-start(f32[192,384]{1,0:T(8,128)} %collective-permute-done.8), channel_id=1, source_target_pairs={{96,97},{97,96},{98,99},{99,98},{100,101},{101,100},{102,103},{103... | collective-permute-start | bytes 884744 | tf_op jit(solution)/shard_map/ppermute | solution.py:157
  29.0 14.9 %collective-permute-start.2 = (f32[64,384]{1,0:T(8,128)}, f32[64,384]{1,0:T(8,128)S(1)}, u32[]{:S(2)}, u32[]{:S(2)}) collective-permute-start(f32[64,384]{1,0:T(8,128)} %get-tuple-element.9), channel_id=1, source_target_pairs={{0,32},{16,48},{1,33},{17,49},{2,34},{18,50},{3,35},{19,51},{4,36}... | collective-permute-start | bytes 294920 | tf_op jit(solution)/shard_map/ppermute | solution.py:144
  37.5 29.6 %collective-permute-start.5 = (f32[64,384]{1,0:T(8,128)}, f32[64,384]{1,0:T(8,128)S(1)}, u32[]{:S(2)}, u32[]{:S(2)}) collective-permute-start(f32[64,384]{1,0:T(8,128)} %get-tuple-element.9), channel_id=1, source_target_pairs={{0,64},{16,80},{1,65},{17,81},{2,66},{18,82},{3,67},{19,83},{4,68}... | collective-permute-start | bytes 294920 | tf_op jit(solution)/shard_map/ppermute | solution.py:144
  38.8 20.8 %collective-permute-start.15 = (f32[192,384]{1,0:T(8,128)S(1)}, f32[192,384]{1,0:T(8,128)S(1)}, u32[]{:S(2)}, u32[]{:S(2)}) collective-permute-start(f32[192,384]{1,0:T(8,128)S(1)} %collective-permute-done.14), channel_id=1, source_target_pairs={{160,161},{161,160},{162,163},{163,162},{164,165},{165,164},{166,1... | collective-permute-start | bytes 884744 | tf_op jit(solution)/shard_map/ppermute | solution.py:157
  39.5 20.1 %collective-permute-start.21 = (f32[192,384]{1,0:T(8,128)S(1)}, f32[192,384]{1,0:T(8,128)S(1)}, u32[]{:S(2)}, u32[]{:S(2)}) collective-permute-start(f32[192,384]{1,0:T(8,128)S(1)} %collective-permute-done.20), channel_id=1, source_target_pairs={{224,225},{225,224},{226,227},{227,226},{228,229},{229,228},{230,2... | collective-permute-start | bytes 884744 | tf_op jit(solution)/shard_map/ppermute | solution.py:157
  45.4 22.4 %collective-permute-start.6 = (f32[64,384]{1,0:T(8,128)S(1)}, f32[64,384]{1,0:T(8,128)S(1)}, u32[]{:S(2)}, u32[]{:S(2)}) collective-permute-start(f32[64,384]{1,0:T(8,128)S(1)} %convolution_subtract_fusion.6), channel_id=1, source_target_pairs={{32,64},{48,80},{0,96},{16,112},{33,65},{49,81},{1,97},{17,113},{3... | collective-permute-start | bytes 294920 | tf_op jit(solution)/shard_map/ppermute | solution.py:144
  54.3 20.4 %collective-permute-start.7 = (f32[64,384]{1,0:T(8,128)S(1)}, f32[64,384]{1,0:T(8,128)S(1)}, u32[]{:S(2)}, u32[]{:S(2)}) collective-permute-start(f32[64,384]{1,0:T(8,128)S(1)} %convolution_subtract_fusion.6), channel_id=1, source_target_pairs={{32,96},{48,112},{0,128},{16,144},{33,97},{49,113},{1,129},{17,145... | collective-permute-start | bytes 294920 | tf_op jit(solution)/shard_map/ppermute | solution.py:144
  68.6 7.8 %collective-permute-start.10 = (f32[64,384]{1,0:T(8,128)S(1)}, f32[64,384]{1,0:T(8,128)S(1)}, u32[]{:S(2)}, u32[]{:S(2)}) collective-permute-start(f32[64,384]{1,0:T(8,128)S(1)} %sub.92), channel_id=1, source_target_pairs={{64,96},{80,112},{32,128},{48,144},{0,160},{16,176},{65,97},{81,11... | collective-permute-start | bytes 294920 | tf_op jit(solution)/shard_map/ppermute | solution.py:144
  73.3 10.6 %collective-permute-start.11 = (f32[64,384]{1,0:T(8,128)S(1)}, f32[64,384]{1,0:T(8,128)S(1)}, u32[]{:S(2)}, u32[]{:S(2)}) collective-permute-start(f32[64,384]{1,0:T(8,128)S(1)} %sub.92), channel_id=1, source_target_pairs={{64,128},{80,144},{32,160},{48,176},{0,192},{16,208},{65,129},{81,... | collective-permute-start | bytes 294920 | tf_op jit(solution)/shard_map/ppermute | solution.py:144
  77.1 8.3 %collective-permute-start.12 = (f32[64,384]{1,0:T(8,128)S(1)}, f32[64,384]{1,0:T(8,128)S(1)}, u32[]{:S(2)}, u32[]{:S(2)}) collective-permute-start(f32[64,384]{1,0:T(8,128)S(1)} %sub.96), channel_id=1, source_target_pairs={{96,128},{112,144},{64,160},{80,176},{32,192},{48,208},{0,224},{16... | collective-permute-start | bytes 294920 | tf_op jit(solution)/shard_map/ppermute | solution.py:144
  83.2 4.3 %collective-permute-start.13 = (f32[64,384]{1,0:T(8,128)S(1)}, f32[64,384]{1,0:T(8,128)S(1)}, u32[]{:S(2)}, u32[]{:S(2)}) collective-permute-start(f32[64,384]{1,0:T(8,128)S(1)} %sub.96), channel_id=1, source_target_pairs={{96,160},{112,176},{64,192},{80,208},{32,224},{48,240},{97,161},{1... | collective-permute-start | bytes 294920 | tf_op jit(solution)/shard_map/ppermute | solution.py:144
  86.2 2.1 %collective-permute-start.16 = (f32[64,384]{1,0:T(8,128)S(1)}, f32[64,384]{1,0:T(8,128)S(1)}, u32[]{:S(2)}, u32[]{:S(2)}) collective-permute-start(f32[64,384]{1,0:T(8,128)S(1)} %sub.99), channel_id=1, source_target_pairs={{128,160},{144,176},{96,192},{112,208},{64,224},{80,240},{129,161}... | collective-permute-start | bytes 294920 | tf_op jit(solution)/shard_map/ppermute | solution.py:144
  86.9 3.8 %collective-permute-start.17 = (f32[64,384]{1,0:T(8,128)S(1)}, f32[64,384]{1,0:T(8,128)S(1)}, u32[]{:S(2)}, u32[]{:S(2)}) collective-permute-start(f32[64,384]{1,0:T(8,128)S(1)} %sub.99), channel_id=1, source_target_pairs={{128,192},{144,208},{96,224},{112,240},{129,193},{145,209},{97,225... | collective-permute-start | bytes 294920 | tf_op jit(solution)/shard_map/ppermute | solution.py:144
  89.1 2.3 %collective-permute-start.18 = (f32[64,384]{1,0:T(8,128)S(1)}, f32[64,384]{1,0:T(8,128)S(1)}, u32[]{:S(2)}, u32[]{:S(2)}) collective-permute-start(f32[64,384]{1,0:T(8,128)S(1)} %sub.102), channel_id=1, source_target_pairs={{160,192},{176,208},{128,224},{144,240},{161,193},{177,209},{129,2... | collective-permute-start | bytes 294920 | tf_op jit(solution)/shard_map/ppermute | solution.py:144
  89.8 3.1 %collective-permute-start.19 = (f32[64,384]{1,0:T(8,128)S(1)}, f32[64,384]{1,0:T(8,128)S(1)}, u32[]{:S(2)}, u32[]{:S(2)}) collective-permute-start(f32[64,384]{1,0:T(8,128)S(1)} %sub.102), channel_id=1, source_target_pairs={{160,224},{176,240},{161,225},{177,241},{162,226},{178,242},{163,2... | collective-permute-start | bytes 294920 | tf_op jit(solution)/shard_map/ppermute | solution.py:144
  92.2 1.4 collective-permute-start.22
  94.4 4.7 %collective-permute-start.23 = (f32[64,384]{1,0:T(8,128)S(1)}, f32[64,384]{1,0:T(8,128)S(1)}, u32[]{:S(2)}, u32[]{:S(2)}) collective-permute-start(f32[64,384]{1,0:T(8,128)S(1)} %sub.106), channel_id=1, source_target_pairs={{0,16},{16,0},{32,48},{48,32},{64,80},{80,64},{96,112},{112,96},{1... | collective-permute-start | bytes 294920 | tf_op jit(solution)/shard_map/ppermute | solution.py:181
  99.2 9.9 %collective-permute-start.25 = (f32[192,128]{0,1:T(8,128)S(1)}, f32[192,128]{0,1:T(8,128)S(1)}, u32[]{:S(2)}, u32[]{:S(2)}) collective-permute-start(f32[192,128]{0,1:T(8,128)S(1)} %get-tuple-element.66), channel_id=1, source_target_pairs={{0,0},{4,1},{8,2},{12,3},{16,4},{20,5},{24,6},{28,7},{32,8},{36,9}... | collective-permute-start | bytes 294920 | tf_op jit(solution)/shard_map/ppermute | solution.py:197
  110.5 28.5 %all-to-all-start = ((f32[16,192,128]{2,1,0:T(8,128)}), f32[16,192,128]{2,1,0:T(8,128)S(1)}, u32[]{:S(2)}, u32[]{:S(2)}) async-start(f32[16,192,128]{2,1,0:T(8,128)} %broadcast_in_dim.5), calls=%async_computation | async-start | bytes 3145728 | tf_op jit(solution)/shard_map/all_to_all | solution.py:203
  115.2 23.9 %collective-permute-start.26 = (f32[192,128]{0,1:T(8,128)S(1)}, f32[192,128]{0,1:T(8,128)S(1)}, u32[]{:S(2)}, u32[]{:S(2)}) collective-permute-start(f32[192,128]{0,1:T(8,128)S(1)} %get-tuple-element.66), channel_id=1, source_target_pairs={{0,16},{16,0},{32,48},{48,32},{64,80},{80,64},{96,112},{112,96},{1... | collective-permute-start | bytes 294920 | tf_op jit(solution)/shard_map/ppermute | solution.py:201
  115.4 23.6 %collective-permute-start.27 = (f32[192,128]{0,1:T(8,128)S(1)}, f32[192,128]{0,1:T(8,128)S(1)}, u32[]{:S(2)}, u32[]{:S(2)}) collective-permute-start(f32[192,128]{0,1:T(8,128)S(1)} %get-tuple-element.66), channel_id=1, source_target_pairs={{0,32},{16,48},{32,0},{48,16},{64,96},{80,112},{96,64},{112,80},{1... | collective-permute-start | bytes 294920 | tf_op jit(solution)/shard_map/ppermute | solution.py:201
  116.8 22.3 %collective-permute-start.28 = (f32[192,128]{0,1:T(8,128)S(1)}, f32[192,128]{0,1:T(8,128)S(1)}, u32[]{:S(2)}, u32[]{:S(2)}) collective-permute-start(f32[192,128]{0,1:T(8,128)S(1)} %get-tuple-element.66), channel_id=1, source_target_pairs={{0,48},{16,32},{32,16},{48,0},{64,112},{80,96},{96,80},{112,64},{1... | collective-permute-start | bytes 294920 | tf_op jit(solution)/shard_map/ppermute | solution.py:201
  139.1 28.2 %copy-start.4 = (f32[32,128]{1,0:T(8,128)S(1)}, f32[32,128]{1,0:T(8,128)}, u32[]{:S(2)}) copy-start(f32[32,128]{1,0:T(8,128)} %get-tuple-element.71) | copy-start | bytes 49156
  143.3 35.8 %all-to-all-start.1 = ((f32[4,128,128]{2,1,0:T(8,128)}), f32[4,128,128]{2,1,0:T(8,128)S(1)}, u32[]{:S(2)}, u32[]{:S(2)}) async-start(f32[4,128,128]{2,1,0:T(8,128)} %convolution_bitcast_fusion), calls=%async_computation.1 | async-start | bytes 524288 | tf_op jit(solution)/shard_map/all_to_all | solution.py:208
  (7 other events, 50.2 us)

commit v5 on v4

--- a/solution.py
+++ b/solution.py
@@ -5,9 +5,8 @@
 from jax.experimental.pallas import tpu as pltpu
 from jax.sharding import PartitionSpec as P
 
-HIGH = lax.Precision.HIGHEST
+FULL = lax.Precision.HIGHEST
 BASE = 32
-QUAD = 4
 
 
 def matern(first_set, second_set):
@@ -17,7 +16,17 @@
 
 
 def mm(a, b):
-    return jnp.dot(a, b, precision=HIGH, preferred_element_type=jnp.float32)
+    return jnp.dot(a, b, precision=FULL, preferred_element_type=jnp.float32)
+
+
+def quick(a, b, contract=0):
+    return lax.dot_general(
+        a,
+        b,
+        (((1,), (contract,)), ((), ())),
+        precision=lax.Precision.HIGH,
+        preferred_element_type=jnp.float32,
+    )
 
 
 def invert_into(l_ref, d_ref):
@@ -52,7 +61,7 @@
 
 def across_rows(a, b):
     return lax.dot_general(
-        a, b, (((1,), (1,)), ((), ())), precision=HIGH, preferred_element_type=jnp.float32
+        a, b, (((1,), (1,)), ((), ())), precision=FULL, preferred_element_type=jnp.float32
     )
 
 
@@ -104,15 +113,25 @@
     )(side, own, other, cross)
 
 
+def both_of(place, own, other, axis=1):
+    return jnp.where(
+        place == 0,
+        jnp.concatenate([own, other], axis=axis),
+        jnp.concatenate([other, own], axis=axis),
+    )
+
+
+def unset(value):
+    corner = value[0, 0]
+    return (corner != corner).astype(jnp.int32)
+
+
 def shards(archive_inputs, candidate_inputs, lengthscales, factor):
     height = factor.shape[0]
     width = candidate_inputs.shape[1]
     chain = lax.axis_size("chain")
     cand = lax.axis_size("cand")
-    quads = chain // QUAD
     position = lax.axis_index("chain")
-    inside = [[QUAD * g + i for i in range(QUAD)] for g in range(quads)]
-    across = [[QUAD * g + i for g in range(quads)] for i in range(QUAD)]
     layers = chain // 2
     layer, side = position // 2, position % 2
     odd = layer % 2
@@ -122,11 +141,7 @@
     scaled_candidates = candidate_inputs * scaling[:, None]
 
     def both(own, other, axis):
-        return jnp.where(
-            side == 0,
-            jnp.concatenate([own, other], axis=axis),
-            jnp.concatenate([other, own], axis=axis),
-        )
+        return both_of(side, own, other, axis)
 
     def after(value, *events):
         return lax.optimization_barrier((value, *events))[0]
@@ -145,68 +160,73 @@
 
     span = 2 * height
     core = lax.axis_index("cand") % 2
-    chunks = [factor[:, k * span : (k + 1) * span] for k in range(layers)]
-    lefts, rights = [], []
-    for s in range(layers // 2):
+    late = after(factor, own_part)
+    chunks = [late[:, k * span : (k + 1) * span] for k in range(layers)]
+
+    def send(s):
         left = jnp.where(odd == 1, chunks[max(2 * s - 1, 0)], chunks[2 * s])
         right = jnp.where(odd == 1, chunks[2 * s], chunks[2 * s + 1])
-        sent = after(jnp.where(core == 0, left, right), other_part if s == 0 else solved)
+        sent = jnp.where(core == 0, left, right)
+        sent = after(sent, solved) if s else sent
         got = lax.ppermute(sent, "chain", [(p, p ^ 1) for p in range(chain) if p // 2 >= 2 * s + 1])
+        return left, right, got
+
+    def settle(s, left, right, got):
         users = [p for p in range(chain) if p // 2 >= 2 * s + 1]
         twins = [(p * cand + c, p * cand + (c ^ 1)) for p in users for c in range(cand)]
         twin = lax.ppermute(got, ("chain", "cand"), twins)
-        yours_left = jnp.where(core == 0, got, twin)
-        yours_right = jnp.where(core == 0, twin, got)
-        mine = jnp.concatenate([left, right], axis=1)
-        yours = jnp.concatenate([yours_left, yours_right], axis=1)
-        slab = mm(for_mine, mine) + mm(for_yours, yours)
-        lefts.append(after(slab[:, :span]))
-        rights.append(after(slab[:, span:]))
-
-    far = None
+        yours = jnp.concatenate(
+            [jnp.where(core == 0, got, twin), jnp.where(core == 0, twin, got)], axis=1
+        )
+        slab = quick(for_mine, jnp.concatenate([left, right], axis=1)) + quick(for_yours, yours)
+        return after(slab[:, :span]), after(slab[:, span:])
+
+    parts = [send(s) for s in range(layers // 2)]
+    slabs = [settle(0, *parts[0][:2], after(parts[0][2], solved))]
+
     for t in range(layers - 1):
         near = hop(solved, [(t - k, t + 1 + k) for k in range(layers) if t - k >= 0 and t + 1 + k < layers])
-        pairs = [(t - k, t + 2 + k) for k in range(layers) if t - k >= 0 and t + 2 + k < layers]
-        ahead = hop(solved, pairs) if pairs else None
         users = sorted({t - z // 2 for z in range(t + 1, min(2 * t + 1, layers - 1) + 1)})
-        left, right = lefts[users[0]], rights[users[0]]
+        left, right = slabs[users[0]]
         if len(users) > 1:
             second = t - layer // 2 == users[1]
-            left = after(jnp.where(second, lefts[users[1]], left))
-            right = after(jnp.where(second, rights[users[1]], right))
-        if far is not None:
-            solved = after(solved - across_rows(far, left))
-        solved = solved - across_rows(near, right)
-        far = ahead
-    other = lax.ppermute(solved, "chain", pair_all)
-    rows = jnp.where(
-        side == 0,
-        jnp.concatenate([solved[:, :height], other[:, :height]], axis=0),
-        jnp.concatenate([other[:, height:], solved[:, height:]], axis=0),
-    ).T
+            left = after(jnp.where(second, slabs[users[1]][0], left))
+            right = after(jnp.where(second, slabs[users[1]][1], right))
+        if t:
+            pairs = [(t - 1 - k, t + 1 + k) for k in range(layers) if t - 1 - k >= 0 and t + 1 + k < layers]
+            solved = after(solved - quick(hop(solved, pairs), left, 1))
+        solved = solved - quick(near, right, 1)
+        if t in (0, 2, 4):
+            s = t // 2 + 1
+            slabs.append(settle(s, *parts[s][:2], after(parts[s][2], solved)))
+        if t == 3:
+            wanted = jnp.where(unset(solved) == 0, candidate_inputs, 0.0)
+    turn = [
+        ((2 * z + h) * cand + 4 * j + 2 * k + y, (2 * z + y) * cand + 4 * j + 2 * h + k)
+        for z in range(layers)
+        for j in range(cand // 4)
+        for h in range(2)
+        for k in range(2)
+        for y in range(2)
+    ]
+    turned = lax.ppermute(solved, ("chain", "cand"), turn)
+    columns_all = both(solved, lax.ppermute(solved, "chain", pair_all), 0)
+    rows = jnp.where(side == 0, columns_all[:, :height], columns_all[:, height:]).T
+    twin_columns = lax.ppermute(columns_all, "cand", [(c, c ^ 1) for c in range(cand)])
+    same_core = [[2 * i + k for i in range(cand // 2)] for k in range(2)]
+    copies = jnp.broadcast_to(turned[None], (cand // 2,) + turned.shape)
+    others = lax.all_to_all(copies, "cand", 0, 0, axis_index_groups=same_core, tiled=True)
     swap = [(a * cand + b, b * cand + a) for a in range(chain) for b in range(cand)]
-    chosen = lax.ppermute(candidate_inputs, ("chain", "cand"), swap)
-
-    turn = [
-        ((QUAD * g + (i ^ j)) * cand + QUAD * m + i, (QUAD * g + i) * cand + QUAD * j + m)
-        for g in range(quads)
-        for i in range(QUAD)
-        for j in range(QUAD)
-        for m in range(cand // QUAD)
-    ]
-    turned = lax.ppermute(rows, ("chain", "cand"), turn)
-    mine = [rows]
-    for r in range(1, QUAD):
-        pairs = [(QUAD * g + i, QUAD * g + (i ^ r)) for g in range(quads) for i in range(QUAD)]
-        mine.append(lax.ppermute(rows, "chain", pairs))
-    copies = jnp.broadcast_to(turned[None], (cand,) + turned.shape)
-    others = lax.all_to_all(copies, "cand", 0, 0, tiled=True)
-    others = others.reshape(QUAD, cand // QUAD, height, width)
-    shares = jnp.einsum(
-        "jmra,jrb->mab", others, jnp.stack(mine), precision=HIGH, preferred_element_type=jnp.float32
-    )
-    shared = lax.all_to_all(shares, "chain", 0, 0, axis_index_groups=across, tiled=True).sum(axis=0)
-    prior_cov = matern(chosen * scaling[:, None], scaled_candidates)
+    chosen = lax.ppermute(wanted, ("chain", "cand"), swap)
+    prior_cov = matern(chosen * after(scaling, solved)[:, None], scaled_candidates)
+    others = others.reshape(cand // 2 * half, span)
+    theirs = lax.ppermute(quick(others, twin_columns, 1), "cand", [(c, c ^ 1) for c in range(cand)])
+    ours = quick(others, columns_all, 1)
+    ours = ours.reshape(layers // 2, 1, width, width)
+    theirs = theirs.reshape(layers // 2, 1, width, width)
+    shares = both_of(core + unset(prior_cov), ours, theirs).reshape(layers, width, width)
+    same_side = [[2 * z + y for z in range(layers)] for y in range(2)]
+    shared = lax.all_to_all(shares, "chain", 0, 0, axis_index_groups=same_side, tiled=True).sum(axis=0)
     return (rows, prior_cov - shared)
 
 

time: 181 us -> 157 us (0.87)
  waiting for transfers between devices: 45.7 us -> 29.1 us
  matrix products: 22.9 us -> 13.5 us
  starting transfers between devices: 91.1 us -> 85.5 us
  local copies, waits for them, and re-layouts: 3.53 us -> 7.71 us
  between operations: 1.35 us -> 3.97 us
    ppermute x14 -> x13, waiting for transfers between devices: 32.5 us -> 4.71 us  [the longest x1 3.12 us: shards(): turned = lax.ppermute(solved, ('chain', 'cand'), turn)]
    ppermute x13, starting transfers between devices: 40.3 us -> 28.9 us  [hop(): lax.ppermute(value, 'chain', [(2 * a + i, 2 * b + i) for a, b in pairs fo...]
    dot_general x22 -> x23, matrix products: 22.9 us -> 13.5 us  [quick(): lax.dot_general(a, b, (((1,), (contract,)), ((), ())), precision=lax.Prec...]
    all_to_all x2, starting transfers between devices: 28.6 us -> 36.1 us  [the longest x1 29.1 us: shards(): lax.all_to_all(shares, 'chain', 0, 0, axis_index_groups=same_side, tiled=...]
    all_to_all x2, waiting for transfers between devices: 10.4 us -> 17.4 us  [the longest x1 17.4 us: shards(): lax.all_to_all(shares, 'chain', 0, 0, axis_index_groups=same_side, tiled=...]
    ppermute x1, waiting for transfers between devices: 0.01 us -> 3.33 us  [shards(): other_part = lax.ppermute(own_part, 'chain', pair_all)]
    ppermute x13, waiting for transfers between devices: 1.78 us -> 3.71 us  [hop(): lax.ppermute(value, 'chain', [(2 * a + i, 2 * b + i) for a, b in pairs fo...]
    ppermute x14 -> x13, starting transfers between devices: 19.9 us -> 18.3 us  [the longest x1 9.41 us: shards(): chosen = lax.ppermute(wanted, ('chain', 'cand'), swap)]
  transfers between devices with their start and end apart: 31 -> 30, of which waited for: 8 -> 8; matrix products, arithmetic and copies ran while one was open for 13% -> 16% of each run, Pallas kernels for 2% -> 5%
where the time goes in v5:
time: 157 us; the launch traced here: 155 us
  starting transfers between devices  85.5 us (54%)
  waiting for transfers between devices  29.1 us (19%)
  matrix products  13.5 us (9%)
  other arithmetic  8.06 us (5%)
  local copies, waits for them, and re-layouts  7.71 us (5%)
  Pallas kernels  7.42 us (5%)
  between operations  3.97 us (3%)
    all_to_all x1, starting transfers between devices, shards(): lax.all_to_all(shares, 'chain', 0, 0, axis_index_groups=same_side, tiled=...  29.1 us
    ppermute x13, starting transfers between devices, hop(): lax.ppermute(value, 'chain', [(2 * a + i, 2 * b + i) for a, b in pairs fo...  28.9 us
    all_to_all x1, waiting for transfers between devices, shards(): lax.all_to_all(shares, 'chain', 0, 0, axis_index_groups=same_side, tiled=...  17.4 us
    dot_general x23, matrix products, quick(): lax.dot_general(a, b, (((1,), (contract,)), ((), ())), precision=lax.Prec...  13.5 us
    ppermute x1, starting transfers between devices, shards(): chosen = lax.ppermute(wanted, ('chain', 'cand'), swap)  9.41 us
    all_to_all x1, starting transfers between devices, shards(): lax.all_to_all(copies, 'cand', 0, 0, axis_index_groups=same_core, tiled=T...  7.04 us
    pallas_call x1, Pallas kernels, own_inverse(): pl.pallas_call(own_kernel, in_specs=[pl.BlockSpec(memory_space=pltpu.SMEM...  4.18 us
    ppermute x13, waiting for transfers between devices, hop(): lax.ppermute(value, 'chain', [(2 * a + i, 2 * b + i) for a, b in pairs fo...  3.71 us
  transfers between devices with their start and end apart: 30, of which 8 were waited for; matrix products, arithmetic and copies ran while one was open for 16% of the time, Pallas kernels for 5%

profile of v5, /device:TPU:2, one launch (start us, length us, event | category | flops | bytes accessed | tf_op | source)
XLA Modules:
  0.0 155.3 jit_solution(11683097661942670873)
XLA Ops:
  0.6 1.7 %collective-permute-start.1 = (f32[32,192]{1,0:T(8,128)}, f32[32,192]{1,0:T(8,128)S(1)}, u32[]{:S(2)}, u32[]{:S(2)}) collective-permute-start(f32[32,192]{1,0:T(8,128)} %param.4), channel_id=1, source_target_pairs={{0,16},{16,0},{32,48},{48,32},{64,80},{80,64},{96,112},{112,96},{1... | collective-permute-start | bytes 73736 | tf_op jit(solution)/shard_map/ppermute | solution.py:149
  2.3 1.7 %constant_dynamic-slice_fusion.1.own_ref = f32[192,384]{1,0:T(8,128)} fusion(f32[192,3072]{1,0:T(8,128)} %param.7, s32[]{:T(128)S(6)} %select_n.198), kind=kLoop, calls=%fused_computation.80 | loop fusion | bytes 589828 | tf_op jit(solution)/shard_map/dynamic_slice | solution.py:150
  4.0 4.2 %shard_map.59.own_ref = f32[192,384]{1,0:T(8,128)} custom-call(s32[1]{0:T(128)} %bitcast.side_ref, f32[192,384]{1,0:T(8,128)} %constant_dynamic-slice_fusion.1.own_ref), custom_call_target="tpu_custom_call" | custom-call | tf_op jit(solution)/shard_map/pallas_call | solution.py:81
  8.6 2.8 %broadcast_select_fusion.8 = (f32[192,384]{1,0:T(8,128)}, f32[192,384]{1,0:T(8,128)S(1)}, f32[192,384]{1,0:T(8,128)}, f32[192,384]{1,0:T(8,128)S(1)}, f32[192,38...) fusion(pred[]{:T(512)S(6)} %eq.25, ...), kind=kLoop, calls=%fused_computation.60 | loop fusion | flops 811008 | bytes 5898242 | tf_op jit(solution)/shard_map/jit(_where)/select_n | solution.py:169
  13.5 3.3 %collective-permute-done.other_ref = f32[192,384]{1,0:T(8,128)S(1)} collective-permute-done((f32[192,384]{1,0:T(8,128)}, f32[192,384]{1,0:T(8,128)S(1)}, u32[]{:S(2)}, u32[]{:S(2)}) %collective-permute-start) | collective-permute-done | bytes 294944 | tf_op jit(solution)/shard_map/ppermute | solution.py:152
  16.8 0.7 copy-done.6
  17.6 3.2 %shard_map.60 = (f32[384,192]{1,0:T(8,128)}, f32[384,192]{1,0:T(8,128)}, f32[64,384]{1,0:T(8,128)}) custom-call(s32[1]{0:T(128)} %bitcast.side_ref, f32[192,384]{1,0:T(8,128)} %shard_map.59.own_ref, f32[192,384]{1,0:T(8,128)} %copy-done.6, f32[64,384]{1,0:T(8,128)} %exponential_multiply_fusion.cross_ref), custom_call_target="tpu_custom_call" | custom-call | tf_op jit(solution)/shard_map/pallas_call | solution.py:108
  20.8 0.8 collective-permute-start.4
  21.6 7.3 %collective-permute-start.2 = (f32[64,384]{1,0:T(8,128)}, f32[64,384]{1,0:T(8,128)S(1)}, u32[]{:S(2)}, u32[]{:S(2)}) collective-permute-start(f32[64,384]{1,0:T(8,128)} %get-tuple-element.14), channel_id=1, source_target_pairs={{0,32},{16,48},{1,33},{17,49},{2,34},{18,50},{3,35},{19,51},{4,36}... | collective-permute-start | bytes 294920 | tf_op jit(solution)/shard_map/ppermute | solution.py:159
  32.6 2.8 %collective-permute-start.5 = (f32[64,384]{1,0:T(8,128)S(1)}, f32[64,384]{1,0:T(8,128)}, u32[]{:S(2)}, u32[]{:S(2)}) collective-permute-start(f32[64,384]{1,0:T(8,128)S(1)} %convolution_subtract_fusion.6), channel_id=1, source_target_pairs={{0,64},{16,80},{1,65},{17,81},{2,66},{18,82},{3,67},{19,83},{4,68}... | collective-permute-start | bytes 294920 | tf_op jit(solution)/shard_map/ppermute | solution.py:159
  35.4 1.4 collective-permute-start.14
  36.8 3.5 %collective-permute-start.6 = (f32[64,384]{1,0:T(8,128)S(1)}, f32[64,384]{1,0:T(8,128)S(1)}, u32[]{:S(2)}, u32[]{:S(2)}) collective-permute-start(f32[64,384]{1,0:T(8,128)S(1)} %convolution_subtract_fusion.6), channel_id=1, source_target_pairs={{32,64},{48,80},{0,96},{16,112},{33,65},{49,81},{1,97},{17,113},{3... | collective-permute-start | bytes 294920 | tf_op jit(solution)/shard_map/ppermute | solution.py:159
  41.1 1.3 convolution_subtract_fusion.5
  43.2 6.2 %collective-permute-start.10 = (f32[64,384]{1,0:T(8,128)S(1)}, f32[64,384]{1,0:T(8,128)S(1)}, u32[]{:S(2)}, u32[]{:S(2)}) collective-permute-start(f32[64,384]{1,0:T(8,128)S(1)} %sub.92), channel_id=1, source_target_pairs={{64,96},{80,112},{32,128},{48,144},{0,160},{16,176},{65,97},{81,11... | collective-permute-start | bytes 294920 | tf_op jit(solution)/shard_map/ppermute | solution.py:159
  49.4 1.7 %collective-permute-start.7 = (f32[64,384]{1,0:T(8,128)S(1)}, f32[64,384]{1,0:T(8,128)S(1)}, u32[]{:S(2)}, u32[]{:S(2)}) collective-permute-start(f32[64,384]{1,0:T(8,128)S(1)} %sub.92), channel_id=1, source_target_pairs={{32,96},{48,112},{0,128},{16,144},{33,97},{49,113},{1,129},{17,145... | collective-permute-start | bytes 294920 | tf_op jit(solution)/shard_map/ppermute | solution.py:159
  52.6 0.9 broadcast_select_fusion.3
  54.8 1.9 %collective-permute-start.11 = (f32[64,384]{1,0:T(8,128)S(1)}, f32[64,384]{1,0:T(8,128)}, u32[]{:S(2)}, u32[]{:S(2)}) collective-permute-start(f32[64,384]{1,0:T(8,128)S(1)} %sub.96), channel_id=1, source_target_pairs={{64,128},{80,144},{32,160},{48,176},{0,192},{16,208},{65,129},{81,... | collective-permute-start | bytes 294920 | tf_op jit(solution)/shard_map/ppermute | solution.py:159
  57.4 1.3 collective-permute-start.12
  59.4 1.3 convolution_subtract_fusion.3
  60.8 2.5 %collective-permute-done.12 = f32[64,384]{1,0:T(8,128)S(1)} collective-permute-done((f32[64,384]{1,0:T(8,128)S(1)}, f32[64,384]{1,0:T(8,128)S(1)}, u32[]{:S(2)}, u32[]{:S(2)}) %collective-permute-start.12) | collective-permute-done | bytes 98336 | tf_op jit(solution)/shard_map/ppermute | solution.py:159
  64.4 0.8 collective-permute-start.13
  65.3 1.0 broadcast_select_fusion.10
  76.1 1.9 %collective-permute-start.25 = (f32[64,384]{1,0:T(8,128)S(1)}, f32[64,384]{1,0:T(8,128)S(1)}, u32[]{:S(2)}, u32[]{:S(2)}) collective-permute-start(f32[64,384]{1,0:T(8,128)S(1)} %sub.106), channel_id=1, source_target_pairs={{0,0},{1,16},{2,1},{3,17},{16,2},{17,18},{18,3},{19,19},{4,4},{5,2... | collective-permute-start | bytes 294920 | tf_op jit(solution)/shard_map/ppermute | solution.py:212
  80.4 3.1 %collective-permute-done.25 = f32[64,384]{1,0:T(8,128)S(1)} collective-permute-done((f32[64,384]{1,0:T(8,128)S(1)}, f32[64,384]{1,0:T(8,128)S(1)}, u32[]{:S(2)}, u32[]{:S(2)}) %collective-permute-start.25) | collective-permute-done | bytes 98336 | tf_op jit(solution)/shard_map/ppermute | solution.py:212
  83.5 1.0 broadcast_in_dim.10
  84.4 7.0 %all-to-all-start = ((f32[8,64,384]{2,1,0:T(8,128)}), f32[8,64,384]{2,1,0:T(8,128)S(1)}, u32[]{:S(2)}, u32[]{:S(2)}) async-start(f32[8,64,384]{2,1,0:T(8,128)} %broadcast_in_dim.10), calls=%async_computation | async-start | bytes 1572864 | tf_op jit(solution)/shard_map/all_to_all | solution.py:218
  91.5 9.4 %collective-permute-start.24 = (f32[32,128]{1,0:T(8,128)S(1)}, f32[32,128]{1,0:T(8,128)S(1)}, u32[]{:S(2)}, u32[]{:S(2)}) collective-permute-start(f32[32,128]{1,0:T(8,128)S(1)} %broadcast_select_fusion.18), channel_id=1, source_target_pairs={{0,0},{1,16},{2,32},{3,48},{4,64},{5,80},{6,96},{7,112},{8,128},{9... | collective-permute-start | bytes 49160 | tf_op jit(solution)/shard_map/ppermute | solution.py:220
  101.0 1.6 %collective-permute-done.24 = f32[32,128]{1,0:T(8,128)S(1)} collective-permute-done((f32[32,128]{1,0:T(8,128)S(1)}, f32[32,128]{1,0:T(8,128)S(1)}, u32[]{:S(2)}, u32[]{:S(2)}) %collective-permute-start.24) | collective-permute-done | bytes 16416 | tf_op jit(solution)/shard_map/ppermute | solution.py:220
  106.4 0.8 copy.9
  107.3 29.1 %all-to-all-start.1 = ((f32[8,128,128]{2,1,0:T(8,128)}), f32[8,128,128]{2,1,0:T(8,128)S(1)}, u32[]{:S(2)}, u32[]{:S(2)}) async-start(f32[8,128,128]{2,1,0:T(8,128)} %bitcast.9), calls=%async_computation.1 | async-start | bytes 1048576 | tf_op jit(solution)/shard_map/all_to_all | solution.py:229
  136.5 0.7 copy.10
  137.2 17.4 %all-to-all-done.1 = f32[8,128,128]{2,1,0:T(8,128)S(1)} async-done(((f32[8,128,128]{2,1,0:T(8,128)}), f32[8,128,128]{2,1,0:T(8,128)S(1)}, u32[]{:S(2)}, u32[]{:S(2)}) %all-to-all-start.1) | async-done | bytes 524320 | tf_op jit(solution)/shard_map/all_to_all | solution.py:229
  (121 shorter events, 26.8 us)
Async XLA Ops:
  0.6 11.7 %collective-permute-start.1 = (f32[32,192]{1,0:T(8,128)}, f32[32,192]{1,0:T(8,128)S(1)}, u32[]{:S(2)}, u32[]{:S(2)}) collective-permute-start(f32[32,192]{1,0:T(8,128)} %param.4), channel_id=1, source_target_pairs={{0,16},{16,0},{32,48},{48,32},{64,80},{80,64},{96,112},{112,96},{1... | collective-permute-start | bytes 73736 | tf_op jit(solution)/shard_map/ppermute | solution.py:149
  8.2 8.7 %collective-permute-start = (f32[192,384]{1,0:T(8,128)}, f32[192,384]{1,0:T(8,128)S(1)}, u32[]{:S(2)}, u32[]{:S(2)}) collective-permute-start(f32[192,384]{1,0:T(8,128)} %shard_map.59.own_ref), channel_id=1, source_target_pairs={{0,16},{16,0},{32,48},{48,32},{64,80},{80,64},{96,112},{112,96},{1... | collective-permute-start | bytes 884744 | tf_op jit(solution)/shard_map/ppermute | solution.py:152
  11.4 9.4 %collective-permute-start.3 = (f32[192,384]{1,0:T(8,128)S(1)}, f32[192,384]{1,0:T(8,128)S(1)}, u32[]{:S(2)}, u32[]{:S(2)}) collective-permute-start(f32[192,384]{1,0:T(8,128)S(1)} %get-tuple-element.50), channel_id=1, source_target_pairs={{32,48},{48,32},{64,80},{80,64},{96,112},{112,96},{128,144},{144,1... | collective-permute-start | bytes 884744 | tf_op jit(solution)/shard_map/ppermute | solution.py:171
  12.1 17.5 %copy-start.11 = (f32[32]{0:T(128)}, f32[32]{0:T(128)S(1)}, u32[]{:S(2)}) copy-start(f32[32]{0:T(128)S(1)} %broadcast_divide_fusion) | copy-start | bytes 388
  20.8 8.8 %collective-permute-start.4 = (f32[192,384]{1,0:T(8,128)S(1)}, f32[192,384]{1,0:T(8,128)S(1)}, u32[]{:S(2)}, u32[]{:S(2)}) collective-permute-start(f32[192,384]{1,0:T(8,128)S(1)} %collective-permute-done.3), channel_id=1, source_target_pairs={{32,33},{33,32},{34,35},{35,34},{36,37},{37,36},{38,39},{39,38},{4... | collective-permute-start | bytes 884744 | tf_op jit(solution)/shard_map/ppermute | solution.py:177
  21.6 10.3 %collective-permute-start.2 = (f32[64,384]{1,0:T(8,128)}, f32[64,384]{1,0:T(8,128)S(1)}, u32[]{:S(2)}, u32[]{:S(2)}) collective-permute-start(f32[64,384]{1,0:T(8,128)} %get-tuple-element.14), channel_id=1, source_target_pairs={{0,32},{16,48},{1,33},{17,49},{2,34},{18,50},{3,35},{19,51},{4,36}... | collective-permute-start | bytes 294920 | tf_op jit(solution)/shard_map/ppermute | solution.py:159
  28.9 11.5 %collective-permute-start.8 = (f32[192,384]{1,0:T(8,128)S(1)}, f32[192,384]{1,0:T(8,128)S(1)}, u32[]{:S(2)}, u32[]{:S(2)}) collective-permute-start(f32[192,384]{1,0:T(8,128)S(1)} %get-tuple-element.19), channel_id=1, source_target_pairs={{96,112},{112,96},{128,144},{144,128},{160,176},{176,160},{192,208... | collective-permute-start | bytes 884744 | tf_op jit(solution)/shard_map/ppermute | solution.py:171
  32.6 8.4 %collective-permute-start.5 = (f32[64,384]{1,0:T(8,128)S(1)}, f32[64,384]{1,0:T(8,128)}, u32[]{:S(2)}, u32[]{:S(2)}) collective-permute-start(f32[64,384]{1,0:T(8,128)S(1)} %convolution_subtract_fusion.6), channel_id=1, source_target_pairs={{0,64},{16,80},{1,65},{17,81},{2,66},{18,82},{3,67},{19,83},{4,68}... | collective-permute-start | bytes 294920 | tf_op jit(solution)/shard_map/ppermute | solution.py:159
  35.4 23.3 %collective-permute-start.14 = (f32[192,384]{1,0:T(8,128)}, f32[192,384]{1,0:T(8,128)}, u32[]{:S(2)}, u32[]{:S(2)}) collective-permute-start(f32[192,384]{1,0:T(8,128)} %get-tuple-element.21), channel_id=1, source_target_pairs={{160,176},{176,160},{192,208},{208,192},{224,240},{240,224},{161,1... | collective-permute-start | bytes 884744 | tf_op jit(solution)/shard_map/ppermute | solution.py:171
  36.8 5.9 %collective-permute-start.6 = (f32[64,384]{1,0:T(8,128)S(1)}, f32[64,384]{1,0:T(8,128)S(1)}, u32[]{:S(2)}, u32[]{:S(2)}) collective-permute-start(f32[64,384]{1,0:T(8,128)S(1)} %convolution_subtract_fusion.6), channel_id=1, source_target_pairs={{32,64},{48,80},{0,96},{16,112},{33,65},{49,81},{1,97},{17,113},{3... | collective-permute-start | bytes 294920 | tf_op jit(solution)/shard_map/ppermute | solution.py:159
  40.4 10.8 %collective-permute-start.9 = (f32[192,384]{1,0:T(8,128)S(1)}, f32[192,384]{1,0:T(8,128)S(1)}, u32[]{:S(2)}, u32[]{:S(2)}) collective-permute-start(f32[192,384]{1,0:T(8,128)S(1)} %collective-permute-done.8), channel_id=1, source_target_pairs={{96,97},{97,96},{98,99},{99,98},{100,101},{101,100},{102,103},{103... | collective-permute-start | bytes 884744 | tf_op jit(solution)/shard_map/ppermute | solution.py:177
  43.2 11.1 %collective-permute-start.10 = (f32[64,384]{1,0:T(8,128)S(1)}, f32[64,384]{1,0:T(8,128)S(1)}, u32[]{:S(2)}, u32[]{:S(2)}) collective-permute-start(f32[64,384]{1,0:T(8,128)S(1)} %sub.92), channel_id=1, source_target_pairs={{64,96},{80,112},{32,128},{48,144},{0,160},{16,176},{65,97},{81,11... | collective-permute-start | bytes 294920 | tf_op jit(solution)/shard_map/ppermute | solution.py:159
  49.4 4.5 %collective-permute-start.7 = (f32[64,384]{1,0:T(8,128)S(1)}, f32[64,384]{1,0:T(8,128)S(1)}, u32[]{:S(2)}, u32[]{:S(2)}) collective-permute-start(f32[64,384]{1,0:T(8,128)S(1)} %sub.92), channel_id=1, source_target_pairs={{32,96},{48,112},{0,128},{16,144},{33,97},{49,113},{1,129},{17,145... | collective-permute-start | bytes 294920 | tf_op jit(solution)/shard_map/ppermute | solution.py:159
  54.8 4.6 %collective-permute-start.11 = (f32[64,384]{1,0:T(8,128)S(1)}, f32[64,384]{1,0:T(8,128)}, u32[]{:S(2)}, u32[]{:S(2)}) collective-permute-start(f32[64,384]{1,0:T(8,128)S(1)} %sub.96), channel_id=1, source_target_pairs={{64,128},{80,144},{32,160},{48,176},{0,192},{16,208},{65,129},{81,... | collective-permute-start | bytes 294920 | tf_op jit(solution)/shard_map/ppermute | solution.py:159
  56.7 13.7 %collective-permute-start.20 = (f32[192,384]{1,0:T(8,128)}, f32[192,384]{1,0:T(8,128)S(1)}, u32[]{:S(2)}, u32[]{:S(2)}) collective-permute-start(f32[192,384]{1,0:T(8,128)} %get-tuple-element.23), channel_id=1, source_target_pairs={{224,240},{240,224},{225,241},{241,225},{226,242},{242,226},{227,2... | collective-permute-start | bytes 884744 | tf_op jit(solution)/shard_map/ppermute | solution.py:171
  57.4 5.8 %collective-permute-start.12 = (f32[64,384]{1,0:T(8,128)S(1)}, f32[64,384]{1,0:T(8,128)S(1)}, u32[]{:S(2)}, u32[]{:S(2)}) collective-permute-start(f32[64,384]{1,0:T(8,128)S(1)} %sub.96), channel_id=1, source_target_pairs={{96,128},{112,144},{64,160},{80,176},{32,192},{48,208},{0,224},{16... | collective-permute-start | bytes 294920 | tf_op jit(solution)/shard_map/ppermute | solution.py:159
  58.7 6.5 %collective-permute-start.15 = (f32[192,384]{1,0:T(8,128)}, f32[192,384]{1,0:T(8,128)S(1)}, u32[]{:S(2)}, u32[]{:S(2)}) collective-permute-start(f32[192,384]{1,0:T(8,128)} %collective-permute-done.14), channel_id=1, source_target_pairs={{160,161},{161,160},{162,163},{163,162},{164,165},{165,164},{166,1... | collective-permute-start | bytes 884744 | tf_op jit(solution)/shard_map/ppermute | solution.py:177
  63.7 4.9 %collective-permute-start.16 = (f32[64,384]{1,0:T(8,128)S(1)}, f32[64,384]{1,0:T(8,128)S(1)}, u32[]{:S(2)}, u32[]{:S(2)}) collective-permute-start(f32[64,384]{1,0:T(8,128)S(1)} %sub.99), channel_id=1, source_target_pairs={{128,160},{144,176},{96,192},{112,208},{64,224},{80,240},{129,161}... | collective-permute-start | bytes 294920 | tf_op jit(solution)/shard_map/ppermute | solution.py:159
  64.4 3.8 %collective-permute-start.13 = (f32[64,384]{1,0:T(8,128)S(1)}, f32[64,384]{1,0:T(8,128)S(1)}, u32[]{:S(2)}, u32[]{:S(2)}) collective-permute-start(f32[64,384]{1,0:T(8,128)S(1)} %sub.99), channel_id=1, source_target_pairs={{96,160},{112,176},{64,192},{80,208},{32,224},{48,240},{97,161},{1... | collective-permute-start | bytes 294920 | tf_op jit(solution)/shard_map/ppermute | solution.py:159
  69.1 2.0 %collective-permute-start.17 = (f32[64,384]{1,0:T(8,128)S(1)}, f32[64,384]{1,0:T(8,128)S(1)}, u32[]{:S(2)}, u32[]{:S(2)}) collective-permute-start(f32[64,384]{1,0:T(8,128)S(1)} %sub.102), channel_id=1, source_target_pairs={{128,192},{144,208},{96,224},{112,240},{129,193},{145,209},{97,225... | collective-permute-start | bytes 294920 | tf_op jit(solution)/shard_map/ppermute | solution.py:159
  69.8 1.8 %collective-permute-start.18 = (f32[64,384]{1,0:T(8,128)S(1)}, f32[64,384]{1,0:T(8,128)S(1)}, u32[]{:S(2)}, u32[]{:S(2)}) collective-permute-start(f32[64,384]{1,0:T(8,128)S(1)} %sub.102), channel_id=1, source_target_pairs={{160,192},{176,208},{128,224},{144,240},{161,193},{177,209},{129,2... | collective-permute-start | bytes 294920 | tf_op jit(solution)/shard_map/ppermute | solution.py:159
  70.5 2.9 %collective-permute-start.21 = (f32[192,384]{1,0:T(8,128)S(1)}, f32[192,384]{1,0:T(8,128)S(1)}, u32[]{:S(2)}, u32[]{:S(2)}) collective-permute-start(f32[192,384]{1,0:T(8,128)S(1)} %collective-permute-done.20), channel_id=1, source_target_pairs={{224,225},{225,224},{226,227},{227,226},{228,229},{229,228},{230,2... | collective-permute-start | bytes 884744 | tf_op jit(solution)/shard_map/ppermute | solution.py:177
  72.1 3.6 %collective-permute-start.22 = (f32[64,384]{1,0:T(8,128)S(1)}, f32[64,384]{1,0:T(8,128)S(1)}, u32[]{:S(2)}, u32[]{:S(2)}) collective-permute-start(f32[64,384]{1,0:T(8,128)S(1)} %sub.104), channel_id=1, source_target_pairs={{192,224},{208,240},{193,225},{209,241},{194,226},{210,242},{195,2... | collective-permute-start | bytes 294920 | tf_op jit(solution)/shard_map/ppermute | solution.py:159
  72.7 2.4 %collective-permute-start.19 = (f32[64,384]{1,0:T(8,128)S(1)}, f32[64,384]{1,0:T(8,128)S(1)}, u32[]{:S(2)}, u32[]{:S(2)}) collective-permute-start(f32[64,384]{1,0:T(8,128)S(1)} %sub.104), channel_id=1, source_target_pairs={{160,224},{176,240},{161,225},{177,241},{162,226},{178,242},{163,2... | collective-permute-start | bytes 294920 | tf_op jit(solution)/shard_map/ppermute | solution.py:159
  76.1 7.4 %collective-permute-start.25 = (f32[64,384]{1,0:T(8,128)S(1)}, f32[64,384]{1,0:T(8,128)S(1)}, u32[]{:S(2)}, u32[]{:S(2)}) collective-permute-start(f32[64,384]{1,0:T(8,128)S(1)} %sub.106), channel_id=1, source_target_pairs={{0,0},{1,16},{2,1},{3,17},{16,2},{17,18},{18,3},{19,19},{4,4},{5,2... | collective-permute-start | bytes 294920 | tf_op jit(solution)/shard_map/ppermute | solution.py:212
  79.8 21.1 %collective-permute-start.23 = (f32[64,384]{1,0:T(8,128)S(1)}, f32[64,384]{1,0:T(8,128)S(1)}, u32[]{:S(2)}, u32[]{:S(2)}) collective-permute-start(f32[64,384]{1,0:T(8,128)S(1)} %sub.106), channel_id=1, source_target_pairs={{0,16},{16,0},{32,48},{48,32},{64,80},{80,64},{96,112},{112,96},{1... | collective-permute-start | bytes 294920 | tf_op jit(solution)/shard_map/ppermute | solution.py:213
  84.4 18.2 %copy-start.12 = (f32[32]{0:T(128)S(1)}, f32[32]{0:T(128)}, u32[]{:S(2)}) copy-start(f32[32]{0:T(128)} %copy-done.11) | copy-start | bytes 388
  84.4 19.0 %all-to-all-start = ((f32[8,64,384]{2,1,0:T(8,128)}), f32[8,64,384]{2,1,0:T(8,128)S(1)}, u32[]{:S(2)}, u32[]{:S(2)}) async-start(f32[8,64,384]{2,1,0:T(8,128)} %broadcast_in_dim.10), calls=%async_computation | async-start | bytes 1572864 | tf_op jit(solution)/shard_map/all_to_all | solution.py:218
  91.5 11.1 %collective-permute-start.24 = (f32[32,128]{1,0:T(8,128)S(1)}, f32[32,128]{1,0:T(8,128)S(1)}, u32[]{:S(2)}, u32[]{:S(2)}) collective-permute-start(f32[32,128]{1,0:T(8,128)S(1)} %broadcast_select_fusion.18), channel_id=1, source_target_pairs={{0,0},{1,16},{2,32},{3,48},{4,64},{5,80},{6,96},{7,112},{8,128},{9... | collective-permute-start | bytes 49160 | tf_op jit(solution)/shard_map/ppermute | solution.py:220
  100.9 2.4 %collective-permute-start.26 = (f32[128,384]{1,0:T(8,128)S(1)}, f32[128,384]{1,0:T(8,128)S(1)}, u32[]{:S(2)}, u32[]{:S(2)}) collective-permute-start(f32[128,384]{1,0:T(8,128)S(1)} %maximum_select_fusion.1), channel_id=1, source_target_pairs={{0,1},{1,0},{2,3},{3,2},{4,5},{5,4},{6,7},{7,6},{8,9},{9,8},{10,11... | collective-permute-start | bytes 589832 | tf_op jit(solution)/shard_map/ppermute | solution.py:215
  103.9 2.5 %collective-permute-start.27 = (f32[512,128]{1,0:T(8,128)S(1)}, f32[512,128]{1,0:T(8,128)S(1)}, u32[]{:S(2)}, u32[]{:S(2)}) collective-permute-start(f32[512,128]{1,0:T(8,128)S(1)} %fusion.50), channel_id=1, source_target_pairs={{0,1},{1,0},{2,3},{3,2},{4,5},{5,4},{6,7},{7,6},{8,9},{9,8},{10,11... | collective-permute-start | bytes 786440 | tf_op jit(solution)/shard_map/ppermute | solution.py:223
  107.3 47.3 %all-to-all-start.1 = ((f32[8,128,128]{2,1,0:T(8,128)}), f32[8,128,128]{2,1,0:T(8,128)S(1)}, u32[]{:S(2)}, u32[]{:S(2)}) async-start(f32[8,128,128]{2,1,0:T(8,128)} %bitcast.9), calls=%async_computation.1 | async-start | bytes 1048576 | tf_op jit(solution)/shard_map/all_to_all | solution.py:229
  (12 other events, 42.7 us)

commit v6 on v5

--- a/solution.py
+++ b/solution.py
@@ -4,6 +4,7 @@
 from jax.experimental import pallas as pl
 from jax.experimental.pallas import tpu as pltpu
 from jax.sharding import PartitionSpec as P
+
 
 FULL = lax.Precision.HIGHEST
 BASE = 32
@@ -65,9 +66,9 @@
     )
 
 
-def own_kernel(side_ref, own_ref, out_ref, l_ref, d_ref):
+def own_kernel(place_ref, own_ref, out_ref, l_ref, d_ref):
     height = own_ref.shape[0]
-    even = side_ref[0] == 0
+    even = place_ref[1] == 0
     left, right = own_ref[:, 0:height], own_ref[:, height:]
     l_ref[...] = jnp.where(even, left, right)
     invert_into(l_ref, d_ref)
@@ -75,20 +76,25 @@
     out_ref[:, height:] = jnp.where(even, 0.0, d_ref[...])
 
 
-def own_inverse(side, own):
-    height = own.shape[0]
+def own_inverse(place, factor):
+    height = factor.shape[0]
     square = pltpu.VMEM((height, height), jnp.float32)
     return pl.pallas_call(
         own_kernel,
-        in_specs=[pl.BlockSpec(memory_space=pltpu.SMEM), pl.BlockSpec(memory_space=pltpu.VMEM)],
-        out_shape=jax.ShapeDtypeStruct(own.shape, jnp.float32),
-        scratch_shapes=[square, square],
-    )(side, own)
-
-
-def join_kernel(side_ref, own_ref, other_ref, cross_ref, mine_ref, yours_ref, x_ref, d_ref):
+        grid_spec=pltpu.PrefetchScalarGridSpec(
+            num_scalar_prefetch=1,
+            grid=(1,),
+            in_specs=[pl.BlockSpec((height, 2 * height), lambda _, place: (0, place[0]))],
+            out_specs=pl.BlockSpec((height, 2 * height), lambda _, place: (0, 0)),
+            scratch_shapes=[square, square],
+        ),
+        out_shape=jax.ShapeDtypeStruct((height, 2 * height), jnp.float32),
+    )(place, factor)
+
+
+def join_kernel(place_ref, own_ref, other_ref, cross_ref, mine_ref, yours_ref, x_ref, d_ref):
     height = own_ref.shape[0]
-    even = side_ref[0] == 0
+    even = place_ref[1] == 0
     own, other = own_ref[...], other_ref[...]
     upper = jnp.where(even, own[:, 0:height], other[:, 0:height])
     lower = jnp.where(even, other, own)
@@ -102,7 +108,7 @@
     x_ref[...] = across_rows(cross_ref[...], d_ref[...])
 
 
-def join(side, own, other, cross):
+def join(place, own, other, cross):
     height = own.shape[0]
     tall = jax.ShapeDtypeStruct((2 * height, height), jnp.float32)
     return pl.pallas_call(
@@ -110,7 +116,7 @@
         in_specs=[pl.BlockSpec(memory_space=pltpu.SMEM)] + [pl.BlockSpec(memory_space=pltpu.VMEM)] * 3,
         out_shape=[tall, tall, jax.ShapeDtypeStruct(cross.shape, jnp.float32)],
         scratch_shapes=[pltpu.VMEM((2 * height, 2 * height), jnp.float32)],
-    )(side, own, other, cross)
+    )(place, own, other, cross)
 
 
 def both_of(place, own, other, axis=1):
@@ -135,7 +141,7 @@
     layers = chain // 2
     layer, side = position // 2, position % 2
     odd = layer % 2
-    side_word = jnp.full((1,), side, jnp.int32)
+    place = jnp.stack([layer, side]).astype(jnp.int32)
     pair_all = [(p, p ^ 1) for p in range(chain)]
     scaling = 1.0 / lengthscales
     scaled_candidates = candidate_inputs * scaling[:, None]
@@ -147,13 +153,12 @@
         return lax.optimization_barrier((value, *events))[0]
 
     other_archive = lax.ppermute(archive_inputs, "chain", pair_all)
-    own_diagonal = lax.dynamic_slice_in_dim(factor, layer * 2 * height, 2 * height, 1)
-    own_part = own_inverse(side_word, own_diagonal)
+    own_part = own_inverse(place, factor)
     other_part = lax.ppermute(own_part, "chain", pair_all)
     half = width // 2
     columns = lax.dynamic_slice_in_dim(scaled_candidates, side * half, half, 1)
     cross = matern(columns, both(archive_inputs, other_archive, 1) * scaling[:, None])
-    for_mine, for_yours, solved = join(side_word, own_part, other_part, cross)
+    for_mine, for_yours, solved = join(place, own_part, other_part, cross)
 
     def hop(value, pairs):
         return lax.ppermute(value, "chain", [(2 * a + i, 2 * b + i) for a, b in pairs for i in range(2)])
@@ -184,18 +189,22 @@
     parts = [send(s) for s in range(layers // 2)]
     slabs = [settle(0, *parts[0][:2], after(parts[0][2], solved))]
 
+    far = None
     for t in range(layers - 1):
         near = hop(solved, [(t - k, t + 1 + k) for k in range(layers) if t - k >= 0 and t + 1 + k < layers])
+        pairs = [(t - k, t + 2 + k) for k in range(layers) if t - k >= 0 and t + 2 + k < layers]
+        if pairs:
+            ahead = hop(solved, pairs)
         users = sorted({t - z // 2 for z in range(t + 1, min(2 * t + 1, layers - 1) + 1)})
         left, right = slabs[users[0]]
         if len(users) > 1:
             second = t - layer // 2 == users[1]
             left = after(jnp.where(second, slabs[users[1]][0], left))
             right = after(jnp.where(second, slabs[users[1]][1], right))
-        if t:
-            pairs = [(t - 1 - k, t + 1 + k) for k in range(layers) if t - 1 - k >= 0 and t + 1 + k < layers]
-            solved = after(solved - quick(hop(solved, pairs), left, 1))
+        if far is not None:
+            solved = after(solved - quick(far, left, 1))
         solved = solved - quick(near, right, 1)
+        far = ahead
         if t in (0, 2, 4):
             s = t // 2 + 1
             slabs.append(settle(s, *parts[s][:2], after(parts[s][2], solved)))

time: 157 us -> 159 us (1.013)
  waiting for transfers between devices: 29.1 us -> 39.6 us
  starting transfers between devices: 85.5 us -> 81 us
  local copies, waits for them, and re-layouts: 7.71 us -> 5.65 us
  matrix products: 13.5 us -> 11.7 us
    ppermute x1, starting transfers between devices: 9.41 us -> 1.92 us  [shards(): chosen = lax.ppermute(wanted, ('chain', 'cand'), swap)]
    all_to_all x1, waiting for transfers between devices: 0.01 us -> 5.41 us  [shards(): lax.all_to_all(copies, 'cand', 0, 0, axis_index_groups=same_core, tiled=T...]
    ppermute x13, starting transfers between devices: 28.9 us -> 34.2 us  [hop(): lax.ppermute(value, 'chain', [(2 * a + i, 2 * b + i) for a, b in pairs fo...]
    ppermute x13, waiting for transfers between devices: 3.71 us -> 7.09 us  [hop(): lax.ppermute(value, 'chain', [(2 * a + i, 2 * b + i) for a, b in pairs fo...]
    ppermute x1, waiting for transfers between devices: 1.57 us -> 4.57 us  [shards(): chosen = lax.ppermute(wanted, ('chain', 'cand'), swap)]
    all_to_all x1, starting transfers between devices: 29.1 us -> 26.3 us  [shards(): lax.all_to_all(shares, 'chain', 0, 0, axis_index_groups=same_side, tiled=...]
    dot_general x23, matrix products: 13.5 us -> 11.7 us  [quick(): lax.dot_general(a, b, (((1,), (contract,)), ((), ())), precision=lax.Prec...]
    dynamic_slice x1 -> x0, local copies, waits for them, and re-layouts: 1.68 us -> none  [shards(): lax.dynamic_slice_in_dim(factor, layer * 2 * height, 2 * height, 1)]
  transfers between devices with their start and end apart: 30 -> 30, of which waited for: 8 -> 8; matrix products, arithmetic and copies ran while one was open for 16% -> 13% of each run, Pallas kernels for 5% -> 5%
where the time goes in v6:
time: 159 us; the launch traced here: 157 us
  starting transfers between devices  81 us (51%)
  waiting for transfers between devices  39.6 us (25%)
  matrix products  11.7 us (7%)
  Pallas kernels  8.2 us (5%)
  other arithmetic  7.17 us (5%)
  local copies, waits for them, and re-layouts  5.65 us (4%)
  between operations  4.05 us (3%)
    ppermute x13, starting transfers between devices, hop(): lax.ppermute(value, 'chain', [(2 * a + i, 2 * b + i) for a, b in pairs fo...  34.2 us
    all_to_all x1, starting transfers between devices, shards(): lax.all_to_all(shares, 'chain', 0, 0, axis_index_groups=same_side, tiled=...  26.3 us
    all_to_all x1, waiting for transfers between devices, shards(): lax.all_to_all(shares, 'chain', 0, 0, axis_index_groups=same_side, tiled=...  17.4 us
    dot_general x23, matrix products, quick(): lax.dot_general(a, b, (((1,), (contract,)), ((), ())), precision=lax.Prec...  11.7 us
    ppermute x13, waiting for transfers between devices, hop(): lax.ppermute(value, 'chain', [(2 * a + i, 2 * b + i) for a, b in pairs fo...  7.09 us
    all_to_all x1, starting transfers between devices, shards(): lax.all_to_all(copies, 'cand', 0, 0, axis_index_groups=same_core, tiled=T...  6.96 us
    all_to_all x1, waiting for transfers between devices, shards(): lax.all_to_all(copies, 'cand', 0, 0, axis_index_groups=same_core, tiled=T...  5.41 us
    pallas_call x1, Pallas kernels, own_inverse(): pl.pallas_call(own_kernel, grid_spec=pltpu.PrefetchScalarGridSpec(num_sca...  4.94 us
  transfers between devices with their start and end apart: 30, of which 8 were waited for; matrix products, arithmetic and copies ran while one was open for 13% of the time, Pallas kernels for 5%

profile of v6, /device:TPU:2, one launch (start us, length us, event | category | flops | bytes accessed | tf_op | source)
XLA Modules:
  0.0 157.3 jit_solution(18080547539785473769)
XLA Ops:
  0.6 1.7 %collective-permute-start.1 = (f32[32,192]{1,0:T(8,128)}, f32[32,192]{1,0:T(8,128)}, u32[]{:S(2)}, u32[]{:S(2)}) collective-permute-start(f32[32,192]{1,0:T(8,128)} %param.4), channel_id=1, source_target_pairs={{0,16},{16,0},{32,48},{48,32},{64,80},{80,64},{96,112},{112,96},{1... | collective-permute-start | bytes 73736 | tf_op jit(solution)/shard_map/ppermute | solution.py:155
  2.9 4.9 %shard_map.59.own_ref = f32[192,384]{1,0:T(8,128)} custom-call(s32[2]{0:T(128)} %pad_add_fusion.place_ref, f32[192,3072]{1,0:T(8,128)} %own_ref.1), custom_call_target="tpu_custom_call" | custom-call | tf_op jit(solution)/shard_map/pallas_call | solution.py:82
  8.3 1.5 broadcast_select_fusion.8
  9.8 0.8 collective-permute-start.3
  10.7 0.8 broadcast_multiply_fusion.1
  11.6 0.9 fusion.30
  13.6 3.1 %collective-permute-done.other_ref = f32[192,384]{1,0:T(8,128)} collective-permute-done((f32[192,384]{1,0:T(8,128)}, f32[192,384]{1,0:T(8,128)}, u32[]{:S(2)}, u32[]{:S(2)}) %collective-permute-start) | collective-permute-done | bytes 294944 | tf_op jit(solution)/shard_map/ppermute | solution.py:157
  16.7 3.3 %shard_map.60 = (f32[384,192]{1,0:T(8,128)}, f32[384,192]{1,0:T(8,128)}, f32[64,384]{1,0:T(8,128)}) custom-call(s32[2]{0:T(128)} %pad_add_fusion.place_ref, f32[192,384]{1,0:T(8,128)} %shard_map.59.own_ref, f32[192,384]{1,0:T(8,128)} %collective-permute-done.other_ref, f32[64,384]{1,0:T(8,128)} %exponential_multiply_fusion.cross_ref), custom_call_target="tpu_custom_call" | custom-call | tf_op jit(solution)/shard_map/pallas_call | solution.py:114
  19.9 0.8 collective-permute-start.4
  20.8 9.2 %collective-permute-start.5 = (f32[64,384]{1,0:T(8,128)}, f32[64,384]{1,0:T(8,128)S(1)}, u32[]{:S(2)}, u32[]{:S(2)}) collective-permute-start(f32[64,384]{1,0:T(8,128)} %get-tuple-element.14), channel_id=1, source_target_pairs={{0,64},{16,80},{1,65},{17,81},{2,66},{18,82},{3,67},{19,83},{4,68}... | collective-permute-start | bytes 294920 | tf_op jit(solution)/shard_map/ppermute | solution.py:164
  30.0 1.3 collective-permute-start.2
  35.4 0.8 copy-done.9
  36.6 5.6 %collective-permute-start.7 = (f32[64,384]{1,0:T(8,128)S(1)}, f32[64,384]{1,0:T(8,128)S(1)}, u32[]{:S(2)}, u32[]{:S(2)}) collective-permute-start(f32[64,384]{1,0:T(8,128)S(1)} %convolution_subtract_fusion.6), channel_id=1, source_target_pairs={{32,96},{48,112},{0,128},{16,144},{33,97},{49,113},{1,129},{17,145... | collective-permute-start | bytes 294920 | tf_op jit(solution)/shard_map/ppermute | solution.py:164
  42.3 2.4 %collective-permute-start.6 = (f32[64,384]{1,0:T(8,128)S(1)}, f32[64,384]{1,0:T(8,128)S(1)}, u32[]{:S(2)}, u32[]{:S(2)}) collective-permute-start(f32[64,384]{1,0:T(8,128)S(1)} %convolution_subtract_fusion.6), channel_id=1, source_target_pairs={{32,64},{48,80},{0,96},{16,112},{33,65},{49,81},{1,97},{17,113},{3... | collective-permute-start | bytes 294920 | tf_op jit(solution)/shard_map/ppermute | solution.py:164
  45.9 1.1 collective-permute-done.6
  47.4 8.4 %collective-permute-start.11 = (f32[64,384]{1,0:T(8,128)S(1)}, f32[64,384]{1,0:T(8,128)S(1)}, u32[]{:S(2)}, u32[]{:S(2)}) collective-permute-start(f32[64,384]{1,0:T(8,128)S(1)} %sub.92), channel_id=1, source_target_pairs={{64,128},{80,144},{32,160},{48,176},{0,192},{16,208},{65,129},{81,... | collective-permute-start | bytes 294920 | tf_op jit(solution)/shard_map/ppermute | solution.py:164
  55.8 1.7 %collective-permute-start.10 = (f32[64,384]{1,0:T(8,128)S(1)}, f32[64,384]{1,0:T(8,128)S(1)}, u32[]{:S(2)}, u32[]{:S(2)}) collective-permute-start(f32[64,384]{1,0:T(8,128)S(1)} %sub.92), channel_id=1, source_target_pairs={{64,96},{80,112},{32,128},{48,144},{0,160},{16,176},{65,97},{81,11... | collective-permute-start | bytes 294920 | tf_op jit(solution)/shard_map/ppermute | solution.py:164
  60.0 2.7 %collective-permute-done.10 = f32[64,384]{1,0:T(8,128)S(1)} collective-permute-done((f32[64,384]{1,0:T(8,128)S(1)}, f32[64,384]{1,0:T(8,128)S(1)}, u32[]{:S(2)}, u32[]{:S(2)}) %collective-permute-start.10) | collective-permute-done | bytes 98336 | tf_op jit(solution)/shard_map/ppermute | solution.py:164
  63.8 1.3 collective-permute-start.12
  66.2 3.3 %collective-permute-done.12 = f32[64,384]{1,0:T(8,128)S(1)} collective-permute-done((f32[64,384]{1,0:T(8,128)S(1)}, f32[64,384]{1,0:T(8,128)S(1)}, u32[]{:S(2)}, u32[]{:S(2)}) %collective-permute-start.12) | collective-permute-done | bytes 98336 | tf_op jit(solution)/shard_map/ppermute | solution.py:164
  70.7 0.8 collective-permute-start.16
  80.0 2.1 %collective-permute-start.25 = (f32[64,384]{1,0:T(8,128)S(1)}, f32[64,384]{1,0:T(8,128)S(1)}, u32[]{:S(2)}, u32[]{:S(2)}) collective-permute-start(f32[64,384]{1,0:T(8,128)S(1)} %sub.106), channel_id=1, source_target_pairs={{0,0},{1,16},{2,1},{3,17},{16,2},{17,18},{18,3},{19,19},{4,4},{5,2... | collective-permute-start | bytes 294920 | tf_op jit(solution)/shard_map/ppermute | solution.py:221
  83.9 1.6 %collective-permute-start.23 = (f32[64,384]{1,0:T(8,128)S(1)}, f32[64,384]{1,0:T(8,128)S(1)}, u32[]{:S(2)}, u32[]{:S(2)}) collective-permute-start(f32[64,384]{1,0:T(8,128)S(1)} %sub.106), channel_id=1, source_target_pairs={{0,16},{16,0},{32,48},{48,32},{64,80},{80,64},{96,112},{112,96},{1... | collective-permute-start | bytes 294920 | tf_op jit(solution)/shard_map/ppermute | solution.py:222
  85.5 2.0 %collective-permute-done.25 = f32[64,384]{1,0:T(8,128)S(1)} collective-permute-done((f32[64,384]{1,0:T(8,128)S(1)}, f32[64,384]{1,0:T(8,128)S(1)}, u32[]{:S(2)}, u32[]{:S(2)}) %collective-permute-start.25) | collective-permute-done | bytes 98336 | tf_op jit(solution)/shard_map/ppermute | solution.py:221
  87.5 1.0 broadcast_in_dim.7
  88.4 7.0 %all-to-all-start = ((f32[8,64,384]{2,1,0:T(8,128)}), f32[8,64,384]{2,1,0:T(8,128)S(1)}, u32[]{:S(2)}, u32[]{:S(2)}) async-start(f32[8,64,384]{2,1,0:T(8,128)} %broadcast_in_dim.7), calls=%async_computation | async-start | bytes 1572864 | tf_op jit(solution)/shard_map/all_to_all | solution.py:227
  95.4 1.9 %collective-permute-start.24 = (f32[32,128]{1,0:T(8,128)S(1)}, f32[32,128]{1,0:T(8,128)S(1)}, u32[]{:S(2)}, u32[]{:S(2)}) collective-permute-start(f32[32,128]{1,0:T(8,128)S(1)} %broadcast_select_fusion.18), channel_id=1, source_target_pairs={{0,0},{1,16},{2,32},{3,48},{4,64},{5,80},{6,96},{7,112},{8,128},{9... | collective-permute-start | bytes 49160 | tf_op jit(solution)/shard_map/ppermute | solution.py:229
  97.5 4.6 %collective-permute-done.24 = f32[32,128]{1,0:T(8,128)S(1)} collective-permute-done((f32[32,128]{1,0:T(8,128)S(1)}, f32[32,128]{1,0:T(8,128)S(1)}, u32[]{:S(2)}, u32[]{:S(2)}) %collective-permute-start.24) | collective-permute-done | bytes 16416 | tf_op jit(solution)/shard_map/ppermute | solution.py:229
  102.8 5.4 %all-to-all-done = f32[8,64,384]{2,1,0:T(8,128)S(1)} async-done(((f32[8,64,384]{2,1,0:T(8,128)}), f32[8,64,384]{2,1,0:T(8,128)S(1)}, u32[]{:S(2)}, u32[]{:S(2)}) %all-to-all-start) | async-done | bytes 786464 | tf_op jit(solution)/shard_map/all_to_all | solution.py:227
  111.3 0.8 copy.9
  112.1 26.3 %all-to-all-start.1 = ((f32[8,128,128]{2,1,0:T(8,128)}), f32[8,128,128]{2,1,0:T(8,128)S(1)}, u32[]{:S(2)}, u32[]{:S(2)}) async-start(f32[8,128,128]{2,1,0:T(8,128)} %bitcast.10), calls=%async_computation.1 | async-start | bytes 1048576 | tf_op jit(solution)/shard_map/all_to_all | solution.py:238
  139.3 17.4 %all-to-all-done.1 = f32[8,128,128]{2,1,0:T(8,128)S(1)} async-done(((f32[8,128,128]{2,1,0:T(8,128)}), f32[8,128,128]{2,1,0:T(8,128)S(1)}, u32[]{:S(2)}, u32[]{:S(2)}) %all-to-all-start.1) | async-done | bytes 524320 | tf_op jit(solution)/shard_map/all_to_all | solution.py:238
  (121 shorter events, 26.9 us)
Async XLA Ops:
  0.6 10.9 %collective-permute-start.1 = (f32[32,192]{1,0:T(8,128)}, f32[32,192]{1,0:T(8,128)}, u32[]{:S(2)}, u32[]{:S(2)}) collective-permute-start(f32[32,192]{1,0:T(8,128)} %param.4), channel_id=1, source_target_pairs={{0,16},{16,0},{32,48},{48,32},{64,80},{80,64},{96,112},{112,96},{1... | collective-permute-start | bytes 73736 | tf_op jit(solution)/shard_map/ppermute | solution.py:155
  7.9 8.8 %collective-permute-start = (f32[192,384]{1,0:T(8,128)}, f32[192,384]{1,0:T(8,128)}, u32[]{:S(2)}, u32[]{:S(2)}) collective-permute-start(f32[192,384]{1,0:T(8,128)} %shard_map.59.own_ref), channel_id=1, source_target_pairs={{0,16},{16,0},{32,48},{48,32},{64,80},{80,64},{96,112},{112,96},{1... | collective-permute-start | bytes 884744 | tf_op jit(solution)/shard_map/ppermute | solution.py:157
  9.8 22.9 %copy-start.7 = (f32[192,384]{1,0:T(8,128)S(1)}, f32[192,384]{1,0:T(8,128)}, u32[]{:S(2)}) copy-start(f32[192,384]{1,0:T(8,128)} %get-tuple-element.23) | copy-start | bytes 884740
  9.8 10.1 %collective-permute-start.3 = (f32[192,384]{1,0:T(8,128)}, f32[192,384]{1,0:T(8,128)S(1)}, u32[]{:S(2)}, u32[]{:S(2)}) collective-permute-start(f32[192,384]{1,0:T(8,128)} %get-tuple-element.50), channel_id=1, source_target_pairs={{32,48},{48,32},{64,80},{80,64},{96,112},{112,96},{128,144},{144,1... | collective-permute-start | bytes 884744 | tf_op jit(solution)/shard_map/ppermute | solution.py:176
  10.7 22.8 %copy-start.11 = (f32[32]{0:T(128)}, f32[32]{0:T(128)S(1)}, u32[]{:S(2)}) copy-start(f32[32]{0:T(128)S(1)} %broadcast_divide_fusion) | copy-start | bytes 388
  19.9 12.8 %collective-permute-start.4 = (f32[192,384]{1,0:T(8,128)S(1)}, f32[192,384]{1,0:T(8,128)S(1)}, u32[]{:S(2)}, u32[]{:S(2)}) collective-permute-start(f32[192,384]{1,0:T(8,128)S(1)} %collective-permute-done.3), channel_id=1, source_target_pairs={{32,33},{33,32},{34,35},{35,34},{36,37},{37,36},{38,39},{39,38},{4... | collective-permute-start | bytes 884744 | tf_op jit(solution)/shard_map/ppermute | solution.py:182
  20.8 23.9 %collective-permute-start.5 = (f32[64,384]{1,0:T(8,128)}, f32[64,384]{1,0:T(8,128)S(1)}, u32[]{:S(2)}, u32[]{:S(2)}) collective-permute-start(f32[64,384]{1,0:T(8,128)} %get-tuple-element.14), channel_id=1, source_target_pairs={{0,64},{16,80},{1,65},{17,81},{2,66},{18,82},{3,67},{19,83},{4,68}... | collective-permute-start | bytes 294920 | tf_op jit(solution)/shard_map/ppermute | solution.py:164
  30.0 5.4 %collective-permute-start.2 = (f32[64,384]{1,0:T(8,128)}, f32[64,384]{1,0:T(8,128)S(1)}, u32[]{:S(2)}, u32[]{:S(2)}) collective-permute-start(f32[64,384]{1,0:T(8,128)} %get-tuple-element.14), channel_id=1, source_target_pairs={{0,32},{16,48},{1,33},{17,49},{2,34},{18,50},{3,35},{19,51},{4,36}... | collective-permute-start | bytes 294920 | tf_op jit(solution)/shard_map/ppermute | solution.py:164
  31.3 33.8 %collective-permute-start.14 = (f32[192,384]{1,0:T(8,128)}, f32[192,384]{1,0:T(8,128)S(1)}, u32[]{:S(2)}, u32[]{:S(2)}) collective-permute-start(f32[192,384]{1,0:T(8,128)} %get-tuple-element.21), channel_id=1, source_target_pairs={{160,176},{176,160},{192,208},{208,192},{224,240},{240,224},{161,1... | collective-permute-start | bytes 884744 | tf_op jit(solution)/shard_map/ppermute | solution.py:176
  32.0 10.2 %collective-permute-start.8 = (f32[192,384]{1,0:T(8,128)S(1)}, f32[192,384]{1,0:T(8,128)S(1)}, u32[]{:S(2)}, u32[]{:S(2)}) collective-permute-start(f32[192,384]{1,0:T(8,128)S(1)} %copy-done.8), channel_id=1, source_target_pairs={{96,112},{112,96},{128,144},{144,128},{160,176},{176,160},{192,208... | collective-permute-start | bytes 884744 | tf_op jit(solution)/shard_map/ppermute | solution.py:176
  32.7 42.6 %collective-permute-start.20 = (f32[192,384]{1,0:T(8,128)S(1)}, f32[192,384]{1,0:T(8,128)S(1)}, u32[]{:S(2)}, u32[]{:S(2)}) collective-permute-start(f32[192,384]{1,0:T(8,128)S(1)} %copy-done.7), channel_id=1, source_target_pairs={{224,240},{240,224},{225,241},{241,225},{226,242},{242,226},{227,2... | collective-permute-start | bytes 884744 | tf_op jit(solution)/shard_map/ppermute | solution.py:176
  36.6 22.9 %collective-permute-start.7 = (f32[64,384]{1,0:T(8,128)S(1)}, f32[64,384]{1,0:T(8,128)S(1)}, u32[]{:S(2)}, u32[]{:S(2)}) collective-permute-start(f32[64,384]{1,0:T(8,128)S(1)} %convolution_subtract_fusion.6), channel_id=1, source_target_pairs={{32,96},{48,112},{0,128},{16,144},{33,97},{49,113},{1,129},{17,145... | collective-permute-start | bytes 294920 | tf_op jit(solution)/shard_map/ppermute | solution.py:164
  42.3 4.6 %collective-permute-start.6 = (f32[64,384]{1,0:T(8,128)S(1)}, f32[64,384]{1,0:T(8,128)S(1)}, u32[]{:S(2)}, u32[]{:S(2)}) collective-permute-start(f32[64,384]{1,0:T(8,128)S(1)} %convolution_subtract_fusion.6), channel_id=1, source_target_pairs={{32,64},{48,80},{0,96},{16,112},{33,65},{49,81},{1,97},{17,113},{3... | collective-permute-start | bytes 294920 | tf_op jit(solution)/shard_map/ppermute | solution.py:164
  44.7 11.0 %collective-permute-start.9 = (f32[192,384]{1,0:T(8,128)S(1)}, f32[192,384]{1,0:T(8,128)S(1)}, u32[]{:S(2)}, u32[]{:S(2)}) collective-permute-start(f32[192,384]{1,0:T(8,128)S(1)} %collective-permute-done.8), channel_id=1, source_target_pairs={{96,97},{97,96},{98,99},{99,98},{100,101},{101,100},{102,103},{103... | collective-permute-start | bytes 884744 | tf_op jit(solution)/shard_map/ppermute | solution.py:182
  47.4 18.4 %collective-permute-start.11 = (f32[64,384]{1,0:T(8,128)S(1)}, f32[64,384]{1,0:T(8,128)S(1)}, u32[]{:S(2)}, u32[]{:S(2)}) collective-permute-start(f32[64,384]{1,0:T(8,128)S(1)} %sub.92), channel_id=1, source_target_pairs={{64,128},{80,144},{32,160},{48,176},{0,192},{16,208},{65,129},{81,... | collective-permute-start | bytes 294920 | tf_op jit(solution)/shard_map/ppermute | solution.py:164
  55.8 6.9 %collective-permute-start.10 = (f32[64,384]{1,0:T(8,128)S(1)}, f32[64,384]{1,0:T(8,128)S(1)}, u32[]{:S(2)}, u32[]{:S(2)}) collective-permute-start(f32[64,384]{1,0:T(8,128)S(1)} %sub.92), channel_id=1, source_target_pairs={{64,96},{80,112},{32,128},{48,144},{0,160},{16,176},{65,97},{81,11... | collective-permute-start | bytes 294920 | tf_op jit(solution)/shard_map/ppermute | solution.py:164
  63.1 10.0 %collective-permute-start.13 = (f32[64,384]{1,0:T(8,128)S(1)}, f32[64,384]{1,0:T(8,128)S(1)}, u32[]{:S(2)}, u32[]{:S(2)}) collective-permute-start(f32[64,384]{1,0:T(8,128)S(1)} %sub.96), channel_id=1, source_target_pairs={{96,160},{112,176},{64,192},{80,208},{32,224},{48,240},{97,161},{1... | collective-permute-start | bytes 294920 | tf_op jit(solution)/shard_map/ppermute | solution.py:164
  63.8 5.8 %collective-permute-start.12 = (f32[64,384]{1,0:T(8,128)S(1)}, f32[64,384]{1,0:T(8,128)S(1)}, u32[]{:S(2)}, u32[]{:S(2)}) collective-permute-start(f32[64,384]{1,0:T(8,128)S(1)} %sub.96), channel_id=1, source_target_pairs={{96,128},{112,144},{64,160},{80,176},{32,192},{48,208},{0,224},{16... | collective-permute-start | bytes 294920 | tf_op jit(solution)/shard_map/ppermute | solution.py:164
  65.1 6.4 %collective-permute-start.15 = (f32[192,384]{1,0:T(8,128)S(1)}, f32[192,384]{1,0:T(8,128)S(1)}, u32[]{:S(2)}, u32[]{:S(2)}) collective-permute-start(f32[192,384]{1,0:T(8,128)S(1)} %collective-permute-done.14), channel_id=1, source_target_pairs={{160,161},{161,160},{162,163},{163,162},{164,165},{165,164},{166,1... | collective-permute-start | bytes 884744 | tf_op jit(solution)/shard_map/ppermute | solution.py:182
  70.0 6.1 %collective-permute-start.17 = (f32[64,384]{1,0:T(8,128)S(1)}, f32[64,384]{1,0:T(8,128)S(1)}, u32[]{:S(2)}, u32[]{:S(2)}) collective-permute-start(f32[64,384]{1,0:T(8,128)S(1)} %sub.99), channel_id=1, source_target_pairs={{128,192},{144,208},{96,224},{112,240},{129,193},{145,209},{97,225... | collective-permute-start | bytes 294920 | tf_op jit(solution)/shard_map/ppermute | solution.py:164
  70.7 2.9 %collective-permute-start.16 = (f32[64,384]{1,0:T(8,128)S(1)}, f32[64,384]{1,0:T(8,128)S(1)}, u32[]{:S(2)}, u32[]{:S(2)}) collective-permute-start(f32[64,384]{1,0:T(8,128)S(1)} %sub.99), channel_id=1, source_target_pairs={{128,160},{144,176},{96,192},{112,208},{64,224},{80,240},{129,161}... | collective-permute-start | bytes 294920 | tf_op jit(solution)/shard_map/ppermute | solution.py:164
  74.0 5.1 %collective-permute-start.19 = (f32[64,384]{1,0:T(8,128)S(1)}, f32[64,384]{1,0:T(8,128)S(1)}, u32[]{:S(2)}, u32[]{:S(2)}) collective-permute-start(f32[64,384]{1,0:T(8,128)S(1)} %sub.102), channel_id=1, source_target_pairs={{160,224},{176,240},{161,225},{177,241},{162,226},{178,242},{163,2... | collective-permute-start | bytes 294920 | tf_op jit(solution)/shard_map/ppermute | solution.py:164
  74.7 1.8 %collective-permute-start.18 = (f32[64,384]{1,0:T(8,128)S(1)}, f32[64,384]{1,0:T(8,128)S(1)}, u32[]{:S(2)}, u32[]{:S(2)}) collective-permute-start(f32[64,384]{1,0:T(8,128)S(1)} %sub.102), channel_id=1, source_target_pairs={{160,192},{176,208},{128,224},{144,240},{161,193},{177,209},{129,2... | collective-permute-start | bytes 294920 | tf_op jit(solution)/shard_map/ppermute | solution.py:164
  75.4 2.3 %collective-permute-start.21 = (f32[192,384]{1,0:T(8,128)S(1)}, f32[192,384]{1,0:T(8,128)S(1)}, u32[]{:S(2)}, u32[]{:S(2)}) collective-permute-start(f32[192,384]{1,0:T(8,128)S(1)} %collective-permute-done.20), channel_id=1, source_target_pairs={{224,225},{225,224},{226,227},{227,226},{228,229},{229,228},{230,2... | collective-permute-start | bytes 884744 | tf_op jit(solution)/shard_map/ppermute | solution.py:182
  77.0 2.6 %collective-permute-start.22 = (f32[64,384]{1,0:T(8,128)S(1)}, f32[64,384]{1,0:T(8,128)S(1)}, u32[]{:S(2)}, u32[]{:S(2)}) collective-permute-start(f32[64,384]{1,0:T(8,128)S(1)} %sub.104), channel_id=1, source_target_pairs={{192,224},{208,240},{193,225},{209,241},{194,226},{210,242},{195,2... | collective-permute-start | bytes 294920 | tf_op jit(solution)/shard_map/ppermute | solution.py:164
  80.0 7.5 %collective-permute-start.25 = (f32[64,384]{1,0:T(8,128)S(1)}, f32[64,384]{1,0:T(8,128)S(1)}, u32[]{:S(2)}, u32[]{:S(2)}) collective-permute-start(f32[64,384]{1,0:T(8,128)S(1)} %sub.106), channel_id=1, source_target_pairs={{0,0},{1,16},{2,1},{3,17},{16,2},{17,18},{18,3},{19,19},{4,4},{5,2... | collective-permute-start | bytes 294920 | tf_op jit(solution)/shard_map/ppermute | solution.py:221
  83.9 13.5 %collective-permute-start.23 = (f32[64,384]{1,0:T(8,128)S(1)}, f32[64,384]{1,0:T(8,128)S(1)}, u32[]{:S(2)}, u32[]{:S(2)}) collective-permute-start(f32[64,384]{1,0:T(8,128)S(1)} %sub.106), channel_id=1, source_target_pairs={{0,16},{16,0},{32,48},{48,32},{64,80},{80,64},{96,112},{112,96},{1... | collective-permute-start | bytes 294920 | tf_op jit(solution)/shard_map/ppermute | solution.py:222
  88.4 19.8 %all-to-all-start = ((f32[8,64,384]{2,1,0:T(8,128)}), f32[8,64,384]{2,1,0:T(8,128)S(1)}, u32[]{:S(2)}, u32[]{:S(2)}) async-start(f32[8,64,384]{2,1,0:T(8,128)} %broadcast_in_dim.7), calls=%async_computation | async-start | bytes 1572864 | tf_op jit(solution)/shard_map/all_to_all | solution.py:227
  95.4 6.6 %collective-permute-start.24 = (f32[32,128]{1,0:T(8,128)S(1)}, f32[32,128]{1,0:T(8,128)S(1)}, u32[]{:S(2)}, u32[]{:S(2)}) collective-permute-start(f32[32,128]{1,0:T(8,128)S(1)} %broadcast_select_fusion.18), channel_id=1, source_target_pairs={{0,0},{1,16},{2,32},{3,48},{4,64},{5,80},{6,96},{7,112},{8,128},{9... | collective-permute-start | bytes 49160 | tf_op jit(solution)/shard_map/ppermute | solution.py:229
  97.4 5.4 %collective-permute-start.26 = (f32[128,384]{1,0:T(8,128)S(1)}, f32[128,384]{1,0:T(8,128)S(1)}, u32[]{:S(2)}, u32[]{:S(2)}) collective-permute-start(f32[128,384]{1,0:T(8,128)S(1)} %maximum_select_fusion.1), channel_id=1, source_target_pairs={{0,1},{1,0},{2,3},{3,2},{4,5},{5,4},{6,7},{7,6},{8,9},{9,8},{10,11... | collective-permute-start | bytes 589832 | tf_op jit(solution)/shard_map/ppermute | solution.py:224
  108.7 2.5 %collective-permute-start.27 = (f32[512,128]{1,0:T(8,128)S(1)}, f32[512,128]{1,0:T(8,128)S(1)}, u32[]{:S(2)}, u32[]{:S(2)}) collective-permute-start(f32[512,128]{1,0:T(8,128)S(1)} %fusion.50), channel_id=1, source_target_pairs={{0,1},{1,0},{2,3},{3,2},{4,5},{5,4},{6,7},{7,6},{8,9},{9,8},{10,11... | collective-permute-start | bytes 786440 | tf_op jit(solution)/shard_map/ppermute | solution.py:232
  112.1 44.5 %all-to-all-start.1 = ((f32[8,128,128]{2,1,0:T(8,128)}), f32[8,128,128]{2,1,0:T(8,128)S(1)}, u32[]{:S(2)}, u32[]{:S(2)}) async-start(f32[8,128,128]{2,1,0:T(8,128)} %bitcast.10), calls=%async_computation.1 | async-start | bytes 1048576 | tf_op jit(solution)/shard_map/all_to_all | solution.py:238
  (12 other events, 74.7 us)

commit v7 on v6

--- a/solution.py
+++ b/solution.py
@@ -166,13 +166,13 @@
     span = 2 * height
     core = lax.axis_index("cand") % 2
     late = after(factor, own_part)
-    chunks = [late[:, k * span : (k + 1) * span] for k in range(layers)]
 
     def send(s):
+        chunks = [(late if s else factor)[:, k * span : (k + 1) * span] for k in range(layers)]
         left = jnp.where(odd == 1, chunks[max(2 * s - 1, 0)], chunks[2 * s])
         right = jnp.where(odd == 1, chunks[2 * s], chunks[2 * s + 1])
         sent = jnp.where(core == 0, left, right)
-        sent = after(sent, solved) if s else sent
+        sent = after(sent, solved) if s > 1 else sent
         got = lax.ppermute(sent, "chain", [(p, p ^ 1) for p in range(chain) if p // 2 >= 2 * s + 1])
         return left, right, got
 
@@ -187,53 +187,61 @@
         return after(slab[:, :span]), after(slab[:, span:])
 
     parts = [send(s) for s in range(layers // 2)]
-    slabs = [settle(0, *parts[0][:2], after(parts[0][2], solved))]
-
-    far = None
+    slabs = [settle(0, *parts[0])]
+
+    far = mid = before = None
     for t in range(layers - 1):
-        near = hop(solved, [(t - k, t + 1 + k) for k in range(layers) if t - k >= 0 and t + 1 + k < layers])
+        hops = [(k, t - k, t + 1 + k) for k in range(layers) if t - k >= 0 and t + 1 + k < layers]
+        near = hop(solved, [(a, b) for k, a, b in hops if k != 1])
         pairs = [(t - k, t + 2 + k) for k in range(layers) if t - k >= 0 and t + 2 + k < layers]
         if pairs:
             ahead = hop(solved, pairs)
+        behind = [(a, b) for k, a, b in hops if k == 1]
+        if behind:
+            behind = hop(solved, behind)
         users = sorted({t - z // 2 for z in range(t + 1, min(2 * t + 1, layers - 1) + 1)})
         left, right = slabs[users[0]]
         if len(users) > 1:
             second = t - layer // 2 == users[1]
             left = after(jnp.where(second, slabs[users[1]][0], left))
             right = after(jnp.where(second, slabs[users[1]][1], right))
+        if mid is not None:
+            solved = solved - quick(mid, before, 1)
         if far is not None:
             solved = after(solved - quick(far, left, 1))
         solved = solved - quick(near, right, 1)
-        far = ahead
+        far, mid, before = ahead, (behind if len(behind) else None), right
         if t in (0, 2, 4):
             s = t // 2 + 1
             slabs.append(settle(s, *parts[s][:2], after(parts[s][2], solved)))
         if t == 3:
             wanted = jnp.where(unset(solved) == 0, candidate_inputs, 0.0)
-    turn = [
-        ((2 * z + h) * cand + 4 * j + 2 * k + y, (2 * z + y) * cand + 4 * j + 2 * h + k)
-        for z in range(layers)
-        for j in range(cand // 4)
-        for h in range(2)
-        for k in range(2)
-        for y in range(2)
+    turns = [
+        [
+            ((2 * z + h) * cand + 8 * k + 2 * x + y, (2 * z + y) * cand + 8 * (h ^ other) + 2 * x + k)
+            for z in range(layers)
+            for h in range(2)
+            for k in range(2)
+            for x in range(cand // 4)
+            for y in range(2)
+        ]
+        for other in range(2)
     ]
-    turned = lax.ppermute(solved, ("chain", "cand"), turn)
+    turned = [lax.ppermute(solved, ("chain", "cand"), turn) for turn in turns]
+    turned = both_of(lax.axis_index("cand") // 8, *turned, 0)
     columns_all = both(solved, lax.ppermute(solved, "chain", pair_all), 0)
     rows = jnp.where(side == 0, columns_all[:, :height], columns_all[:, height:]).T
     twin_columns = lax.ppermute(columns_all, "cand", [(c, c ^ 1) for c in range(cand)])
-    same_core = [[2 * i + k for i in range(cand // 2)] for k in range(2)]
-    copies = jnp.broadcast_to(turned[None], (cand // 2,) + turned.shape)
-    others = lax.all_to_all(copies, "cand", 0, 0, axis_index_groups=same_core, tiled=True)
+    same_row = [[8 * j + 2 * x + k for x in range(cand // 4)] for j in range(2) for k in range(2)]
+    copies = jnp.broadcast_to(turned[None], (cand // 4,) + turned.shape)
+    others = lax.all_to_all(copies, "cand", 0, 0, axis_index_groups=same_row, tiled=True)
     swap = [(a * cand + b, b * cand + a) for a in range(chain) for b in range(cand)]
     chosen = lax.ppermute(wanted, ("chain", "cand"), swap)
     prior_cov = matern(chosen * after(scaling, solved)[:, None], scaled_candidates)
-    others = others.reshape(cand // 2 * half, span)
+    others = others.reshape(cand // 4 * width, span)
     theirs = lax.ppermute(quick(others, twin_columns, 1), "cand", [(c, c ^ 1) for c in range(cand)])
     ours = quick(others, columns_all, 1)
-    ours = ours.reshape(layers // 2, 1, width, width)
-    theirs = theirs.reshape(layers // 2, 1, width, width)
-    shares = both_of(core + unset(prior_cov), ours, theirs).reshape(layers, width, width)
+    shares = both_of(core + unset(prior_cov), ours, theirs, 0).reshape(layers, width, width)
     same_side = [[2 * z + y for z in range(layers)] for y in range(2)]
     shared = lax.all_to_all(shares, "chain", 0, 0, axis_index_groups=same_side, tiled=True).sum(axis=0)
     return (rows, prior_cov - shared)

time: 159 us -> 156 us (0.981)
  waiting for transfers between devices: 39.6 us -> 30.6 us
  starting transfers between devices: 81 us -> 83.9 us
  other arithmetic: 7.17 us -> 9.41 us
  matrix products: 11.7 us -> 13.9 us
    ppermute x13 -> x18, waiting for transfers between devices: 7.09 us -> 4.23 us  [hop(): lax.ppermute(value, 'chain', [(2 * a + i, 2 * b + i) for a, b in pairs fo...]
    ppermute x1 -> x2, starting transfers between devices: 2.06 us -> 4.84 us  [shards(): turned = [lax.ppermute(solved, ('chain', 'cand'), turn) for turn in turns]]
    ppermute x1, waiting for transfers between devices: 3.08 us -> 0.35 us  [shards(): other_part = lax.ppermute(own_part, 'chain', pair_all)]
    dot_general x23 -> x28, matrix products: 11.7 us -> 13.9 us  [quick(): lax.dot_general(a, b, (((1,), (contract,)), ((), ())), precision=lax.Prec...]
    all_to_all x1, starting transfers between devices: 6.96 us -> 4.82 us  [shards(): lax.all_to_all(copies, 'cand', 0, 0, axis_index_groups=same_row, tiled=True)]
    ppermute x13 -> x18, starting transfers between devices: 34.2 us -> 35.2 us  [hop(): lax.ppermute(value, 'chain', [(2 * a + i, 2 * b + i) for a, b in pairs fo...]
  transfers between devices with their start and end apart: 30 -> 36, of which waited for: 8 -> 7; matrix products, arithmetic and copies ran while one was open for 13% -> 15% of each run, Pallas kernels for 5% -> 5%
where the time goes in v7:
time: 156 us; the launch traced here: 155 us
  starting transfers between devices  83.9 us (54%)
  waiting for transfers between devices  30.6 us (20%)
  matrix products  13.9 us (9%)
  other arithmetic  9.41 us (6%)
  Pallas kernels  8.22 us (5%)
  local copies, waits for them, and re-layouts  4.79 us (3%)
  between operations  4.03 us (3%)
    ppermute x18, starting transfers between devices, hop(): lax.ppermute(value, 'chain', [(2 * a + i, 2 * b + i) for a, b in pairs fo...  35.2 us
    all_to_all x1, starting transfers between devices, shards(): lax.all_to_all(shares, 'chain', 0, 0, axis_index_groups=same_side, tiled=...  26.9 us
    all_to_all x1, waiting for transfers between devices, shards(): lax.all_to_all(shares, 'chain', 0, 0, axis_index_groups=same_side, tiled=...  17.4 us
    dot_general x28, matrix products, quick(): lax.dot_general(a, b, (((1,), (contract,)), ((), ())), precision=lax.Prec...  13.9 us
    pallas_call x1, Pallas kernels, own_inverse(): pl.pallas_call(own_kernel, grid_spec=pltpu.PrefetchScalarGridSpec(num_sca...  4.96 us
    ppermute x2, starting transfers between devices, shards(): turned = [lax.ppermute(solved, ('chain', 'cand'), turn) for turn in turns]  4.84 us
    all_to_all x1, starting transfers between devices, shards(): lax.all_to_all(copies, 'cand', 0, 0, axis_index_groups=same_row, tiled=True)  4.82 us
    ppermute x18, waiting for transfers between devices, hop(): lax.ppermute(value, 'chain', [(2 * a + i, 2 * b + i) for a, b in pairs fo...  4.23 us
  transfers between devices with their start and end apart: 36, of which 7 were waited for; matrix products, arithmetic and copies ran while one was open for 15% of the time, Pallas kernels for 5%

profile of v7, /device:TPU:2, one launch (start us, length us, event | category | flops | bytes accessed | tf_op | source)
XLA Modules:
  0.0 154.9 jit_solution(12906617278156830134)
XLA Ops:
  0.6 1.7 %collective-permute-start.1 = (f32[32,192]{1,0:T(8,128)}, f32[32,192]{1,0:T(8,128)}, u32[]{:S(2)}, u32[]{:S(2)}) collective-permute-start(f32[32,192]{1,0:T(8,128)} %param.4), channel_id=1, source_target_pairs={{0,16},{16,0},{32,48},{48,32},{64,80},{80,64},{96,112},{112,96},{1... | collective-permute-start | bytes 73736 | tf_op jit(solution)/shard_map/ppermute | solution.py:155
  2.8 5.0 %shard_map.59.own_ref = f32[192,384]{1,0:T(8,128)} custom-call(s32[2]{0:T(128)} %pad_add_fusion.place_ref, f32[192,3072]{1,0:T(8,128)} %own_ref.1), custom_call_target="tpu_custom_call" | custom-call | tf_op jit(solution)/shard_map/pallas_call | solution.py:82
  8.3 1.0 broadcast_select_fusion.17
  9.2 1.5 collective-permute-start.3
  10.7 1.2 broadcast_select_fusion.8
  11.9 0.8 collective-permute-start.9
  13.5 0.9 fusion.34
  15.5 0.7 exponential_multiply_fusion.cross_ref
  16.6 3.3 %shard_map.60 = (f32[384,192]{1,0:T(8,128)}, f32[384,192]{1,0:T(8,128)}, f32[64,384]{1,0:T(8,128)}) custom-call(s32[2]{0:T(128)} %pad_add_fusion.place_ref, f32[192,384]{1,0:T(8,128)} %shard_map.59.own_ref, f32[192,384]{1,0:T(8,128)} %collective-permute-done.other_ref, f32[64,384]{1,0:T(8,128)} %exponential_multiply_fusion.cross_ref), custom_call_target="tpu_custom_call" | custom-call | tf_op jit(solution)/shard_map/pallas_call | solution.py:114
  19.9 14.6 %collective-permute-start.5 = (f32[64,384]{1,0:T(8,128)}, f32[64,384]{1,0:T(8,128)S(1)}, u32[]{:S(2)}, u32[]{:S(2)}) collective-permute-start(f32[64,384]{1,0:T(8,128)} %get-tuple-element.12), channel_id=1, source_target_pairs={{0,64},{16,80},{1,65},{17,81},{2,66},{18,82},{3,67},{19,83},{4,68}... | collective-permute-start | bytes 294920 | tf_op jit(solution)/shard_map/ppermute | solution.py:164
  34.5 1.3 collective-permute-start.2
  37.2 1.0 broadcast_select_fusion.16
  40.1 0.8 copy-done.9
  41.4 5.4 %collective-permute-start.8 = (f32[64,384]{1,0:T(8,128)S(1)}, f32[64,384]{1,0:T(8,128)S(1)}, u32[]{:S(2)}, u32[]{:S(2)}) collective-permute-start(f32[64,384]{1,0:T(8,128)S(1)} %convolution_subtract_fusion.6), channel_id=1, source_target_pairs={{32,96},{48,112},{0,128},{16,144},{33,97},{49,113},{1,129},{17,145... | collective-permute-start | bytes 294920 | tf_op jit(solution)/shard_map/ppermute | solution.py:164
  48.6 1.3 collective-permute-start.7
  50.3 2.3 %collective-permute-start.13 = (f32[64,384]{1,0:T(8,128)S(1)}, f32[64,384]{1,0:T(8,128)S(1)}, u32[]{:S(2)}, u32[]{:S(2)}) collective-permute-start(f32[64,384]{1,0:T(8,128)S(1)} %sub.110), channel_id=1, source_target_pairs={{64,128},{80,144},{32,160},{48,176},{0,192},{16,208},{65,129},{81,... | collective-permute-start | bytes 294920 | tf_op jit(solution)/shard_map/ppermute | solution.py:164
  55.8 1.7 %collective-permute-start.11 = (f32[64,384]{1,0:T(8,128)S(1)}, f32[64,384]{1,0:T(8,128)S(1)}, u32[]{:S(2)}, u32[]{:S(2)}) collective-permute-start(f32[64,384]{1,0:T(8,128)S(1)} %sub.110), channel_id=1, source_target_pairs={{64,96},{80,112},{0,160},{16,176},{65,97},{81,113},{1,161},{17,177... | collective-permute-start | bytes 294920 | tf_op jit(solution)/shard_map/ppermute | solution.py:164
  57.9 2.1 %collective-permute-done.11 = f32[64,384]{1,0:T(8,128)S(1)} collective-permute-done((f32[64,384]{1,0:T(8,128)S(1)}, f32[64,384]{1,0:T(8,128)S(1)}, u32[]{:S(2)}, u32[]{:S(2)}) %collective-permute-start.11) | collective-permute-done | bytes 98336 | tf_op jit(solution)/shard_map/ppermute | solution.py:164
  62.2 1.3 collective-permute-start.14
  63.5 0.9 collective-permute-start.18
  64.8 2.1 %collective-permute-done.14 = f32[64,384]{1,0:T(8,128)S(1)} collective-permute-done((f32[64,384]{1,0:T(8,128)S(1)}, f32[64,384]{1,0:T(8,128)S(1)}, u32[]{:S(2)}, u32[]{:S(2)}) %collective-permute-start.14) | collective-permute-done | bytes 98336 | tf_op jit(solution)/shard_map/ppermute | solution.py:164
  80.6 4.2 %collective-permute-start.31 = (f32[64,384]{1,0:T(8,128)S(1)}, f32[64,384]{1,0:T(8,128)S(1)}, u32[]{:S(2)}, u32[]{:S(2)}) collective-permute-start(f32[64,384]{1,0:T(8,128)S(1)} %sub.129), channel_id=1, source_target_pairs={{0,8},{1,24},{2,10},{3,26},{4,12},{5,28},{6,14},{7,30},{8,9},{9,25... | collective-permute-start | bytes 294920 | tf_op jit(solution)/shard_map/ppermute | solution.py:230
  86.7 1.6 %collective-permute-done.31 = f32[64,384]{1,0:T(8,128)S(1)} collective-permute-done((f32[64,384]{1,0:T(8,128)S(1)}, f32[64,384]{1,0:T(8,128)S(1)}, u32[]{:S(2)}, u32[]{:S(2)}) %collective-permute-start.31) | collective-permute-done | bytes 98336 | tf_op jit(solution)/shard_map/ppermute | solution.py:230
  88.3 0.9 broadcast_in_dim.7
  89.3 4.8 %all-to-all-start = ((f32[4,128,384]{2,1,0:T(8,128)}), f32[4,128,384]{2,1,0:T(8,128)S(1)}, u32[]{:S(2)}, u32[]{:S(2)}) async-start(f32[4,128,384]{2,1,0:T(8,128)} %broadcast_in_dim.7), calls=%async_computation | async-start | bytes 1572864 | tf_op jit(solution)/shard_map/all_to_all | solution.py:237
  94.1 3.2 %collective-permute-start.29 = (f32[32,128]{1,0:T(8,128)S(1)}, f32[32,128]{1,0:T(8,128)S(1)}, u32[]{:S(2)}, u32[]{:S(2)}) collective-permute-start(f32[32,128]{1,0:T(8,128)S(1)} %broadcast_select_fusion.18), channel_id=1, source_target_pairs={{0,0},{1,16},{2,32},{3,48},{4,64},{5,80},{6,96},{7,112},{8,128},{9... | collective-permute-start | bytes 49160 | tf_op jit(solution)/shard_map/ppermute | solution.py:239
  97.5 3.1 %collective-permute-done.29 = f32[32,128]{1,0:T(8,128)S(1)} collective-permute-done((f32[32,128]{1,0:T(8,128)S(1)}, f32[32,128]{1,0:T(8,128)S(1)}, u32[]{:S(2)}, u32[]{:S(2)}) %collective-permute-start.29) | collective-permute-done | bytes 16416 | tf_op jit(solution)/shard_map/ppermute | solution.py:239
  101.4 4.0 %all-to-all-done = f32[4,128,384]{2,1,0:T(8,128)S(1)} async-done(((f32[4,128,384]{2,1,0:T(8,128)}), f32[4,128,384]{2,1,0:T(8,128)S(1)}, u32[]{:S(2)}, u32[]{:S(2)}) %all-to-all-start) | async-done | bytes 786464 | tf_op jit(solution)/shard_map/all_to_all | solution.py:237
  108.3 0.8 maximum_select_fusion
  109.1 26.9 %all-to-all-start.1 = ((f32[8,128,128]{2,1,0:T(8,128)}), f32[8,128,128]{2,1,0:T(8,128)S(1)}, u32[]{:S(2)}, u32[]{:S(2)}) async-start(f32[8,128,128]{2,1,0:T(8,128)} %bitcast.6), calls=%async_computation.1 | async-start | bytes 1048576 | tf_op jit(solution)/shard_map/all_to_all | solution.py:246
  136.1 0.7 copy.7
  136.8 17.4 %all-to-all-done.1 = f32[8,128,128]{2,1,0:T(8,128)S(1)} async-done(((f32[8,128,128]{2,1,0:T(8,128)}), f32[8,128,128]{2,1,0:T(8,128)S(1)}, u32[]{:S(2)}, u32[]{:S(2)}) %all-to-all-start.1) | async-done | bytes 524320 | tf_op jit(solution)/shard_map/all_to_all | solution.py:246
  (133 shorter events, 32.6 us)
Async XLA Ops:
  0.6 12.9 %collective-permute-start.1 = (f32[32,192]{1,0:T(8,128)}, f32[32,192]{1,0:T(8,128)}, u32[]{:S(2)}, u32[]{:S(2)}) collective-permute-start(f32[32,192]{1,0:T(8,128)} %param.4), channel_id=1, source_target_pairs={{0,16},{16,0},{32,48},{48,32},{64,80},{80,64},{96,112},{112,96},{1... | collective-permute-start | bytes 73736 | tf_op jit(solution)/shard_map/ppermute | solution.py:155
  7.8 8.8 %collective-permute-start = (f32[192,384]{1,0:T(8,128)}, f32[192,384]{1,0:T(8,128)}, u32[]{:S(2)}, u32[]{:S(2)}) collective-permute-start(f32[192,384]{1,0:T(8,128)} %shard_map.59.own_ref), channel_id=1, source_target_pairs={{0,16},{16,0},{32,48},{48,32},{64,80},{80,64},{96,112},{112,96},{1... | collective-permute-start | bytes 884744 | tf_op jit(solution)/shard_map/ppermute | solution.py:157
  9.2 5.2 %collective-permute-start.3 = (f32[192,384]{1,0:T(8,128)}, f32[192,384]{1,0:T(8,128)}, u32[]{:S(2)}, u32[]{:S(2)}) collective-permute-start(f32[192,384]{1,0:T(8,128)} %get-tuple-element.35), channel_id=1, source_target_pairs={{32,48},{48,32},{64,80},{80,64},{96,112},{112,96},{128,144},{144,1... | collective-permute-start | bytes 884744 | tf_op jit(solution)/shard_map/ppermute | solution.py:176
  11.9 34.9 %collective-permute-start.9 = (f32[192,384]{1,0:T(8,128)}, f32[192,384]{1,0:T(8,128)S(1)}, u32[]{:S(2)}, u32[]{:S(2)}) collective-permute-start(f32[192,384]{1,0:T(8,128)} %get-tuple-element.37), channel_id=1, source_target_pairs={{96,112},{112,96},{128,144},{144,128},{160,176},{176,160},{192,208... | collective-permute-start | bytes 884744 | tf_op jit(solution)/shard_map/ppermute | solution.py:176
  14.5 22.0 %collective-permute-start.4 = (f32[192,384]{1,0:T(8,128)}, f32[192,384]{1,0:T(8,128)S(1)}, u32[]{:S(2)}, u32[]{:S(2)}) collective-permute-start(f32[192,384]{1,0:T(8,128)} %collective-permute-done.3), channel_id=1, source_target_pairs={{32,33},{33,32},{34,35},{35,34},{36,37},{37,36},{38,39},{39,38},{4... | collective-permute-start | bytes 884744 | tf_op jit(solution)/shard_map/ppermute | solution.py:182
  19.9 27.6 %collective-permute-start.5 = (f32[64,384]{1,0:T(8,128)}, f32[64,384]{1,0:T(8,128)S(1)}, u32[]{:S(2)}, u32[]{:S(2)}) collective-permute-start(f32[64,384]{1,0:T(8,128)} %get-tuple-element.12), channel_id=1, source_target_pairs={{0,64},{16,80},{1,65},{17,81},{2,66},{18,82},{3,67},{19,83},{4,68}... | collective-permute-start | bytes 294920 | tf_op jit(solution)/shard_map/ppermute | solution.py:164
  34.5 5.6 %collective-permute-start.2 = (f32[64,384]{1,0:T(8,128)}, f32[64,384]{1,0:T(8,128)S(1)}, u32[]{:S(2)}, u32[]{:S(2)}) collective-permute-start(f32[64,384]{1,0:T(8,128)} %get-tuple-element.12), channel_id=1, source_target_pairs={{0,32},{16,48},{1,33},{17,49},{2,34},{18,50},{3,35},{19,51},{4,36}... | collective-permute-start | bytes 294920 | tf_op jit(solution)/shard_map/ppermute | solution.py:164
  35.8 26.4 %collective-permute-start.17 = (f32[192,384]{1,0:T(8,128)S(1)}, f32[192,384]{1,0:T(8,128)S(1)}, u32[]{:S(2)}, u32[]{:S(2)}) collective-permute-start(f32[192,384]{1,0:T(8,128)S(1)} %copy-done.8), channel_id=1, source_target_pairs={{160,176},{176,160},{192,208},{208,192},{224,240},{240,224},{161,1... | collective-permute-start | bytes 884744 | tf_op jit(solution)/shard_map/ppermute | solution.py:176
  36.5 37.2 %collective-permute-start.25 = (f32[192,384]{1,0:T(8,128)S(1)}, f32[192,384]{1,0:T(8,128)S(1)}, u32[]{:S(2)}, u32[]{:S(2)}) collective-permute-start(f32[192,384]{1,0:T(8,128)S(1)} %copy-done.7), channel_id=1, source_target_pairs={{224,240},{240,224},{225,241},{241,225},{226,242},{242,226},{227,2... | collective-permute-start | bytes 884744 | tf_op jit(solution)/shard_map/ppermute | solution.py:176
  41.4 13.3 %collective-permute-start.8 = (f32[64,384]{1,0:T(8,128)S(1)}, f32[64,384]{1,0:T(8,128)S(1)}, u32[]{:S(2)}, u32[]{:S(2)}) collective-permute-start(f32[64,384]{1,0:T(8,128)S(1)} %convolution_subtract_fusion.6), channel_id=1, source_target_pairs={{32,96},{48,112},{0,128},{16,144},{33,97},{49,113},{1,129},{17,145... | collective-permute-start | bytes 294920 | tf_op jit(solution)/shard_map/ppermute | solution.py:164
  47.4 2.9 %collective-permute-start.10 = (f32[192,384]{1,0:T(8,128)S(1)}, f32[192,384]{1,0:T(8,128)S(1)}, u32[]{:S(2)}, u32[]{:S(2)}) collective-permute-start(f32[192,384]{1,0:T(8,128)S(1)} %collective-permute-done.9), channel_id=1, source_target_pairs={{96,97},{97,96},{98,99},{99,98},{100,101},{101,100},{102,103},{103... | collective-permute-start | bytes 884744 | tf_op jit(solution)/shard_map/ppermute | solution.py:182
  48.6 7.2 %collective-permute-start.7 = (f32[64,384]{1,0:T(8,128)S(1)}, f32[64,384]{1,0:T(8,128)S(1)}, u32[]{:S(2)}, u32[]{:S(2)}) collective-permute-start(f32[64,384]{1,0:T(8,128)S(1)} %convolution_subtract_fusion.6), channel_id=1, source_target_pairs={{0,96},{16,112},{1,97},{17,113},{2,98},{18,114},{3,99},{19,115},{4... | collective-permute-start | bytes 294920 | tf_op jit(solution)/shard_map/ppermute | solution.py:164
  50.3 10.8 %collective-permute-start.13 = (f32[64,384]{1,0:T(8,128)S(1)}, f32[64,384]{1,0:T(8,128)S(1)}, u32[]{:S(2)}, u32[]{:S(2)}) collective-permute-start(f32[64,384]{1,0:T(8,128)S(1)} %sub.110), channel_id=1, source_target_pairs={{64,128},{80,144},{32,160},{48,176},{0,192},{16,208},{65,129},{81,... | collective-permute-start | bytes 294920 | tf_op jit(solution)/shard_map/ppermute | solution.py:164
  54.6 8.9 %collective-permute-start.12 = (f32[64,384]{1,0:T(8,128)S(1)}, f32[64,384]{1,0:T(8,128)S(1)}, u32[]{:S(2)}, u32[]{:S(2)}) collective-permute-start(f32[64,384]{1,0:T(8,128)S(1)} %sub.110), channel_id=1, source_target_pairs={{32,128},{48,144},{33,129},{49,145},{34,130},{50,146},{35,131},{51... | collective-permute-start | bytes 294920 | tf_op jit(solution)/shard_map/ppermute | solution.py:164
  55.8 4.2 %collective-permute-start.11 = (f32[64,384]{1,0:T(8,128)S(1)}, f32[64,384]{1,0:T(8,128)S(1)}, u32[]{:S(2)}, u32[]{:S(2)}) collective-permute-start(f32[64,384]{1,0:T(8,128)S(1)} %sub.110), channel_id=1, source_target_pairs={{64,96},{80,112},{0,160},{16,176},{65,97},{81,113},{1,161},{17,177... | collective-permute-start | bytes 294920 | tf_op jit(solution)/shard_map/ppermute | solution.py:164
  60.4 9.9 %collective-permute-start.16 = (f32[64,384]{1,0:T(8,128)S(1)}, f32[64,384]{1,0:T(8,128)S(1)}, u32[]{:S(2)}, u32[]{:S(2)}) collective-permute-start(f32[64,384]{1,0:T(8,128)S(1)} %sub.115), channel_id=1, source_target_pairs={{96,160},{112,176},{64,192},{80,208},{32,224},{48,240},{97,161},{1... | collective-permute-start | bytes 294920 | tf_op jit(solution)/shard_map/ppermute | solution.py:164
  61.1 10.4 %collective-permute-start.15 = (f32[64,384]{1,0:T(8,128)S(1)}, f32[64,384]{1,0:T(8,128)S(1)}, u32[]{:S(2)}, u32[]{:S(2)}) collective-permute-start(f32[64,384]{1,0:T(8,128)S(1)} %sub.115), channel_id=1, source_target_pairs={{64,160},{80,176},{65,161},{81,177},{66,162},{82,178},{67,163},{83... | collective-permute-start | bytes 294920 | tf_op jit(solution)/shard_map/ppermute | solution.py:164
  62.2 4.8 %collective-permute-start.14 = (f32[64,384]{1,0:T(8,128)S(1)}, f32[64,384]{1,0:T(8,128)S(1)}, u32[]{:S(2)}, u32[]{:S(2)}) collective-permute-start(f32[64,384]{1,0:T(8,128)S(1)} %sub.115), channel_id=1, source_target_pairs={{96,128},{112,144},{32,192},{48,208},{0,224},{16,240},{97,129},{11... | collective-permute-start | bytes 294920 | tf_op jit(solution)/shard_map/ppermute | solution.py:164
  63.5 4.6 %collective-permute-start.18 = (f32[192,384]{1,0:T(8,128)S(1)}, f32[192,384]{1,0:T(8,128)S(1)}, u32[]{:S(2)}, u32[]{:S(2)}) collective-permute-start(f32[192,384]{1,0:T(8,128)S(1)} %collective-permute-done.17), channel_id=1, source_target_pairs={{160,161},{161,160},{162,163},{163,162},{164,165},{165,164},{166,1... | collective-permute-start | bytes 884744 | tf_op jit(solution)/shard_map/ppermute | solution.py:182
  67.4 7.0 %collective-permute-start.21 = (f32[64,384]{1,0:T(8,128)S(1)}, f32[64,384]{1,0:T(8,128)S(1)}, u32[]{:S(2)}, u32[]{:S(2)}) collective-permute-start(f32[64,384]{1,0:T(8,128)S(1)} %sub.119), channel_id=1, source_target_pairs={{128,192},{144,208},{96,224},{112,240},{129,193},{145,209},{97,225... | collective-permute-start | bytes 294920 | tf_op jit(solution)/shard_map/ppermute | solution.py:164
  68.1 7.4 %collective-permute-start.20 = (f32[64,384]{1,0:T(8,128)S(1)}, f32[64,384]{1,0:T(8,128)S(1)}, u32[]{:S(2)}, u32[]{:S(2)}) collective-permute-start(f32[64,384]{1,0:T(8,128)S(1)} %sub.119), channel_id=1, source_target_pairs={{96,192},{112,208},{97,193},{113,209},{98,194},{114,210},{99,195},... | collective-permute-start | bytes 294920 | tf_op jit(solution)/shard_map/ppermute | solution.py:164
  72.4 6.2 %collective-permute-start.24 = (f32[64,384]{1,0:T(8,128)S(1)}, f32[64,384]{1,0:T(8,128)S(1)}, u32[]{:S(2)}, u32[]{:S(2)}) collective-permute-start(f32[64,384]{1,0:T(8,128)S(1)} %sub.123), channel_id=1, source_target_pairs={{160,224},{176,240},{161,225},{177,241},{162,226},{178,242},{163,2... | collective-permute-start | bytes 294920 | tf_op jit(solution)/shard_map/ppermute | solution.py:164
  73.1 6.0 %collective-permute-start.23 = (f32[64,384]{1,0:T(8,128)S(1)}, f32[64,384]{1,0:T(8,128)S(1)}, u32[]{:S(2)}, u32[]{:S(2)}) collective-permute-start(f32[64,384]{1,0:T(8,128)S(1)} %sub.123), channel_id=1, source_target_pairs={{128,224},{144,240},{129,225},{145,241},{130,226},{146,242},{131,2... | collective-permute-start | bytes 294920 | tf_op jit(solution)/shard_map/ppermute | solution.py:164
  74.4 2.7 %collective-permute-start.26 = (f32[192,384]{1,0:T(8,128)S(1)}, f32[192,384]{1,0:T(8,128)S(1)}, u32[]{:S(2)}, u32[]{:S(2)}) collective-permute-start(f32[192,384]{1,0:T(8,128)S(1)} %collective-permute-done.25), channel_id=1, source_target_pairs={{224,225},{225,224},{226,227},{227,226},{228,229},{229,228},{230,2... | collective-permute-start | bytes 884744 | tf_op jit(solution)/shard_map/ppermute | solution.py:182
  76.5 3.0 %collective-permute-start.27 = (f32[64,384]{1,0:T(8,128)S(1)}, f32[64,384]{1,0:T(8,128)S(1)}, u32[]{:S(2)}, u32[]{:S(2)}) collective-permute-start(f32[64,384]{1,0:T(8,128)S(1)} %sub.126), channel_id=1, source_target_pairs={{192,224},{208,240},{193,225},{209,241},{194,226},{210,242},{195,2... | collective-permute-start | bytes 294920 | tf_op jit(solution)/shard_map/ppermute | solution.py:164
  79.9 6.8 %collective-permute-start.30 = (f32[64,384]{1,0:T(8,128)S(1)}, f32[64,384]{1,0:T(8,128)S(1)}, u32[]{:S(2)}, u32[]{:S(2)}) collective-permute-start(f32[64,384]{1,0:T(8,128)S(1)} %sub.129), channel_id=1, source_target_pairs={{0,0},{1,16},{2,2},{3,18},{4,4},{5,20},{6,6},{7,22},{8,1},{9,17},{... | collective-permute-start | bytes 294920 | tf_op jit(solution)/shard_map/ppermute | solution.py:230
  80.6 7.7 %collective-permute-start.31 = (f32[64,384]{1,0:T(8,128)S(1)}, f32[64,384]{1,0:T(8,128)S(1)}, u32[]{:S(2)}, u32[]{:S(2)}) collective-permute-start(f32[64,384]{1,0:T(8,128)S(1)} %sub.129), channel_id=1, source_target_pairs={{0,8},{1,24},{2,10},{3,26},{4,12},{5,28},{6,14},{7,30},{8,9},{9,25... | collective-permute-start | bytes 294920 | tf_op jit(solution)/shard_map/ppermute | solution.py:230
  86.6 10.7 %collective-permute-start.28 = (f32[64,384]{1,0:T(8,128)S(1)}, f32[64,384]{1,0:T(8,128)S(1)}, u32[]{:S(2)}, u32[]{:S(2)}) collective-permute-start(f32[64,384]{1,0:T(8,128)S(1)} %sub.129), channel_id=1, source_target_pairs={{0,16},{16,0},{32,48},{48,32},{64,80},{80,64},{96,112},{112,96},{1... | collective-permute-start | bytes 294920 | tf_op jit(solution)/shard_map/ppermute | solution.py:232
  89.3 16.1 %all-to-all-start = ((f32[4,128,384]{2,1,0:T(8,128)}), f32[4,128,384]{2,1,0:T(8,128)S(1)}, u32[]{:S(2)}, u32[]{:S(2)}) async-start(f32[4,128,384]{2,1,0:T(8,128)} %broadcast_in_dim.7), calls=%async_computation | async-start | bytes 1572864 | tf_op jit(solution)/shard_map/all_to_all | solution.py:237
  94.1 6.5 %collective-permute-start.29 = (f32[32,128]{1,0:T(8,128)S(1)}, f32[32,128]{1,0:T(8,128)S(1)}, u32[]{:S(2)}, u32[]{:S(2)}) collective-permute-start(f32[32,128]{1,0:T(8,128)S(1)} %broadcast_select_fusion.18), channel_id=1, source_target_pairs={{0,0},{1,16},{2,32},{3,48},{4,64},{5,80},{6,96},{7,112},{8,128},{9... | collective-permute-start | bytes 49160 | tf_op jit(solution)/shard_map/ppermute | solution.py:239
  97.4 4.0 %collective-permute-start.32 = (f32[128,384]{1,0:T(8,128)S(1)}, f32[128,384]{1,0:T(8,128)S(1)}, u32[]{:S(2)}, u32[]{:S(2)}) collective-permute-start(f32[128,384]{1,0:T(8,128)S(1)} %maximum_select_fusion.1), channel_id=1, source_target_pairs={{0,1},{1,0},{2,3},{3,2},{4,5},{5,4},{6,7},{7,6},{8,9},{9,8},{10,11... | collective-permute-start | bytes 589832 | tf_op jit(solution)/shard_map/ppermute | solution.py:234
  109.1 45.0 %all-to-all-start.1 = ((f32[8,128,128]{2,1,0:T(8,128)}), f32[8,128,128]{2,1,0:T(8,128)S(1)}, u32[]{:S(2)}, u32[]{:S(2)}) async-start(f32[8,128,128]{2,1,0:T(8,128)} %bitcast.6), calls=%async_computation.1 | async-start | bytes 1048576 | tf_op jit(solution)/shard_map/all_to_all | solution.py:246
  (15 other events, 90.7 us)

commit v8 on v7

--- a/solution.py
+++ b/solution.py
@@ -68,7 +68,7 @@
 
 def own_kernel(place_ref, own_ref, out_ref, l_ref, d_ref):
     height = own_ref.shape[0]
-    even = place_ref[1] == 0
+    even = place_ref[0] % 2 == 0
     left, right = own_ref[:, 0:height], own_ref[:, height:]
     l_ref[...] = jnp.where(even, left, right)
     invert_into(l_ref, d_ref)
@@ -84,7 +84,7 @@
         grid_spec=pltpu.PrefetchScalarGridSpec(
             num_scalar_prefetch=1,
             grid=(1,),
-            in_specs=[pl.BlockSpec((height, 2 * height), lambda _, place: (0, place[0]))],
+            in_specs=[pl.BlockSpec((height, 2 * height), lambda _, place: (0, place[0] // 2))],
             out_specs=pl.BlockSpec((height, 2 * height), lambda _, place: (0, 0)),
             scratch_shapes=[square, square],
         ),
@@ -94,7 +94,7 @@
 
 def join_kernel(place_ref, own_ref, other_ref, cross_ref, mine_ref, yours_ref, x_ref, d_ref):
     height = own_ref.shape[0]
-    even = place_ref[1] == 0
+    even = place_ref[0] % 2 == 0
     own, other = own_ref[...], other_ref[...]
     upper = jnp.where(even, own[:, 0:height], other[:, 0:height])
     lower = jnp.where(even, other, own)
@@ -141,7 +141,7 @@
     layers = chain // 2
     layer, side = position // 2, position % 2
     odd = layer % 2
-    place = jnp.stack([layer, side]).astype(jnp.int32)
+    place = jnp.full((1,), position, jnp.int32)
     pair_all = [(p, p ^ 1) for p in range(chain)]
     scaling = 1.0 / lengthscales
     scaled_candidates = candidate_inputs * scaling[:, None]
@@ -172,22 +172,24 @@
         left = jnp.where(odd == 1, chunks[max(2 * s - 1, 0)], chunks[2 * s])
         right = jnp.where(odd == 1, chunks[2 * s], chunks[2 * s + 1])
         sent = jnp.where(core == 0, left, right)
-        sent = after(sent, solved) if s > 1 else sent
+        sent = after(sent, solved) if s else sent
         got = lax.ppermute(sent, "chain", [(p, p ^ 1) for p in range(chain) if p // 2 >= 2 * s + 1])
         return left, right, got
 
-    def settle(s, left, right, got):
+    def share(s, got):
         users = [p for p in range(chain) if p // 2 >= 2 * s + 1]
         twins = [(p * cand + c, p * cand + (c ^ 1)) for p in users for c in range(cand)]
         twin = lax.ppermute(got, ("chain", "cand"), twins)
-        yours = jnp.concatenate(
-            [jnp.where(core == 0, got, twin), jnp.where(core == 0, twin, got)], axis=1
-        )
+        return jnp.where(core == 0, got, twin), jnp.where(core == 0, twin, got)
+
+    def settle(left, right, yours_left, yours_right):
+        yours = jnp.concatenate([yours_left, yours_right], axis=1)
         slab = quick(for_mine, jnp.concatenate([left, right], axis=1)) + quick(for_yours, yours)
         return after(slab[:, :span]), after(slab[:, span:])
 
     parts = [send(s) for s in range(layers // 2)]
-    slabs = [settle(0, *parts[0])]
+    slabs = [settle(*parts[s][:2], *share(s, parts[s][2])) for s in range(2)]
+    shared_parts = {}
 
     far = mid = before = None
     for t in range(layers - 1):
@@ -211,9 +213,10 @@
             solved = after(solved - quick(far, left, 1))
         solved = solved - quick(near, right, 1)
         far, mid, before = ahead, (behind if len(behind) else None), right
-        if t in (0, 2, 4):
-            s = t // 2 + 1
-            slabs.append(settle(s, *parts[s][:2], after(parts[s][2], solved)))
+        if t in (1, 2):
+            shared_parts[t + 1] = share(t + 1, after(parts[t + 1][2], solved))
+        if t in (2, 3):
+            slabs.append(settle(*parts[t][:2], *(after(part, solved) for part in shared_parts[t])))
         if t == 3:
             wanted = jnp.where(unset(solved) == 0, candidate_inputs, 0.0)
     turns = [

time: 156 us -> 161 us (1.032)
  starting transfers between devices: 83.9 us -> 90.4 us
    ppermute x18, starting transfers between devices: 35.2 us -> 41.9 us  [hop(): lax.ppermute(value, 'chain', [(2 * a + i, 2 * b + i) for a, b in pairs fo...]
where the time goes in v8:
time: 161 us; the launch traced here: 160 us
  starting transfers between devices  90.4 us (56%)
  waiting for transfers between devices  29.9 us (19%)
  matrix products  13.9 us (9%)
  other arithmetic  9.44 us (6%)
  Pallas kernels  7.59 us (5%)
  local copies, waits for them, and re-layouts  4.81 us (3%)
  between operations  4.03 us (3%)
    ppermute x18, starting transfers between devices, hop(): lax.ppermute(value, 'chain', [(2 * a + i, 2 * b + i) for a, b in pairs fo...  41.9 us
    all_to_all x1, starting transfers between devices, shards(): lax.all_to_all(shares, 'chain', 0, 0, axis_index_groups=same_side, tiled=...  26.2 us
    all_to_all x1, waiting for transfers between devices, shards(): lax.all_to_all(shares, 'chain', 0, 0, axis_index_groups=same_side, tiled=...  17.4 us
    dot_general x28, matrix products, quick(): lax.dot_general(a, b, (((1,), (contract,)), ((), ())), precision=lax.Prec...  13.9 us
    ppermute x2, starting transfers between devices, shards(): turned = [lax.ppermute(solved, ('chain', 'cand'), turn) for turn in turns]  5.96 us
    all_to_all x1, starting transfers between devices, shards(): lax.all_to_all(copies, 'cand', 0, 0, axis_index_groups=same_row, tiled=True)  4.44 us
    pallas_call x1, Pallas kernels, own_inverse(): pl.pallas_call(own_kernel, grid_spec=pltpu.PrefetchScalarGridSpec(num_sca...  4.32 us
    all_to_all x1, waiting for transfers between devices, shards(): lax.all_to_all(copies, 'cand', 0, 0, axis_index_groups=same_row, tiled=True)  4.29 us
  transfers between devices with their start and end apart: 36, of which 7 were waited for; matrix products, arithmetic and copies ran while one was open for 15% of the time, Pallas kernels for 5%

profile of v8, /device:TPU:2, one launch (start us, length us, event | category | flops | bytes accessed | tf_op | source)
XLA Modules:
  0.0 160.1 jit_solution(9945447151392330083)
XLA Ops:
  0.6 1.7 %collective-permute-start.1 = (f32[32,192]{1,0:T(8,128)}, f32[32,192]{1,0:T(8,128)}, u32[]{:S(2)}, u32[]{:S(2)}) collective-permute-start(f32[32,192]{1,0:T(8,128)} %param.4), channel_id=1, source_target_pairs={{0,16},{16,0},{32,48},{48,32},{64,80},{80,64},{96,112},{112,96},{1... | collective-permute-start | bytes 73736 | tf_op jit(solution)/shard_map/ppermute | solution.py:155
  2.3 4.3 %shard_map.59.own_ref = f32[192,384]{1,0:T(8,128)} custom-call(s32[1]{0:T(128)} %bitcast.place_ref, f32[192,3072]{1,0:T(8,128)} %own_ref.1), custom_call_target="tpu_custom_call" | custom-call | tf_op jit(solution)/shard_map/pallas_call | solution.py:82
  7.1 1.0 broadcast_select_fusion.17
  8.1 1.4 collective-permute-start.3
  9.9 1.2 broadcast_select_fusion.8
  11.1 0.7 broadcast_multiply_fusion.1
  12.0 0.9 fusion.34
  14.0 0.7 exponential_multiply_fusion.cross_ref
  14.7 0.7 collective-permute-done.other_ref
  15.4 3.3 %shard_map.60 = (f32[384,192]{1,0:T(8,128)}, f32[384,192]{1,0:T(8,128)}, f32[64,384]{1,0:T(8,128)}) custom-call(s32[1]{0:T(128)} %bitcast.place_ref, f32[192,384]{1,0:T(8,128)} %shard_map.59.own_ref, f32[192,384]{1,0:T(8,128)} %collective-permute-done.other_ref, f32[64,384]{1,0:T(8,128)} %exponential_multiply_fusion.cross_ref), custom_call_target="tpu_custom_call" | custom-call | tf_op jit(solution)/shard_map/pallas_call | solution.py:114
  18.7 14.6 %collective-permute-start.5 = (f32[64,384]{1,0:T(8,128)}, f32[64,384]{1,0:T(8,128)S(1)}, u32[]{:S(2)}, u32[]{:S(2)}) collective-permute-start(f32[64,384]{1,0:T(8,128)} %get-tuple-element.16), channel_id=1, source_target_pairs={{0,64},{16,80},{1,65},{17,81},{2,66},{18,82},{3,67},{19,83},{4,68}... | collective-permute-start | bytes 294920 | tf_op jit(solution)/shard_map/ppermute | solution.py:164
  33.3 1.3 collective-permute-start.2
  36.7 1.0 broadcast_select_fusion.16
  39.7 0.8 copy-done.10
  40.9 5.6 %collective-permute-start.8 = (f32[64,384]{1,0:T(8,128)S(1)}, f32[64,384]{1,0:T(8,128)S(1)}, u32[]{:S(2)}, u32[]{:S(2)}) collective-permute-start(f32[64,384]{1,0:T(8,128)S(1)} %convolution_subtract_fusion.6), channel_id=1, source_target_pairs={{32,96},{48,112},{0,128},{16,144},{33,97},{49,113},{1,129},{17,145... | collective-permute-start | bytes 294920 | tf_op jit(solution)/shard_map/ppermute | solution.py:164
  48.3 2.0 %collective-permute-start.7 = (f32[64,384]{1,0:T(8,128)S(1)}, f32[64,384]{1,0:T(8,128)S(1)}, u32[]{:S(2)}, u32[]{:S(2)}) collective-permute-start(f32[64,384]{1,0:T(8,128)S(1)} %convolution_subtract_fusion.6), channel_id=1, source_target_pairs={{0,96},{16,112},{1,97},{17,113},{2,98},{18,114},{3,99},{19,115},{4... | collective-permute-start | bytes 294920 | tf_op jit(solution)/shard_map/ppermute | solution.py:164
  50.9 8.0 %collective-permute-start.13 = (f32[64,384]{1,0:T(8,128)S(1)}, f32[64,384]{1,0:T(8,128)S(1)}, u32[]{:S(2)}, u32[]{:S(2)}) collective-permute-start(f32[64,384]{1,0:T(8,128)S(1)} %sub.110), channel_id=1, source_target_pairs={{64,128},{80,144},{32,160},{48,176},{0,192},{16,208},{65,129},{81,... | collective-permute-start | bytes 294920 | tf_op jit(solution)/shard_map/ppermute | solution.py:164
  61.5 1.7 %collective-permute-start.11 = (f32[64,384]{1,0:T(8,128)S(1)}, f32[64,384]{1,0:T(8,128)S(1)}, u32[]{:S(2)}, u32[]{:S(2)}) collective-permute-start(f32[64,384]{1,0:T(8,128)S(1)} %sub.110), channel_id=1, source_target_pairs={{64,96},{80,112},{0,160},{16,176},{65,97},{81,113},{1,161},{17,177... | collective-permute-start | bytes 294920 | tf_op jit(solution)/shard_map/ppermute | solution.py:164
  64.8 1.1 collective-permute-done.11
  68.2 1.3 collective-permute-start.14
  70.0 0.9 collective-permute-start.26
  70.8 2.6 %collective-permute-done.14 = f32[64,384]{1,0:T(8,128)S(1)} collective-permute-done((f32[64,384]{1,0:T(8,128)S(1)}, f32[64,384]{1,0:T(8,128)S(1)}, u32[]{:S(2)}, u32[]{:S(2)}) %collective-permute-start.14) | collective-permute-done | bytes 98336 | tf_op jit(solution)/shard_map/ppermute | solution.py:164
  86.3 5.3 %collective-permute-start.31 = (f32[64,384]{1,0:T(8,128)S(1)}, f32[64,384]{1,0:T(8,128)S(1)}, u32[]{:S(2)}, u32[]{:S(2)}) collective-permute-start(f32[64,384]{1,0:T(8,128)S(1)} %sub.129), channel_id=1, source_target_pairs={{0,8},{1,24},{2,10},{3,26},{4,12},{5,28},{6,14},{7,30},{8,9},{9,25... | collective-permute-start | bytes 294920 | tf_op jit(solution)/shard_map/ppermute | solution.py:233
  94.2 1.0 broadcast_in_dim.10
  95.2 4.4 %all-to-all-start = ((f32[4,128,384]{2,1,0:T(8,128)}), f32[4,128,384]{2,1,0:T(8,128)S(1)}, u32[]{:S(2)}, u32[]{:S(2)}) async-start(f32[4,128,384]{2,1,0:T(8,128)} %broadcast_in_dim.10), calls=%async_computation | async-start | bytes 1572864 | tf_op jit(solution)/shard_map/all_to_all | solution.py:240
  99.6 2.8 %collective-permute-start.29 = (f32[32,128]{1,0:T(8,128)S(1)}, f32[32,128]{1,0:T(8,128)S(1)}, u32[]{:S(2)}, u32[]{:S(2)}) collective-permute-start(f32[32,128]{1,0:T(8,128)S(1)} %broadcast_select_fusion.18), channel_id=1, source_target_pairs={{0,0},{1,16},{2,32},{3,48},{4,64},{5,80},{6,96},{7,112},{8,128},{9... | collective-permute-start | bytes 49160 | tf_op jit(solution)/shard_map/ppermute | solution.py:242
  103.0 3.2 %collective-permute-done.29 = f32[32,128]{1,0:T(8,128)S(1)} collective-permute-done((f32[32,128]{1,0:T(8,128)S(1)}, f32[32,128]{1,0:T(8,128)S(1)}, u32[]{:S(2)}, u32[]{:S(2)}) %collective-permute-start.29) | collective-permute-done | bytes 16416 | tf_op jit(solution)/shard_map/ppermute | solution.py:242
  106.9 4.3 %all-to-all-done = f32[4,128,384]{2,1,0:T(8,128)S(1)} async-done(((f32[4,128,384]{2,1,0:T(8,128)}), f32[4,128,384]{2,1,0:T(8,128)S(1)}, u32[]{:S(2)}, u32[]{:S(2)}) %all-to-all-start) | async-done | bytes 786464 | tf_op jit(solution)/shard_map/all_to_all | solution.py:240
  114.2 0.8 maximum_select_fusion
  115.0 26.2 %all-to-all-start.1 = ((f32[8,128,128]{2,1,0:T(8,128)}), f32[8,128,128]{2,1,0:T(8,128)S(1)}, u32[]{:S(2)}, u32[]{:S(2)}) async-start(f32[8,128,128]{2,1,0:T(8,128)} %bitcast.5), calls=%async_computation.1 | async-start | bytes 1048576 | tf_op jit(solution)/shard_map/all_to_all | solution.py:249
  141.3 0.7 copy.7
  142.1 17.4 %all-to-all-done.1 = f32[8,128,128]{2,1,0:T(8,128)S(1)} async-done(((f32[8,128,128]{2,1,0:T(8,128)}), f32[8,128,128]{2,1,0:T(8,128)S(1)}, u32[]{:S(2)}, u32[]{:S(2)}) %all-to-all-start.1) | async-done | bytes 524320 | tf_op jit(solution)/shard_map/all_to_all | solution.py:249
  (138 shorter events, 33.1 us)
Async XLA Ops:
  0.6 11.3 %collective-permute-start.1 = (f32[32,192]{1,0:T(8,128)}, f32[32,192]{1,0:T(8,128)}, u32[]{:S(2)}, u32[]{:S(2)}) collective-permute-start(f32[32,192]{1,0:T(8,128)} %param.4), channel_id=1, source_target_pairs={{0,16},{16,0},{32,48},{48,32},{64,80},{80,64},{96,112},{112,96},{1... | collective-permute-start | bytes 73736 | tf_op jit(solution)/shard_map/ppermute | solution.py:155
  6.6 8.8 %collective-permute-start = (f32[192,384]{1,0:T(8,128)}, f32[192,384]{1,0:T(8,128)}, u32[]{:S(2)}, u32[]{:S(2)}) collective-permute-start(f32[192,384]{1,0:T(8,128)} %shard_map.59.own_ref), channel_id=1, source_target_pairs={{0,16},{16,0},{32,48},{48,32},{64,80},{80,64},{96,112},{112,96},{1... | collective-permute-start | bytes 884744 | tf_op jit(solution)/shard_map/ppermute | solution.py:157
  8.1 4.8 %collective-permute-start.3 = (f32[192,384]{1,0:T(8,128)}, f32[192,384]{1,0:T(8,128)}, u32[]{:S(2)}, u32[]{:S(2)}) collective-permute-start(f32[192,384]{1,0:T(8,128)} %get-tuple-element.43), channel_id=1, source_target_pairs={{32,48},{48,32},{64,80},{80,64},{96,112},{112,96},{128,144},{144,1... | collective-permute-start | bytes 884744 | tf_op jit(solution)/shard_map/ppermute | solution.py:176
  12.9 23.1 %collective-permute-start.4 = (f32[192,384]{1,0:T(8,128)}, f32[192,384]{1,0:T(8,128)S(1)}, u32[]{:S(2)}, u32[]{:S(2)}) collective-permute-start(f32[192,384]{1,0:T(8,128)} %collective-permute-done.3), channel_id=1, source_target_pairs={{32,33},{33,32},{34,35},{35,34},{36,37},{37,36},{38,39},{39,38},{4... | collective-permute-start | bytes 884744 | tf_op jit(solution)/shard_map/ppermute | solution.py:182
  18.7 27.8 %collective-permute-start.5 = (f32[64,384]{1,0:T(8,128)}, f32[64,384]{1,0:T(8,128)S(1)}, u32[]{:S(2)}, u32[]{:S(2)}) collective-permute-start(f32[64,384]{1,0:T(8,128)} %get-tuple-element.16), channel_id=1, source_target_pairs={{0,64},{16,80},{1,65},{17,81},{2,66},{18,82},{3,67},{19,83},{4,68}... | collective-permute-start | bytes 294920 | tf_op jit(solution)/shard_map/ppermute | solution.py:164
  33.3 6.3 %collective-permute-start.2 = (f32[64,384]{1,0:T(8,128)}, f32[64,384]{1,0:T(8,128)S(1)}, u32[]{:S(2)}, u32[]{:S(2)}) collective-permute-start(f32[64,384]{1,0:T(8,128)} %get-tuple-element.16), channel_id=1, source_target_pairs={{0,32},{16,48},{1,33},{17,49},{2,34},{18,50},{3,35},{19,51},{4,36}... | collective-permute-start | bytes 294920 | tf_op jit(solution)/shard_map/ppermute | solution.py:164
  34.6 16.2 %collective-permute-start.17 = (f32[192,384]{1,0:T(8,128)S(1)}, f32[192,384]{1,0:T(8,128)S(1)}, u32[]{:S(2)}, u32[]{:S(2)}) collective-permute-start(f32[192,384]{1,0:T(8,128)S(1)} %copy-done.8), channel_id=1, source_target_pairs={{160,176},{176,160},{192,208},{208,192},{224,240},{240,224},{161,1... | collective-permute-start | bytes 884744 | tf_op jit(solution)/shard_map/ppermute | solution.py:176
  35.3 11.9 %collective-permute-start.9 = (f32[192,384]{1,0:T(8,128)S(1)}, f32[192,384]{1,0:T(8,128)S(1)}, u32[]{:S(2)}, u32[]{:S(2)}) collective-permute-start(f32[192,384]{1,0:T(8,128)S(1)} %copy-done.9), channel_id=1, source_target_pairs={{96,112},{112,96},{128,144},{144,128},{160,176},{176,160},{192,208... | collective-permute-start | bytes 884744 | tf_op jit(solution)/shard_map/ppermute | solution.py:176
  36.0 33.9 %collective-permute-start.25 = (f32[192,384]{1,0:T(8,128)S(1)}, f32[192,384]{1,0:T(8,128)S(1)}, u32[]{:S(2)}, u32[]{:S(2)}) collective-permute-start(f32[192,384]{1,0:T(8,128)S(1)} %copy-done.7), channel_id=1, source_target_pairs={{224,240},{240,224},{225,241},{241,225},{226,242},{242,226},{227,2... | collective-permute-start | bytes 884744 | tf_op jit(solution)/shard_map/ppermute | solution.py:176
  40.9 20.7 %collective-permute-start.8 = (f32[64,384]{1,0:T(8,128)S(1)}, f32[64,384]{1,0:T(8,128)S(1)}, u32[]{:S(2)}, u32[]{:S(2)}) collective-permute-start(f32[64,384]{1,0:T(8,128)S(1)} %convolution_subtract_fusion.6), channel_id=1, source_target_pairs={{32,96},{48,112},{0,128},{16,144},{33,97},{49,113},{1,129},{17,145... | collective-permute-start | bytes 294920 | tf_op jit(solution)/shard_map/ppermute | solution.py:164
  47.2 11.6 %collective-permute-start.10 = (f32[192,384]{1,0:T(8,128)S(1)}, f32[192,384]{1,0:T(8,128)S(1)}, u32[]{:S(2)}, u32[]{:S(2)}) collective-permute-start(f32[192,384]{1,0:T(8,128)S(1)} %collective-permute-done.9), channel_id=1, source_target_pairs={{96,97},{97,96},{98,99},{99,98},{100,101},{101,100},{102,103},{103... | collective-permute-start | bytes 884744 | tf_op jit(solution)/shard_map/ppermute | solution.py:182
  48.3 15.4 %collective-permute-start.7 = (f32[64,384]{1,0:T(8,128)S(1)}, f32[64,384]{1,0:T(8,128)S(1)}, u32[]{:S(2)}, u32[]{:S(2)}) collective-permute-start(f32[64,384]{1,0:T(8,128)S(1)} %convolution_subtract_fusion.6), channel_id=1, source_target_pairs={{0,96},{16,112},{1,97},{17,113},{2,98},{18,114},{3,99},{19,115},{4... | collective-permute-start | bytes 294920 | tf_op jit(solution)/shard_map/ppermute | solution.py:164
  50.9 16.2 %collective-permute-start.13 = (f32[64,384]{1,0:T(8,128)S(1)}, f32[64,384]{1,0:T(8,128)S(1)}, u32[]{:S(2)}, u32[]{:S(2)}) collective-permute-start(f32[64,384]{1,0:T(8,128)S(1)} %sub.110), channel_id=1, source_target_pairs={{64,128},{80,144},{32,160},{48,176},{0,192},{16,208},{65,129},{81,... | collective-permute-start | bytes 294920 | tf_op jit(solution)/shard_map/ppermute | solution.py:164
  58.8 9.4 %collective-permute-start.12 = (f32[64,384]{1,0:T(8,128)S(1)}, f32[64,384]{1,0:T(8,128)S(1)}, u32[]{:S(2)}, u32[]{:S(2)}) collective-permute-start(f32[64,384]{1,0:T(8,128)S(1)} %sub.110), channel_id=1, source_target_pairs={{32,128},{48,144},{33,129},{49,145},{34,130},{50,146},{35,131},{51... | collective-permute-start | bytes 294920 | tf_op jit(solution)/shard_map/ppermute | solution.py:164
  61.5 4.4 %collective-permute-start.11 = (f32[64,384]{1,0:T(8,128)S(1)}, f32[64,384]{1,0:T(8,128)S(1)}, u32[]{:S(2)}, u32[]{:S(2)}) collective-permute-start(f32[64,384]{1,0:T(8,128)S(1)} %sub.110), channel_id=1, source_target_pairs={{64,96},{80,112},{0,160},{16,176},{65,97},{81,113},{1,161},{17,177... | collective-permute-start | bytes 294920 | tf_op jit(solution)/shard_map/ppermute | solution.py:164
  63.7 10.8 %collective-permute-start.18 = (f32[192,384]{1,0:T(8,128)S(1)}, f32[192,384]{1,0:T(8,128)S(1)}, u32[]{:S(2)}, u32[]{:S(2)}) collective-permute-start(f32[192,384]{1,0:T(8,128)S(1)} %collective-permute-done.17), channel_id=1, source_target_pairs={{160,161},{161,160},{162,163},{163,162},{164,165},{165,164},{166,1... | collective-permute-start | bytes 884744 | tf_op jit(solution)/shard_map/ppermute | solution.py:182
  66.4 10.4 %collective-permute-start.16 = (f32[64,384]{1,0:T(8,128)S(1)}, f32[64,384]{1,0:T(8,128)S(1)}, u32[]{:S(2)}, u32[]{:S(2)}) collective-permute-start(f32[64,384]{1,0:T(8,128)S(1)} %sub.115), channel_id=1, source_target_pairs={{96,160},{112,176},{64,192},{80,208},{32,224},{48,240},{97,161},{1... | collective-permute-start | bytes 294920 | tf_op jit(solution)/shard_map/ppermute | solution.py:164
  67.1 10.8 %collective-permute-start.15 = (f32[64,384]{1,0:T(8,128)S(1)}, f32[64,384]{1,0:T(8,128)S(1)}, u32[]{:S(2)}, u32[]{:S(2)}) collective-permute-start(f32[64,384]{1,0:T(8,128)S(1)} %sub.115), channel_id=1, source_target_pairs={{64,160},{80,176},{65,161},{81,177},{66,162},{82,178},{67,163},{83... | collective-permute-start | bytes 294920 | tf_op jit(solution)/shard_map/ppermute | solution.py:164
  68.2 5.2 %collective-permute-start.14 = (f32[64,384]{1,0:T(8,128)S(1)}, f32[64,384]{1,0:T(8,128)S(1)}, u32[]{:S(2)}, u32[]{:S(2)}) collective-permute-start(f32[64,384]{1,0:T(8,128)S(1)} %sub.115), channel_id=1, source_target_pairs={{96,128},{112,144},{32,192},{48,208},{0,224},{16,240},{97,129},{11... | collective-permute-start | bytes 294920 | tf_op jit(solution)/shard_map/ppermute | solution.py:164
  70.0 11.8 %collective-permute-start.26 = (f32[192,384]{1,0:T(8,128)S(1)}, f32[192,384]{1,0:T(8,128)S(1)}, u32[]{:S(2)}, u32[]{:S(2)}) collective-permute-start(f32[192,384]{1,0:T(8,128)S(1)} %collective-permute-done.25), channel_id=1, source_target_pairs={{224,225},{225,224},{226,227},{227,226},{228,229},{229,228},{230,2... | collective-permute-start | bytes 884744 | tf_op jit(solution)/shard_map/ppermute | solution.py:182
  73.9 6.3 %collective-permute-start.21 = (f32[64,384]{1,0:T(8,128)S(1)}, f32[64,384]{1,0:T(8,128)S(1)}, u32[]{:S(2)}, u32[]{:S(2)}) collective-permute-start(f32[64,384]{1,0:T(8,128)S(1)} %sub.119), channel_id=1, source_target_pairs={{128,192},{144,208},{96,224},{112,240},{129,193},{145,209},{97,225... | collective-permute-start | bytes 294920 | tf_op jit(solution)/shard_map/ppermute | solution.py:164
  74.5 6.7 %collective-permute-start.20 = (f32[64,384]{1,0:T(8,128)S(1)}, f32[64,384]{1,0:T(8,128)S(1)}, u32[]{:S(2)}, u32[]{:S(2)}) collective-permute-start(f32[64,384]{1,0:T(8,128)S(1)} %sub.119), channel_id=1, source_target_pairs={{96,192},{112,208},{97,193},{113,209},{98,194},{114,210},{99,195},... | collective-permute-start | bytes 294920 | tf_op jit(solution)/shard_map/ppermute | solution.py:164
  78.8 5.5 %collective-permute-start.24 = (f32[64,384]{1,0:T(8,128)S(1)}, f32[64,384]{1,0:T(8,128)S(1)}, u32[]{:S(2)}, u32[]{:S(2)}) collective-permute-start(f32[64,384]{1,0:T(8,128)S(1)} %sub.123), channel_id=1, source_target_pairs={{160,224},{176,240},{161,225},{177,241},{162,226},{178,242},{163,2... | collective-permute-start | bytes 294920 | tf_op jit(solution)/shard_map/ppermute | solution.py:164
  79.5 5.3 %collective-permute-start.23 = (f32[64,384]{1,0:T(8,128)S(1)}, f32[64,384]{1,0:T(8,128)S(1)}, u32[]{:S(2)}, u32[]{:S(2)}) collective-permute-start(f32[64,384]{1,0:T(8,128)S(1)} %sub.123), channel_id=1, source_target_pairs={{128,224},{144,240},{129,225},{145,241},{130,226},{146,242},{131,2... | collective-permute-start | bytes 294920 | tf_op jit(solution)/shard_map/ppermute | solution.py:164
  80.2 3.0 %collective-permute-start.22 = (f32[64,384]{1,0:T(8,128)S(1)}, f32[64,384]{1,0:T(8,128)S(1)}, u32[]{:S(2)}, u32[]{:S(2)}) collective-permute-start(f32[64,384]{1,0:T(8,128)S(1)} %sub.123), channel_id=1, source_target_pairs={{160,192},{176,208},{161,193},{177,209},{162,194},{178,210},{163,1... | collective-permute-start | bytes 294920 | tf_op jit(solution)/shard_map/ppermute | solution.py:164
  85.7 7.9 %collective-permute-start.30 = (f32[64,384]{1,0:T(8,128)S(1)}, f32[64,384]{1,0:T(8,128)S(1)}, u32[]{:S(2)}, u32[]{:S(2)}) collective-permute-start(f32[64,384]{1,0:T(8,128)S(1)} %sub.129), channel_id=1, source_target_pairs={{0,0},{1,16},{2,2},{3,18},{4,4},{5,20},{6,6},{7,22},{8,1},{9,17},{... | collective-permute-start | bytes 294920 | tf_op jit(solution)/shard_map/ppermute | solution.py:233
  86.3 7.8 %collective-permute-start.31 = (f32[64,384]{1,0:T(8,128)S(1)}, f32[64,384]{1,0:T(8,128)S(1)}, u32[]{:S(2)}, u32[]{:S(2)}) collective-permute-start(f32[64,384]{1,0:T(8,128)S(1)} %sub.129), channel_id=1, source_target_pairs={{0,8},{1,24},{2,10},{3,26},{4,12},{5,28},{6,14},{7,30},{8,9},{9,25... | collective-permute-start | bytes 294920 | tf_op jit(solution)/shard_map/ppermute | solution.py:233
  93.4 9.0 %collective-permute-start.28 = (f32[64,384]{1,0:T(8,128)S(1)}, f32[64,384]{1,0:T(8,128)S(1)}, u32[]{:S(2)}, u32[]{:S(2)}) collective-permute-start(f32[64,384]{1,0:T(8,128)S(1)} %sub.129), channel_id=1, source_target_pairs={{0,16},{16,0},{32,48},{48,32},{64,80},{80,64},{96,112},{112,96},{1... | collective-permute-start | bytes 294920 | tf_op jit(solution)/shard_map/ppermute | solution.py:235
  95.2 16.0 %all-to-all-start = ((f32[4,128,384]{2,1,0:T(8,128)}), f32[4,128,384]{2,1,0:T(8,128)S(1)}, u32[]{:S(2)}, u32[]{:S(2)}) async-start(f32[4,128,384]{2,1,0:T(8,128)} %broadcast_in_dim.10), calls=%async_computation | async-start | bytes 1572864 | tf_op jit(solution)/shard_map/all_to_all | solution.py:240
  99.6 6.5 %collective-permute-start.29 = (f32[32,128]{1,0:T(8,128)S(1)}, f32[32,128]{1,0:T(8,128)S(1)}, u32[]{:S(2)}, u32[]{:S(2)}) collective-permute-start(f32[32,128]{1,0:T(8,128)S(1)} %broadcast_select_fusion.18), channel_id=1, source_target_pairs={{0,0},{1,16},{2,32},{3,48},{4,64},{5,80},{6,96},{7,112},{8,128},{9... | collective-permute-start | bytes 49160 | tf_op jit(solution)/shard_map/ppermute | solution.py:242
  102.5 4.4 %collective-permute-start.32 = (f32[128,384]{1,0:T(8,128)S(1)}, f32[128,384]{1,0:T(8,128)S(1)}, u32[]{:S(2)}, u32[]{:S(2)}) collective-permute-start(f32[128,384]{1,0:T(8,128)S(1)} %maximum_select_fusion.1), channel_id=1, source_target_pairs={{0,1},{1,0},{2,3},{3,2},{4,5},{5,4},{6,7},{7,6},{8,9},{9,8},{10,11... | collective-permute-start | bytes 589832 | tf_op jit(solution)/shard_map/ppermute | solution.py:237
  115.0 44.4 %all-to-all-start.1 = ((f32[8,128,128]{2,1,0:T(8,128)}), f32[8,128,128]{2,1,0:T(8,128)S(1)}, u32[]{:S(2)}, u32[]{:S(2)}) async-start(f32[8,128,128]{2,1,0:T(8,128)} %bitcast.5), calls=%async_computation.1 | async-start | bytes 1048576 | tf_op jit(solution)/shard_map/all_to_all | solution.py:249
  (18 other events, 125.0 us)

commit v9 on v8

--- a/solution.py
+++ b/solution.py
@@ -171,25 +171,25 @@
         chunks = [(late if s else factor)[:, k * span : (k + 1) * span] for k in range(layers)]
         left = jnp.where(odd == 1, chunks[max(2 * s - 1, 0)], chunks[2 * s])
         right = jnp.where(odd == 1, chunks[2 * s], chunks[2 * s + 1])
-        sent = jnp.where(core == 0, left, right)
-        sent = after(sent, solved) if s else sent
+        mine = jnp.concatenate([left, right], axis=1)
+        sent = after(mine, solved) if s else jnp.where(core == 0, left, right)
         got = lax.ppermute(sent, "chain", [(p, p ^ 1) for p in range(chain) if p // 2 >= 2 * s + 1])
-        return left, right, got
+        return mine, got
 
     def share(s, got):
         users = [p for p in range(chain) if p // 2 >= 2 * s + 1]
         twins = [(p * cand + c, p * cand + (c ^ 1)) for p in users for c in range(cand)]
         twin = lax.ppermute(got, ("chain", "cand"), twins)
-        return jnp.where(core == 0, got, twin), jnp.where(core == 0, twin, got)
-
-    def settle(left, right, yours_left, yours_right):
-        yours = jnp.concatenate([yours_left, yours_right], axis=1)
-        slab = quick(for_mine, jnp.concatenate([left, right], axis=1)) + quick(for_yours, yours)
+        return jnp.concatenate(
+            [jnp.where(core == 0, got, twin), jnp.where(core == 0, twin, got)], axis=1
+        )
+
+    def settle(mine, yours):
+        slab = quick(for_mine, mine) + quick(for_yours, yours)
         return after(slab[:, :span]), after(slab[:, span:])
 
     parts = [send(s) for s in range(layers // 2)]
-    slabs = [settle(*parts[s][:2], *share(s, parts[s][2])) for s in range(2)]
-    shared_parts = {}
+    slabs = [settle(parts[0][0], share(0, parts[0][1])), settle(*parts[1])]
 
     far = mid = before = None
     for t in range(layers - 1):
@@ -213,10 +213,8 @@
             solved = after(solved - quick(far, left, 1))
         solved = solved - quick(near, right, 1)
         far, mid, before = ahead, (behind if len(behind) else None), right
-        if t in (1, 2):
-            shared_parts[t + 1] = share(t + 1, after(parts[t + 1][2], solved))
         if t in (2, 3):
-            slabs.append(settle(*parts[t][:2], *(after(part, solved) for part in shared_parts[t])))
+            slabs.append(settle(parts[t][0], after(parts[t][1], solved)))
         if t == 3:
             wanted = jnp.where(unset(solved) == 0, candidate_inputs, 0.0)
     turns = [
@@ -230,14 +228,20 @@
         ]
         for other in range(2)
     ]
-    turned = [lax.ppermute(solved, ("chain", "cand"), turn) for turn in turns]
+    turned = []
+    for turn in turns:
+        turned.append(lax.ppermute(solved, ("chain", "cand"), turn))
     turned = both_of(lax.axis_index("cand") // 8, *turned, 0)
-    columns_all = both(solved, lax.ppermute(solved, "chain", pair_all), 0)
+    other_columns = lax.ppermute(solved, "chain", pair_all)
+    columns_all = both(solved, other_columns, 0)
     rows = jnp.where(side == 0, columns_all[:, :height], columns_all[:, height:]).T
     twin_columns = lax.ppermute(columns_all, "cand", [(c, c ^ 1) for c in range(cand)])
-    same_row = [[8 * j + 2 * x + k for x in range(cand // 4)] for j in range(2) for k in range(2)]
-    copies = jnp.broadcast_to(turned[None], (cand // 4,) + turned.shape)
-    others = lax.all_to_all(copies, "cand", 0, 0, axis_index_groups=same_row, tiled=True)
+    row = lax.axis_index("cand") // 2 % (cand // 4)
+    others = [turned]
+    for r in range(1, cand // 4):
+        others.append(lax.ppermute(turned, "cand", [(c, c ^ (2 * r)) for c in range(cand)]))
+    others = both_of(row // 2, jnp.stack(others[:2]), jnp.stack(others[2:]), 0).reshape(2, 2, width, span)
+    others = both_of(row % 2, others[:, :1], others[:, 1:])
     swap = [(a * cand + b, b * cand + a) for a in range(chain) for b in range(cand)]
     chosen = lax.ppermute(wanted, ("chain", "cand"), swap)
     prior_cov = matern(chosen * after(scaling, solved)[:, None], scaled_candidates)

time: 161 us -> 157 us (0.975)
  starting transfers between devices: 90.4 us -> 86.2 us
    ppermute x3 -> x6, starting transfers between devices: 6.06 us -> 16.2 us  [the longest x3 11.8 us: shards(): lax.ppermute(turned, 'cand', [(c, c ^ 2 * r) for c in range(cand)])]
    all_to_all x1, starting transfers between devices: 26.2 us -> 16.7 us  [shards(): lax.all_to_all(shares, 'chain', 0, 0, axis_index_groups=same_side, tiled=...]
    ppermute x3 -> x6, waiting for transfers between devices: 0.63 us -> 9.19 us  [the longest x3 7.51 us: shards(): lax.ppermute(turned, 'cand', [(c, c ^ 2 * r) for c in range(cand)])]
    all_to_all x1 -> x0, starting transfers between devices: 4.44 us -> none  [shards(): lax.all_to_all(copies, 'cand', 0, 0, axis_index_groups=same_row, tiled=True)]
    all_to_all x1 -> x0, waiting for transfers between devices: 4.29 us -> none  [shards(): lax.all_to_all(copies, 'cand', 0, 0, axis_index_groups=same_row, tiled=True)]
    ppermute x1, waiting for transfers between devices: 3.17 us -> 0.01 us  [shards(): chosen = lax.ppermute(wanted, ('chain', 'cand'), swap)]
    ppermute x18, waiting for transfers between devices: 3.73 us -> 0.58 us  [hop(): lax.ppermute(value, 'chain', [(2 * a + i, 2 * b + i) for a, b in pairs fo...]
    ppermute x1, waiting for transfers between devices: 0.01 us -> 2.52 us  [shards(): other_archive = lax.ppermute(archive_inputs, 'chain', pair_all)]
  transfers between devices with their start and end apart: 36 -> 35, of which waited for: 7 -> 6; matrix products, arithmetic and copies ran while one was open for 15% -> 15% of each run, Pallas kernels for 5% -> 2%
where the time goes in v9:
time: 157 us; the launch traced here: 155 us
  starting transfers between devices  86.2 us (55%)
  waiting for transfers between devices  29.7 us (19%)
  matrix products  13.9 us (9%)
  other arithmetic  9.75 us (6%)
  Pallas kernels  7.57 us (5%)
  between operations  4.05 us (3%)
  local copies, waits for them, and re-layouts  3.53 us (2%)
    ppermute x18, starting transfers between devices, hop(): lax.ppermute(value, 'chain', [(2 * a + i, 2 * b + i) for a, b in pairs fo...  42 us
    all_to_all x1, waiting for transfers between devices, shards(): lax.all_to_all(shares, 'chain', 0, 0, axis_index_groups=same_side, tiled=...  17.4 us
    all_to_all x1, starting transfers between devices, shards(): lax.all_to_all(shares, 'chain', 0, 0, axis_index_groups=same_side, tiled=...  16.7 us
    dot_general x28, matrix products, quick(): lax.dot_general(a, b, (((1,), (contract,)), ((), ())), precision=lax.Prec...  13.9 us
    ppermute x3, starting transfers between devices, shards(): lax.ppermute(turned, 'cand', [(c, c ^ 2 * r) for c in range(cand)])  11.8 us
    ppermute x3, waiting for transfers between devices, shards(): lax.ppermute(turned, 'cand', [(c, c ^ 2 * r) for c in range(cand)])  7.51 us
    pallas_call x1, Pallas kernels, own_inverse(): pl.pallas_call(own_kernel, grid_spec=pltpu.PrefetchScalarGridSpec(num_sca...  4.33 us
    ppermute x2, starting transfers between devices, shards(): turned.append(lax.ppermute(solved, ('chain', 'cand'), turn))  3.56 us
  transfers between devices with their start and end apart: 35, of which 6 were waited for; matrix products, arithmetic and copies ran while one was open for 15% of the time, Pallas kernels for 2%

profile of v9, /device:TPU:2, one launch (start us, length us, event | category | flops | bytes accessed | tf_op | source)
XLA Modules:
  0.0 154.7 jit_solution(7186570133724724549)
XLA Ops:
  0.6 4.3 %shard_map.59.own_ref = f32[192,384]{1,0:T(8,128)} custom-call(s32[1]{0:T(128)} %bitcast.place_ref, f32[192,3072]{1,0:T(8,128)} %own_ref.1), custom_call_target="tpu_custom_call" | custom-call | tf_op jit(solution)/shard_map/pallas_call | solution.py:82
  5.0 1.6 %collective-permute-start = (f32[192,384]{1,0:T(8,128)}, f32[192,384]{1,0:T(8,128)}, u32[]{:S(2)}, u32[]{:S(2)}) collective-permute-start(f32[192,384]{1,0:T(8,128)} %shard_map.59.own_ref), channel_id=1, source_target_pairs={{0,16},{16,0},{32,48},{48,32},{64,80},{80,64},{96,112},{112,96},{1... | collective-permute-start | bytes 884744 | tf_op jit(solution)/shard_map/ppermute | solution.py:157
  7.0 1.0 broadcast_select_fusion.8
  8.0 1.4 collective-permute-start.3
  9.9 0.9 slice_select_fusion.3
  10.9 1.1 pad_maximum_fusion.3
  12.2 2.5 %collective-permute-done.1 = f32[32,192]{1,0:T(8,128)} collective-permute-done((f32[32,192]{1,0:T(8,128)}, f32[32,192]{1,0:T(8,128)}, u32[]{:S(2)}, u32[]{:S(2)}) %collective-permute-start.1) | collective-permute-done | bytes 24608 | tf_op jit(solution)/shard_map/ppermute | solution.py:155
  14.7 0.9 fusion.13
  17.5 3.2 %shard_map.60 = (f32[384,192]{1,0:T(8,128)}, f32[384,192]{1,0:T(8,128)}, f32[64,384]{1,0:T(8,128)}) custom-call(s32[1]{0:T(128)} %bitcast.place_ref, f32[192,384]{1,0:T(8,128)} %shard_map.59.own_ref, f32[192,384]{1,0:T(8,128)} %collective-permute-done.other_ref, f32[64,384]{1,0:T(8,128)} %exponential_multiply_fusion.cross_ref), custom_call_target="tpu_custom_call" | custom-call | tf_op jit(solution)/shard_map/pallas_call | solution.py:114
  20.7 10.6 %collective-permute-start.2 = (f32[64,384]{1,0:T(8,128)}, f32[64,384]{1,0:T(8,128)S(1)}, u32[]{:S(2)}, u32[]{:S(2)}) collective-permute-start(f32[64,384]{1,0:T(8,128)} %get-tuple-element.12), channel_id=1, source_target_pairs={{0,32},{16,48},{1,33},{17,49},{2,34},{18,50},{3,35},{19,51},{4,36}... | collective-permute-start | bytes 294920 | tf_op jit(solution)/shard_map/ppermute | solution.py:164
  31.3 2.0 %collective-permute-start.5 = (f32[64,384]{1,0:T(8,128)}, f32[64,384]{1,0:T(8,128)S(1)}, u32[]{:S(2)}, u32[]{:S(2)}) collective-permute-start(f32[64,384]{1,0:T(8,128)} %get-tuple-element.12), channel_id=1, source_target_pairs={{0,64},{16,80},{1,65},{17,81},{2,66},{18,82},{3,67},{19,83},{4,68}... | collective-permute-start | bytes 294920 | tf_op jit(solution)/shard_map/ppermute | solution.py:164
  35.4 1.0 broadcast_select_fusion.7
  39.6 7.4 %collective-permute-start.8 = (f32[64,384]{1,0:T(8,128)S(1)}, f32[64,384]{1,0:T(8,128)S(1)}, u32[]{:S(2)}, u32[]{:S(2)}) collective-permute-start(f32[64,384]{1,0:T(8,128)S(1)} %convolution_subtract_fusion.6), channel_id=1, source_target_pairs={{32,96},{48,112},{0,128},{16,144},{33,97},{49,113},{1,129},{17,145... | collective-permute-start | bytes 294920 | tf_op jit(solution)/shard_map/ppermute | solution.py:164
  48.1 1.3 collective-permute-start.7
  49.9 5.7 %collective-permute-start.10 = (f32[64,384]{1,0:T(8,128)S(1)}, f32[64,384]{1,0:T(8,128)S(1)}, u32[]{:S(2)}, u32[]{:S(2)}) collective-permute-start(f32[64,384]{1,0:T(8,128)S(1)} %sub.116), channel_id=1, source_target_pairs={{64,96},{80,112},{0,160},{16,176},{65,97},{81,113},{1,161},{17,177... | collective-permute-start | bytes 294920 | tf_op jit(solution)/shard_map/ppermute | solution.py:164
  57.1 1.3 collective-permute-start.12
  61.1 6.4 %collective-permute-start.13 = (f32[64,384]{1,0:T(8,128)S(1)}, f32[64,384]{1,0:T(8,128)S(1)}, u32[]{:S(2)}, u32[]{:S(2)}) collective-permute-start(f32[64,384]{1,0:T(8,128)S(1)} %sub.121), channel_id=1, source_target_pairs={{96,128},{112,144},{32,192},{48,208},{0,224},{16,240},{97,129},{11... | collective-permute-start | bytes 294920 | tf_op jit(solution)/shard_map/ppermute | solution.py:164
  71.5 0.8 collective-permute-start.17
  77.8 2.8 %collective-permute-start.26 = (f32[32,128]{1,0:T(8,128)S(1)}, f32[32,128]{1,0:T(8,128)S(1)}, u32[]{:S(2)}, u32[]{:S(2)}) collective-permute-start(f32[32,128]{1,0:T(8,128)S(1)} %broadcast_select_fusion.9), channel_id=1, source_target_pairs={{0,0},{1,16},{2,32},{3,48},{4,64},{5,80},{6,96},{7,112},{8,128},{9... | collective-permute-start | bytes 49160 | tf_op jit(solution)/shard_map/ppermute | solution.py:246
  86.5 0.8 collective-permute-start.25
  87.3 2.9 %collective-permute-start.28 = (f32[64,384]{1,0:T(8,128)S(1)}, f32[64,384]{1,0:T(8,128)S(1)}, u32[]{:S(2)}, u32[]{:S(2)}) collective-permute-start(f32[64,384]{1,0:T(8,128)S(1)} %sub.135), channel_id=1, source_target_pairs={{0,8},{1,24},{2,10},{3,26},{4,12},{5,28},{6,14},{7,30},{8,9},{9,25... | collective-permute-start | bytes 294920 | tf_op jit(solution)/shard_map/ppermute | solution.py:233
  91.6 1.7 %collective-permute-done.28 = f32[64,384]{1,0:T(8,128)S(1)} collective-permute-done((f32[64,384]{1,0:T(8,128)S(1)}, f32[64,384]{1,0:T(8,128)S(1)}, u32[]{:S(2)}, u32[]{:S(2)}) %collective-permute-start.28) | collective-permute-done | bytes 98336 | tf_op jit(solution)/shard_map/ppermute | solution.py:233
  93.3 7.9 %collective-permute-start.31 = (f32[128,384]{1,0:T(8,128)S(1)}, f32[128,384]{1,0:T(8,128)S(1)}, u32[]{:S(2)}, u32[]{:S(2)}) collective-permute-start(f32[128,384]{1,0:T(8,128)S(1)} %maximum_select_fusion.4), channel_id=1, source_target_pairs={{0,6},{1,7},{2,4},{3,5},{4,2},{5,3},{6,0},{7,1},{8,14},{9,15},{10,... | collective-permute-start | bytes 589832 | tf_op jit(solution)/shard_map/ppermute | solution.py:242
  101.2 2.9 %collective-permute-start.30 = (f32[128,384]{1,0:T(8,128)S(1)}, f32[128,384]{1,0:T(8,128)S(1)}, u32[]{:S(2)}, u32[]{:S(2)}) collective-permute-start(f32[128,384]{1,0:T(8,128)S(1)} %maximum_select_fusion.4), channel_id=1, source_target_pairs={{0,4},{1,5},{2,6},{3,7},{4,0},{5,1},{6,2},{7,3},{8,12},{9,13},{10,... | collective-permute-start | bytes 589832 | tf_op jit(solution)/shard_map/ppermute | solution.py:242
  104.1 1.1 collective-permute-start.29
  105.2 1.5 collective-permute-start.32
  106.7 2.8 %collective-permute-done.30 = f32[128,384]{1,0:T(8,128)S(1)} collective-permute-done((f32[128,384]{1,0:T(8,128)S(1)}, f32[128,384]{1,0:T(8,128)S(1)}, u32[]{:S(2)}, u32[]{:S(2)}) %collective-permute-start.30) | collective-permute-done | bytes 196640 | tf_op jit(solution)/shard_map/ppermute | solution.py:242
  109.5 4.7 %collective-permute-done.29 = f32[128,384]{1,0:T(8,128)S(1)} collective-permute-done((f32[128,384]{1,0:T(8,128)S(1)}, f32[128,384]{1,0:T(8,128)S(1)}, u32[]{:S(2)}, u32[]{:S(2)}) %collective-permute-start.29) | collective-permute-done | bytes 196640 | tf_op jit(solution)/shard_map/ppermute | solution.py:242
  115.0 0.9 collective-permute-start.33
  118.2 0.8 maximum_select_fusion.1
  119.0 16.7 %all-to-all-start = ((f32[8,128,128]{2,1,0:T(8,128)}), f32[8,128,128]{2,1,0:T(8,128)S(1)}, u32[]{:S(2)}, u32[]{:S(2)}) async-start(f32[8,128,128]{2,1,0:T(8,128)} %bitcast.12), calls=%async_computation | async-start | bytes 1048576 | tf_op jit(solution)/shard_map/all_to_all | solution.py:253
  136.6 17.4 %all-to-all-done = f32[8,128,128]{2,1,0:T(8,128)S(1)} async-done(((f32[8,128,128]{2,1,0:T(8,128)}), f32[8,128,128]{2,1,0:T(8,128)S(1)}, u32[]{:S(2)}, u32[]{:S(2)}) %all-to-all-start) | async-done | bytes 524320 | tf_op jit(solution)/shard_map/all_to_all | solution.py:253
  (135 shorter events, 32.6 us)
Async XLA Ops:
  5.0 12.5 %collective-permute-start = (f32[192,384]{1,0:T(8,128)}, f32[192,384]{1,0:T(8,128)}, u32[]{:S(2)}, u32[]{:S(2)}) collective-permute-start(f32[192,384]{1,0:T(8,128)} %shard_map.59.own_ref), channel_id=1, source_target_pairs={{0,16},{16,0},{32,48},{48,32},{64,80},{80,64},{96,112},{112,96},{1... | collective-permute-start | bytes 884744 | tf_op jit(solution)/shard_map/ppermute | solution.py:157
  6.5 8.2 %collective-permute-start.1 = (f32[32,192]{1,0:T(8,128)}, f32[32,192]{1,0:T(8,128)}, u32[]{:S(2)}, u32[]{:S(2)}) collective-permute-start(f32[32,192]{1,0:T(8,128)} %param.4), channel_id=1, source_target_pairs={{0,16},{16,0},{32,48},{48,32},{64,80},{80,64},{96,112},{112,96},{1... | collective-permute-start | bytes 73736 | tf_op jit(solution)/shard_map/ppermute | solution.py:155
  8.0 7.7 %collective-permute-start.3 = (f32[192,384]{1,0:T(8,128)}, f32[192,384]{1,0:T(8,128)}, u32[]{:S(2)}, u32[]{:S(2)}) collective-permute-start(f32[192,384]{1,0:T(8,128)} %get-tuple-element.26), channel_id=1, source_target_pairs={{32,48},{48,32},{64,80},{80,64},{96,112},{112,96},{128,144},{144,1... | collective-permute-start | bytes 884744 | tf_op jit(solution)/shard_map/ppermute | solution.py:176
  15.7 19.0 %collective-permute-start.4 = (f32[192,384]{1,0:T(8,128)}, f32[192,384]{1,0:T(8,128)S(1)}, u32[]{:S(2)}, u32[]{:S(2)}) collective-permute-start(f32[192,384]{1,0:T(8,128)} %collective-permute-done.3), channel_id=1, source_target_pairs={{32,33},{33,32},{34,35},{35,34},{36,37},{37,36},{38,39},{39,38},{4... | collective-permute-start | bytes 884744 | tf_op jit(solution)/shard_map/ppermute | solution.py:182
  20.7 17.6 %collective-permute-start.2 = (f32[64,384]{1,0:T(8,128)}, f32[64,384]{1,0:T(8,128)S(1)}, u32[]{:S(2)}, u32[]{:S(2)}) collective-permute-start(f32[64,384]{1,0:T(8,128)} %get-tuple-element.12), channel_id=1, source_target_pairs={{0,32},{16,48},{1,33},{17,49},{2,34},{18,50},{3,35},{19,51},{4,36}... | collective-permute-start | bytes 294920 | tf_op jit(solution)/shard_map/ppermute | solution.py:164
  31.3 15.7 %collective-permute-start.5 = (f32[64,384]{1,0:T(8,128)}, f32[64,384]{1,0:T(8,128)S(1)}, u32[]{:S(2)}, u32[]{:S(2)}) collective-permute-start(f32[64,384]{1,0:T(8,128)} %get-tuple-element.12), channel_id=1, source_target_pairs={{0,64},{16,80},{1,65},{17,81},{2,66},{18,82},{3,67},{19,83},{4,68}... | collective-permute-start | bytes 294920 | tf_op jit(solution)/shard_map/ppermute | solution.py:164
  33.3 16.5 %collective-permute-start.9 = (f32[192,768]{1,0:T(8,128)S(1)}, f32[192,768]{1,0:T(8,128)S(1)}, u32[]{:S(2)}, u32[]{:S(2)}) collective-permute-start(f32[192,768]{1,0:T(8,128)S(1)} %get-tuple-element.16), channel_id=1, source_target_pairs={{96,112},{112,96},{128,144},{144,128},{160,176},{176,160},{192,208... | collective-permute-start | bytes 1769480 | tf_op jit(solution)/shard_map/ppermute | solution.py:176
  34.0 27.1 %collective-permute-start.16 = (f32[192,768]{1,0:T(8,128)S(1)}, f32[192,768]{1,0:T(8,128)S(1)}, u32[]{:S(2)}, u32[]{:S(2)}) collective-permute-start(f32[192,768]{1,0:T(8,128)S(1)} %get-tuple-element.17), channel_id=1, source_target_pairs={{160,176},{176,160},{192,208},{208,192},{224,240},{240,224},{161,1... | collective-permute-start | bytes 1769480 | tf_op jit(solution)/shard_map/ppermute | solution.py:176
  34.7 38.3 %collective-permute-start.23 = (f32[192,768]{1,0:T(8,128)S(1)}, f32[192,768]{1,0:T(8,128)S(1)}, u32[]{:S(2)}, u32[]{:S(2)}) collective-permute-start(f32[192,768]{1,0:T(8,128)S(1)} %pad_maximum_fusion.3), channel_id=1, source_target_pairs={{224,240},{240,224},{225,241},{241,225},{226,242},{242,226},{227,2... | collective-permute-start | bytes 1769480 | tf_op jit(solution)/shard_map/ppermute | solution.py:176
  39.6 17.5 %collective-permute-start.8 = (f32[64,384]{1,0:T(8,128)S(1)}, f32[64,384]{1,0:T(8,128)S(1)}, u32[]{:S(2)}, u32[]{:S(2)}) collective-permute-start(f32[64,384]{1,0:T(8,128)S(1)} %convolution_subtract_fusion.6), channel_id=1, source_target_pairs={{32,96},{48,112},{0,128},{16,144},{33,97},{49,113},{1,129},{17,145... | collective-permute-start | bytes 294920 | tf_op jit(solution)/shard_map/ppermute | solution.py:164
  48.1 10.8 %collective-permute-start.7 = (f32[64,384]{1,0:T(8,128)S(1)}, f32[64,384]{1,0:T(8,128)S(1)}, u32[]{:S(2)}, u32[]{:S(2)}) collective-permute-start(f32[64,384]{1,0:T(8,128)S(1)} %convolution_subtract_fusion.6), channel_id=1, source_target_pairs={{0,96},{16,112},{1,97},{17,113},{2,98},{18,114},{3,99},{19,115},{4... | collective-permute-start | bytes 294920 | tf_op jit(solution)/shard_map/ppermute | solution.py:164
  49.9 10.1 %collective-permute-start.10 = (f32[64,384]{1,0:T(8,128)S(1)}, f32[64,384]{1,0:T(8,128)S(1)}, u32[]{:S(2)}, u32[]{:S(2)}) collective-permute-start(f32[64,384]{1,0:T(8,128)S(1)} %sub.116), channel_id=1, source_target_pairs={{64,96},{80,112},{0,160},{16,176},{65,97},{81,113},{1,161},{17,177... | collective-permute-start | bytes 294920 | tf_op jit(solution)/shard_map/ppermute | solution.py:164
  57.1 11.9 %collective-permute-start.12 = (f32[64,384]{1,0:T(8,128)S(1)}, f32[64,384]{1,0:T(8,128)S(1)}, u32[]{:S(2)}, u32[]{:S(2)}) collective-permute-start(f32[64,384]{1,0:T(8,128)S(1)} %sub.116), channel_id=1, source_target_pairs={{64,128},{80,144},{32,160},{48,176},{0,192},{16,208},{65,129},{81,... | collective-permute-start | bytes 294920 | tf_op jit(solution)/shard_map/ppermute | solution.py:164
  58.8 11.3 %collective-permute-start.11 = (f32[64,384]{1,0:T(8,128)S(1)}, f32[64,384]{1,0:T(8,128)S(1)}, u32[]{:S(2)}, u32[]{:S(2)}) collective-permute-start(f32[64,384]{1,0:T(8,128)S(1)} %sub.116), channel_id=1, source_target_pairs={{32,128},{48,144},{33,129},{49,145},{34,130},{50,146},{35,131},{51... | collective-permute-start | bytes 294920 | tf_op jit(solution)/shard_map/ppermute | solution.py:164
  60.4 14.7 %collective-permute-start.15 = (f32[64,384]{1,0:T(8,128)S(1)}, f32[64,384]{1,0:T(8,128)S(1)}, u32[]{:S(2)}, u32[]{:S(2)}) collective-permute-start(f32[64,384]{1,0:T(8,128)S(1)} %sub.121), channel_id=1, source_target_pairs={{96,160},{112,176},{64,192},{80,208},{32,224},{48,240},{97,161},{1... | collective-permute-start | bytes 294920 | tf_op jit(solution)/shard_map/ppermute | solution.py:164
  61.1 10.0 %collective-permute-start.13 = (f32[64,384]{1,0:T(8,128)S(1)}, f32[64,384]{1,0:T(8,128)S(1)}, u32[]{:S(2)}, u32[]{:S(2)}) collective-permute-start(f32[64,384]{1,0:T(8,128)S(1)} %sub.121), channel_id=1, source_target_pairs={{96,128},{112,144},{32,192},{48,208},{0,224},{16,240},{97,129},{11... | collective-permute-start | bytes 294920 | tf_op jit(solution)/shard_map/ppermute | solution.py:164
  69.0 8.4 %collective-permute-start.14 = (f32[64,384]{1,0:T(8,128)S(1)}, f32[64,384]{1,0:T(8,128)S(1)}, u32[]{:S(2)}, u32[]{:S(2)}) collective-permute-start(f32[64,384]{1,0:T(8,128)S(1)} %sub.121), channel_id=1, source_target_pairs={{64,160},{80,176},{65,161},{81,177},{66,162},{82,178},{67,163},{83... | collective-permute-start | bytes 294920 | tf_op jit(solution)/shard_map/ppermute | solution.py:164
  71.5 9.1 %collective-permute-start.17 = (f32[64,384]{1,0:T(8,128)S(1)}, f32[64,384]{1,0:T(8,128)S(1)}, u32[]{:S(2)}, u32[]{:S(2)}) collective-permute-start(f32[64,384]{1,0:T(8,128)S(1)} %sub.125), channel_id=1, source_target_pairs={{128,160},{144,176},{64,224},{80,240},{129,161},{145,177},{65,225}... | collective-permute-start | bytes 294920 | tf_op jit(solution)/shard_map/ppermute | solution.py:164
  72.4 10.1 %collective-permute-start.19 = (f32[64,384]{1,0:T(8,128)S(1)}, f32[64,384]{1,0:T(8,128)S(1)}, u32[]{:S(2)}, u32[]{:S(2)}) collective-permute-start(f32[64,384]{1,0:T(8,128)S(1)} %sub.125), channel_id=1, source_target_pairs={{128,192},{144,208},{96,224},{112,240},{129,193},{145,209},{97,225... | collective-permute-start | bytes 294920 | tf_op jit(solution)/shard_map/ppermute | solution.py:164
  73.0 10.5 %collective-permute-start.18 = (f32[64,384]{1,0:T(8,128)S(1)}, f32[64,384]{1,0:T(8,128)S(1)}, u32[]{:S(2)}, u32[]{:S(2)}) collective-permute-start(f32[64,384]{1,0:T(8,128)S(1)} %sub.125), channel_id=1, source_target_pairs={{96,192},{112,208},{97,193},{113,209},{98,194},{114,210},{99,195},... | collective-permute-start | bytes 294920 | tf_op jit(solution)/shard_map/ppermute | solution.py:164
  77.8 13.0 %collective-permute-start.26 = (f32[32,128]{1,0:T(8,128)S(1)}, f32[32,128]{1,0:T(8,128)S(1)}, u32[]{:S(2)}, u32[]{:S(2)}) collective-permute-start(f32[32,128]{1,0:T(8,128)S(1)} %broadcast_select_fusion.9), channel_id=1, source_target_pairs={{0,0},{1,16},{2,32},{3,48},{4,64},{5,80},{6,96},{7,112},{8,128},{9... | collective-permute-start | bytes 49160 | tf_op jit(solution)/shard_map/ppermute | solution.py:246
  81.1 4.1 %collective-permute-start.22 = (f32[64,384]{1,0:T(8,128)S(1)}, f32[64,384]{1,0:T(8,128)S(1)}, u32[]{:S(2)}, u32[]{:S(2)}) collective-permute-start(f32[64,384]{1,0:T(8,128)S(1)} %sub.129), channel_id=1, source_target_pairs={{160,224},{176,240},{161,225},{177,241},{162,226},{178,242},{163,2... | collective-permute-start | bytes 294920 | tf_op jit(solution)/shard_map/ppermute | solution.py:164
  82.5 3.1 %collective-permute-start.21 = (f32[64,384]{1,0:T(8,128)S(1)}, f32[64,384]{1,0:T(8,128)S(1)}, u32[]{:S(2)}, u32[]{:S(2)}) collective-permute-start(f32[64,384]{1,0:T(8,128)S(1)} %sub.129), channel_id=1, source_target_pairs={{128,224},{144,240},{129,225},{145,241},{130,226},{146,242},{131,2... | collective-permute-start | bytes 294920 | tf_op jit(solution)/shard_map/ppermute | solution.py:164
  86.5 18.7 %collective-permute-start.25 = (f32[64,384]{1,0:T(8,128)S(1)}, f32[64,384]{1,0:T(8,128)S(1)}, u32[]{:S(2)}, u32[]{:S(2)}) collective-permute-start(f32[64,384]{1,0:T(8,128)S(1)} %sub.135), channel_id=1, source_target_pairs={{0,16},{16,0},{32,48},{48,32},{64,80},{80,64},{96,112},{112,96},{1... | collective-permute-start | bytes 294920 | tf_op jit(solution)/shard_map/ppermute | solution.py:235
  87.3 6.0 %collective-permute-start.28 = (f32[64,384]{1,0:T(8,128)S(1)}, f32[64,384]{1,0:T(8,128)S(1)}, u32[]{:S(2)}, u32[]{:S(2)}) collective-permute-start(f32[64,384]{1,0:T(8,128)S(1)} %sub.135), channel_id=1, source_target_pairs={{0,8},{1,24},{2,10},{3,26},{4,12},{5,28},{6,14},{7,30},{8,9},{9,25... | collective-permute-start | bytes 294920 | tf_op jit(solution)/shard_map/ppermute | solution.py:233
  90.2 3.1 %collective-permute-start.27 = (f32[64,384]{1,0:T(8,128)S(1)}, f32[64,384]{1,0:T(8,128)S(1)}, u32[]{:S(2)}, u32[]{:S(2)}) collective-permute-start(f32[64,384]{1,0:T(8,128)S(1)} %sub.135), channel_id=1, source_target_pairs={{0,0},{1,16},{2,2},{3,18},{4,4},{5,20},{6,6},{7,22},{8,1},{9,17},{... | collective-permute-start | bytes 294920 | tf_op jit(solution)/shard_map/ppermute | solution.py:233
  93.3 13.4 %collective-permute-start.31 = (f32[128,384]{1,0:T(8,128)S(1)}, f32[128,384]{1,0:T(8,128)S(1)}, u32[]{:S(2)}, u32[]{:S(2)}) collective-permute-start(f32[128,384]{1,0:T(8,128)S(1)} %maximum_select_fusion.4), channel_id=1, source_target_pairs={{0,6},{1,7},{2,4},{3,5},{4,2},{5,3},{6,0},{7,1},{8,14},{9,15},{10,... | collective-permute-start | bytes 589832 | tf_op jit(solution)/shard_map/ppermute | solution.py:242
  101.2 8.3 %collective-permute-start.30 = (f32[128,384]{1,0:T(8,128)S(1)}, f32[128,384]{1,0:T(8,128)S(1)}, u32[]{:S(2)}, u32[]{:S(2)}) collective-permute-start(f32[128,384]{1,0:T(8,128)S(1)} %maximum_select_fusion.4), channel_id=1, source_target_pairs={{0,4},{1,5},{2,6},{3,7},{4,0},{5,1},{6,2},{7,3},{8,12},{9,13},{10,... | collective-permute-start | bytes 589832 | tf_op jit(solution)/shard_map/ppermute | solution.py:242
  104.1 10.1 %collective-permute-start.29 = (f32[128,384]{1,0:T(8,128)S(1)}, f32[128,384]{1,0:T(8,128)S(1)}, u32[]{:S(2)}, u32[]{:S(2)}) collective-permute-start(f32[128,384]{1,0:T(8,128)S(1)} %maximum_select_fusion.4), channel_id=1, source_target_pairs={{0,2},{1,3},{2,0},{3,1},{4,6},{5,7},{6,4},{7,5},{8,10},{9,11},{10,... | collective-permute-start | bytes 589832 | tf_op jit(solution)/shard_map/ppermute | solution.py:242
  105.2 9.3 %collective-permute-start.32 = (f32[128,384]{1,0:T(8,128)S(1)}, f32[128,384]{1,0:T(8,128)S(1)}, u32[]{:S(2)}, u32[]{:S(2)}) collective-permute-start(f32[128,384]{1,0:T(8,128)S(1)} %maximum_select_fusion.2), channel_id=1, source_target_pairs={{0,1},{1,0},{2,3},{3,2},{4,5},{5,4},{6,7},{7,6},{8,9},{9,8},{10,11... | collective-permute-start | bytes 589832 | tf_op jit(solution)/shard_map/ppermute | solution.py:238
  115.0 3.2 %collective-permute-start.33 = (f32[512,128]{1,0:T(8,128)S(1)}, f32[512,128]{1,0:T(8,128)S(1)}, u32[]{:S(2)}, u32[]{:S(2)}) collective-permute-start(f32[512,128]{1,0:T(8,128)S(1)} %fusion.37), channel_id=1, source_target_pairs={{0,1},{1,0},{2,3},{3,2},{4,5},{5,4},{6,7},{7,6},{8,9},{9,8},{10,11... | collective-permute-start | bytes 786440 | tf_op jit(solution)/shard_map/ppermute | solution.py:249
  119.0 34.9 %all-to-all-start = ((f32[8,128,128]{2,1,0:T(8,128)}), f32[8,128,128]{2,1,0:T(8,128)S(1)}, u32[]{:S(2)}, u32[]{:S(2)}) async-start(f32[8,128,128]{2,1,0:T(8,128)} %bitcast.12), calls=%async_computation | async-start | bytes 1048576 | tf_op jit(solution)/shard_map/all_to_all | solution.py:253
  (15 other events, 45.9 us)

commit v10 on v9

--- a/solution.py
+++ b/solution.py
@@ -236,21 +236,24 @@
     columns_all = both(solved, other_columns, 0)
     rows = jnp.where(side == 0, columns_all[:, :height], columns_all[:, height:]).T
     twin_columns = lax.ppermute(columns_all, "cand", [(c, c ^ 1) for c in range(cand)])
-    row = lax.axis_index("cand") // 2 % (cand // 4)
     others = [turned]
     for r in range(1, cand // 4):
         others.append(lax.ppermute(turned, "cand", [(c, c ^ (2 * r)) for c in range(cand)]))
-    others = both_of(row // 2, jnp.stack(others[:2]), jnp.stack(others[2:]), 0).reshape(2, 2, width, span)
-    others = both_of(row % 2, others[:, :1], others[:, 1:])
+    others = jnp.concatenate(others, axis=0)
     swap = [(a * cand + b, b * cand + a) for a in range(chain) for b in range(cand)]
     chosen = lax.ppermute(wanted, ("chain", "cand"), swap)
     prior_cov = matern(chosen * after(scaling, solved)[:, None], scaled_candidates)
-    others = others.reshape(cand // 4 * width, span)
     theirs = lax.ppermute(quick(others, twin_columns, 1), "cand", [(c, c ^ 1) for c in range(cand)])
     ours = quick(others, columns_all, 1)
-    shares = both_of(core + unset(prior_cov), ours, theirs, 0).reshape(layers, width, width)
-    same_side = [[2 * z + y for z in range(layers)] for y in range(2)]
-    shared = lax.all_to_all(shares, "chain", 0, 0, axis_index_groups=same_side, tiled=True).sum(axis=0)
+    shares = jnp.concatenate([ours, theirs], axis=0).reshape(layers, width, width)
+    owners = [
+        [(2 * (4 * (c % 2 ^ j) + (c // 2 % 4 ^ r)) + y) * cand + c for j in range(2) for r in range(4)]
+        for y in range(2)
+        for c in range(cand)
+    ]
+    shared = lax.all_to_all(
+        shares, ("chain", "cand"), 0, 0, axis_index_groups=owners, tiled=True
+    ).sum(axis=0)
     return (rows, prior_cov - shared)
 
 

time: 157 us -> 145 us (0.924)
  the two profiles are of different devices: /device:TPU:2 before, /device:TPU:22 now
where the time goes in v10:
time: 145 us; the launch traced here: 144 us
  starting transfers between devices  83.1 us (57%)
  waiting for transfers between devices  24 us (17%)
  matrix products  13.9 us (10%)
  other arithmetic  9.7 us (7%)
  Pallas kernels  7.6 us (5%)
  local copies, waits for them, and re-layouts  2.96 us (2%)
  between operations  2.67 us (2%)
    ppermute x18, starting transfers between devices, hop(): lax.ppermute(value, 'chain', [(2 * a + i, 2 * b + i) for a, b in pairs fo...  41.2 us
    all_to_all x1, starting transfers between devices, shards(): lax.all_to_all(shares, ('chain', 'cand'), 0, 0, axis_index_groups=owners,...  22 us
    dot_general x28, matrix products, quick(): lax.dot_general(a, b, (((1,), (contract,)), ((), ())), precision=lax.Prec...  13.9 us
    ppermute x1, waiting for transfers between devices, shards(): chosen = lax.ppermute(wanted, ('chain', 'cand'), swap)  10.3 us
    ppermute x3, waiting for transfers between devices, shards(): lax.ppermute(turned, 'cand', [(c, c ^ 2 * r) for c in range(cand)])  6.92 us
    ppermute x2, starting transfers between devices, shards(): turned.append(lax.ppermute(solved, ('chain', 'cand'), turn))  4.43 us
    pallas_call x1, Pallas kernels, own_inverse(): pl.pallas_call(own_kernel, grid_spec=pltpu.PrefetchScalarGridSpec(num_sca...  4.32 us
    ppermute x3, starting transfers between devices, shards(): lax.ppermute(turned, 'cand', [(c, c ^ 2 * r) for c in range(cand)])  4.18 us
  transfers between devices with their start and end apart: 35, of which 8 were waited for; matrix products, arithmetic and copies ran while one was open for 16% of the time, Pallas kernels for 2%

profile of v10, /device:TPU:22, one launch (start us, length us, event | category | flops | bytes accessed | tf_op | source)
XLA Modules:
  0.0 143.9 jit_solution(10192759247981471343)
XLA Ops:
  0.6 4.3 %shard_map.59.own_ref = f32[192,384]{1,0:T(8,128)} custom-call(s32[1]{0:T(128)} %bitcast.place_ref, f32[192,3072]{1,0:T(8,128)} %own_ref.1), custom_call_target="tpu_custom_call" | custom-call | tf_op jit(solution)/shard_map/pallas_call | solution.py:82
  5.0 1.3 collective-permute-start
  6.3 0.7 collective-permute-start.1
  7.0 1.0 broadcast_select_fusion.8
  8.0 1.4 collective-permute-start.3
  10.0 1.0 slice_select_fusion.3
  11.0 1.1 pad_maximum_fusion.3
  12.3 2.5 %collective-permute-done.1 = f32[32,192]{1,0:T(8,128)} collective-permute-done((f32[32,192]{1,0:T(8,128)}, f32[32,192]{1,0:T(8,128)}, u32[]{:S(2)}, u32[]{:S(2)}) %collective-permute-start.1) | collective-permute-done | bytes 24608 | tf_op jit(solution)/shard_map/ppermute | solution.py:155
  14.7 0.9 fusion.15
  15.7 1.4 collective-permute-start.4
  18.2 3.3 %shard_map.60 = (f32[384,192]{1,0:T(8,128)}, f32[384,192]{1,0:T(8,128)}, f32[64,384]{1,0:T(8,128)}) custom-call(s32[1]{0:T(128)} %bitcast.place_ref, f32[192,384]{1,0:T(8,128)} %shard_map.59.own_ref, f32[192,384]{1,0:T(8,128)} %collective-permute-done.other_ref, f32[64,384]{1,0:T(8,128)} %exponential_multiply_fusion.cross_ref), custom_call_target="tpu_custom_call" | custom-call | tf_op jit(solution)/shard_map/pallas_call | solution.py:114
  21.5 9.8 %collective-permute-start.2 = (f32[64,384]{1,0:T(8,128)}, f32[64,384]{1,0:T(8,128)S(1)}, u32[]{:S(2)}, u32[]{:S(2)}) collective-permute-start(f32[64,384]{1,0:T(8,128)} %get-tuple-element.12), channel_id=1, source_target_pairs={{0,32},{16,48},{1,33},{17,49},{2,34},{18,50},{3,35},{19,51},{4,36}... | collective-permute-start | bytes 294920 | tf_op jit(solution)/shard_map/ppermute | solution.py:164
  31.3 2.0 %collective-permute-start.5 = (f32[64,384]{1,0:T(8,128)}, f32[64,384]{1,0:T(8,128)S(1)}, u32[]{:S(2)}, u32[]{:S(2)}) collective-permute-start(f32[64,384]{1,0:T(8,128)} %get-tuple-element.12), channel_id=1, source_target_pairs={{0,64},{16,80},{1,65},{17,81},{2,66},{18,82},{3,67},{19,83},{4,68}... | collective-permute-start | bytes 294920 | tf_op jit(solution)/shard_map/ppermute | solution.py:164
  35.5 1.1 broadcast_select_fusion.7
  38.5 0.8 copy-done.7
  39.7 7.1 %collective-permute-start.8 = (f32[64,384]{1,0:T(8,128)S(1)}, f32[64,384]{1,0:T(8,128)S(1)}, u32[]{:S(2)}, u32[]{:S(2)}) collective-permute-start(f32[64,384]{1,0:T(8,128)S(1)} %convolution_subtract_fusion.6), channel_id=1, source_target_pairs={{32,96},{48,112},{0,128},{16,144},{33,97},{49,113},{1,129},{17,145... | collective-permute-start | bytes 294920 | tf_op jit(solution)/shard_map/ppermute | solution.py:164
  47.9 1.3 collective-permute-start.7
  49.7 5.9 %collective-permute-start.10 = (f32[64,384]{1,0:T(8,128)S(1)}, f32[64,384]{1,0:T(8,128)S(1)}, u32[]{:S(2)}, u32[]{:S(2)}) collective-permute-start(f32[64,384]{1,0:T(8,128)S(1)} %sub.110), channel_id=1, source_target_pairs={{64,96},{80,112},{0,160},{16,176},{65,97},{81,113},{1,161},{17,177... | collective-permute-start | bytes 294920 | tf_op jit(solution)/shard_map/ppermute | solution.py:164
  57.1 1.3 collective-permute-start.12
  61.1 6.4 %collective-permute-start.13 = (f32[64,384]{1,0:T(8,128)S(1)}, f32[64,384]{1,0:T(8,128)S(1)}, u32[]{:S(2)}, u32[]{:S(2)}) collective-permute-start(f32[64,384]{1,0:T(8,128)S(1)} %sub.115), channel_id=1, source_target_pairs={{96,128},{112,144},{32,192},{48,208},{0,224},{16,240},{97,129},{11... | collective-permute-start | bytes 294920 | tf_op jit(solution)/shard_map/ppermute | solution.py:164
  71.6 0.8 collective-permute-start.17
  81.9 1.4 collective-permute-start.25
  83.3 4.4 %collective-permute-start.27 = (f32[64,384]{1,0:T(8,128)S(1)}, f32[64,384]{1,0:T(8,128)S(1)}, u32[]{:S(2)}, u32[]{:S(2)}) collective-permute-start(f32[64,384]{1,0:T(8,128)S(1)} %sub.129), channel_id=1, source_target_pairs={{0,0},{1,16},{2,2},{3,18},{4,4},{5,20},{6,6},{7,22},{8,1},{9,17},{... | collective-permute-start | bytes 294920 | tf_op jit(solution)/shard_map/ppermute | solution.py:233
  87.8 2.0 %collective-permute-done.28 = f32[64,384]{1,0:T(8,128)S(1)} collective-permute-done((f32[64,384]{1,0:T(8,128)S(1)}, f32[64,384]{1,0:T(8,128)S(1)}, u32[]{:S(2)}, u32[]{:S(2)}) %collective-permute-start.28) | collective-permute-done | bytes 98336 | tf_op jit(solution)/shard_map/ppermute | solution.py:233
  91.0 2.4 %collective-permute-start.30 = (f32[128,384]{1,0:T(8,128)S(1)}, f32[128,384]{1,0:T(8,128)S(1)}, u32[]{:S(2)}, u32[]{:S(2)}) collective-permute-start(f32[128,384]{1,0:T(8,128)S(1)} %maximum_select_fusion.1), channel_id=1, source_target_pairs={{0,4},{1,5},{2,6},{3,7},{4,0},{5,1},{6,2},{7,3},{8,12},{9,13},{10,... | collective-permute-start | bytes 589832 | tf_op jit(solution)/shard_map/ppermute | solution.py:241
  93.4 1.2 collective-permute-start.29
  94.6 6.3 %collective-permute-done.31 = f32[128,384]{1,0:T(8,128)S(1)} collective-permute-done((f32[128,384]{1,0:T(8,128)S(1)}, f32[128,384]{1,0:T(8,128)S(1)}, u32[]{:S(2)}, u32[]{:S(2)}) %collective-permute-start.31) | collective-permute-done | bytes 196640 | tf_op jit(solution)/shard_map/ppermute | solution.py:241
  102.7 1.0 collective-permute-done.33
  103.7 0.8 pad_maximum_fusion.4
  104.5 22.0 %all-to-all-start = ((f32[8,128,128]{2,1,0:T(8,128)}), f32[8,128,128]{2,1,0:T(8,128)S(1)}, u32[]{:S(2)}, u32[]{:S(2)}) async-start(f32[8,128,128]{2,1,0:T(8,128)} %bitcast.3), calls=%async_computation | async-start | bytes 1048576 | tf_op jit(solution)/shard_map/all_to_all | solution.py:254
  128.4 2.8 %collective-permute-start.26 = (f32[32,128]{1,0:T(8,128)S(1)}, f32[32,128]{1,0:T(8,128)S(1)}, u32[]{:S(2)}, u32[]{:S(2)}) collective-permute-start(f32[32,128]{1,0:T(8,128)S(1)} %broadcast_select_fusion.9), channel_id=1, source_target_pairs={{0,0},{1,16},{2,32},{3,48},{4,64},{5,80},{6,96},{7,112},{8,128},{9... | collective-permute-start | bytes 49160 | tf_op jit(solution)/shard_map/ppermute | solution.py:244
  131.2 10.3 %collective-permute-done.26 = f32[32,128]{1,0:T(8,128)S(1)} collective-permute-done((f32[32,128]{1,0:T(8,128)S(1)}, f32[32,128]{1,0:T(8,128)S(1)}, u32[]{:S(2)}, u32[]{:S(2)}) %collective-permute-start.26) | collective-permute-done | bytes 16416 | tf_op jit(solution)/shard_map/ppermute | solution.py:244
  (132 shorter events, 31.2 us)
Async XLA Ops:
  5.0 13.2 %collective-permute-start = (f32[192,384]{1,0:T(8,128)}, f32[192,384]{1,0:T(8,128)}, u32[]{:S(2)}, u32[]{:S(2)}) collective-permute-start(f32[192,384]{1,0:T(8,128)} %shard_map.59.own_ref), channel_id=1, source_target_pairs={{0,16},{16,0},{32,48},{48,32},{64,80},{80,64},{96,112},{112,96},{1... | collective-permute-start | bytes 884744 | tf_op jit(solution)/shard_map/ppermute | solution.py:157
  6.3 8.5 %collective-permute-start.1 = (f32[32,192]{1,0:T(8,128)}, f32[32,192]{1,0:T(8,128)}, u32[]{:S(2)}, u32[]{:S(2)}) collective-permute-start(f32[32,192]{1,0:T(8,128)} %param.4), channel_id=1, source_target_pairs={{0,16},{16,0},{32,48},{48,32},{64,80},{80,64},{96,112},{112,96},{1... | collective-permute-start | bytes 73736 | tf_op jit(solution)/shard_map/ppermute | solution.py:155
  8.0 7.7 %collective-permute-start.3 = (f32[192,384]{1,0:T(8,128)}, f32[192,384]{1,0:T(8,128)}, u32[]{:S(2)}, u32[]{:S(2)}) collective-permute-start(f32[192,384]{1,0:T(8,128)} %get-tuple-element.26), channel_id=1, source_target_pairs={{32,48},{48,32},{64,80},{80,64},{96,112},{112,96},{128,144},{144,1... | collective-permute-start | bytes 884744 | tf_op jit(solution)/shard_map/ppermute | solution.py:176
  15.7 19.0 %collective-permute-start.4 = (f32[192,384]{1,0:T(8,128)}, f32[192,384]{1,0:T(8,128)}, u32[]{:S(2)}, u32[]{:S(2)}) collective-permute-start(f32[192,384]{1,0:T(8,128)} %collective-permute-done.3), channel_id=1, source_target_pairs={{32,33},{33,32},{34,35},{35,34},{36,37},{37,36},{38,39},{39,38},{4... | collective-permute-start | bytes 884744 | tf_op jit(solution)/shard_map/ppermute | solution.py:182
  21.5 17.0 %collective-permute-start.2 = (f32[64,384]{1,0:T(8,128)}, f32[64,384]{1,0:T(8,128)S(1)}, u32[]{:S(2)}, u32[]{:S(2)}) collective-permute-start(f32[64,384]{1,0:T(8,128)} %get-tuple-element.12), channel_id=1, source_target_pairs={{0,32},{16,48},{1,33},{17,49},{2,34},{18,50},{3,35},{19,51},{4,36}... | collective-permute-start | bytes 294920 | tf_op jit(solution)/shard_map/ppermute | solution.py:164
  31.3 15.5 %collective-permute-start.5 = (f32[64,384]{1,0:T(8,128)}, f32[64,384]{1,0:T(8,128)S(1)}, u32[]{:S(2)}, u32[]{:S(2)}) collective-permute-start(f32[64,384]{1,0:T(8,128)} %get-tuple-element.12), channel_id=1, source_target_pairs={{0,64},{16,80},{1,65},{17,81},{2,66},{18,82},{3,67},{19,83},{4,68}... | collective-permute-start | bytes 294920 | tf_op jit(solution)/shard_map/ppermute | solution.py:164
  33.3 16.3 %collective-permute-start.9 = (f32[192,768]{1,0:T(8,128)S(1)}, f32[192,768]{1,0:T(8,128)S(1)}, u32[]{:S(2)}, u32[]{:S(2)}) collective-permute-start(f32[192,768]{1,0:T(8,128)S(1)} %get-tuple-element.16), channel_id=1, source_target_pairs={{96,112},{112,96},{128,144},{144,128},{160,176},{176,160},{192,208... | collective-permute-start | bytes 1769480 | tf_op jit(solution)/shard_map/ppermute | solution.py:176
  34.0 27.1 %collective-permute-start.16 = (f32[192,768]{1,0:T(8,128)S(1)}, f32[192,768]{1,0:T(8,128)S(1)}, u32[]{:S(2)}, u32[]{:S(2)}) collective-permute-start(f32[192,768]{1,0:T(8,128)S(1)} %get-tuple-element.17), channel_id=1, source_target_pairs={{160,176},{176,160},{192,208},{208,192},{224,240},{240,224},{161,1... | collective-permute-start | bytes 1769480 | tf_op jit(solution)/shard_map/ppermute | solution.py:176
  34.8 38.3 %collective-permute-start.23 = (f32[192,768]{1,0:T(8,128)S(1)}, f32[192,768]{1,0:T(8,128)S(1)}, u32[]{:S(2)}, u32[]{:S(2)}) collective-permute-start(f32[192,768]{1,0:T(8,128)S(1)} %pad_maximum_fusion.3), channel_id=1, source_target_pairs={{224,240},{240,224},{225,241},{241,225},{226,242},{242,226},{227,2... | collective-permute-start | bytes 1769480 | tf_op jit(solution)/shard_map/ppermute | solution.py:176
  39.7 17.4 %collective-permute-start.8 = (f32[64,384]{1,0:T(8,128)S(1)}, f32[64,384]{1,0:T(8,128)S(1)}, u32[]{:S(2)}, u32[]{:S(2)}) collective-permute-start(f32[64,384]{1,0:T(8,128)S(1)} %convolution_subtract_fusion.6), channel_id=1, source_target_pairs={{32,96},{48,112},{0,128},{16,144},{33,97},{49,113},{1,129},{17,145... | collective-permute-start | bytes 294920 | tf_op jit(solution)/shard_map/ppermute | solution.py:164
  47.9 11.0 %collective-permute-start.7 = (f32[64,384]{1,0:T(8,128)S(1)}, f32[64,384]{1,0:T(8,128)S(1)}, u32[]{:S(2)}, u32[]{:S(2)}) collective-permute-start(f32[64,384]{1,0:T(8,128)S(1)} %convolution_subtract_fusion.6), channel_id=1, source_target_pairs={{0,96},{16,112},{1,97},{17,113},{2,98},{18,114},{3,99},{19,115},{4... | collective-permute-start | bytes 294920 | tf_op jit(solution)/shard_map/ppermute | solution.py:164
  49.7 10.3 %collective-permute-start.10 = (f32[64,384]{1,0:T(8,128)S(1)}, f32[64,384]{1,0:T(8,128)S(1)}, u32[]{:S(2)}, u32[]{:S(2)}) collective-permute-start(f32[64,384]{1,0:T(8,128)S(1)} %sub.110), channel_id=1, source_target_pairs={{64,96},{80,112},{0,160},{16,176},{65,97},{81,113},{1,161},{17,177... | collective-permute-start | bytes 294920 | tf_op jit(solution)/shard_map/ppermute | solution.py:164
  57.1 11.9 %collective-permute-start.12 = (f32[64,384]{1,0:T(8,128)S(1)}, f32[64,384]{1,0:T(8,128)S(1)}, u32[]{:S(2)}, u32[]{:S(2)}) collective-permute-start(f32[64,384]{1,0:T(8,128)S(1)} %sub.110), channel_id=1, source_target_pairs={{64,128},{80,144},{32,160},{48,176},{0,192},{16,208},{65,129},{81,... | collective-permute-start | bytes 294920 | tf_op jit(solution)/shard_map/ppermute | solution.py:164
  58.9 11.3 %collective-permute-start.11 = (f32[64,384]{1,0:T(8,128)S(1)}, f32[64,384]{1,0:T(8,128)S(1)}, u32[]{:S(2)}, u32[]{:S(2)}) collective-permute-start(f32[64,384]{1,0:T(8,128)S(1)} %sub.110), channel_id=1, source_target_pairs={{32,128},{48,144},{33,129},{49,145},{34,130},{50,146},{35,131},{51... | collective-permute-start | bytes 294920 | tf_op jit(solution)/shard_map/ppermute | solution.py:164
  60.4 14.7 %collective-permute-start.15 = (f32[64,384]{1,0:T(8,128)S(1)}, f32[64,384]{1,0:T(8,128)S(1)}, u32[]{:S(2)}, u32[]{:S(2)}) collective-permute-start(f32[64,384]{1,0:T(8,128)S(1)} %sub.115), channel_id=1, source_target_pairs={{96,160},{112,176},{64,192},{80,208},{32,224},{48,240},{97,161},{1... | collective-permute-start | bytes 294920 | tf_op jit(solution)/shard_map/ppermute | solution.py:164
  61.1 10.0 %collective-permute-start.13 = (f32[64,384]{1,0:T(8,128)S(1)}, f32[64,384]{1,0:T(8,128)S(1)}, u32[]{:S(2)}, u32[]{:S(2)}) collective-permute-start(f32[64,384]{1,0:T(8,128)S(1)} %sub.115), channel_id=1, source_target_pairs={{96,128},{112,144},{32,192},{48,208},{0,224},{16,240},{97,129},{11... | collective-permute-start | bytes 294920 | tf_op jit(solution)/shard_map/ppermute | solution.py:164
  69.0 6.6 %collective-permute-start.14 = (f32[64,384]{1,0:T(8,128)S(1)}, f32[64,384]{1,0:T(8,128)S(1)}, u32[]{:S(2)}, u32[]{:S(2)}) collective-permute-start(f32[64,384]{1,0:T(8,128)S(1)} %sub.115), channel_id=1, source_target_pairs={{64,160},{80,176},{65,161},{81,177},{66,162},{82,178},{67,163},{83... | collective-permute-start | bytes 294920 | tf_op jit(solution)/shard_map/ppermute | solution.py:164
  71.6 4.5 %collective-permute-start.17 = (f32[64,384]{1,0:T(8,128)S(1)}, f32[64,384]{1,0:T(8,128)S(1)}, u32[]{:S(2)}, u32[]{:S(2)}) collective-permute-start(f32[64,384]{1,0:T(8,128)S(1)} %sub.119), channel_id=1, source_target_pairs={{128,160},{144,176},{64,224},{80,240},{129,161},{145,177},{65,225}... | collective-permute-start | bytes 294920 | tf_op jit(solution)/shard_map/ppermute | solution.py:164
  72.4 6.1 %collective-permute-start.19 = (f32[64,384]{1,0:T(8,128)S(1)}, f32[64,384]{1,0:T(8,128)S(1)}, u32[]{:S(2)}, u32[]{:S(2)}) collective-permute-start(f32[64,384]{1,0:T(8,128)S(1)} %sub.119), channel_id=1, source_target_pairs={{128,192},{144,208},{96,224},{112,240},{129,193},{145,209},{97,225... | collective-permute-start | bytes 294920 | tf_op jit(solution)/shard_map/ppermute | solution.py:164
  73.1 5.9 %collective-permute-start.18 = (f32[64,384]{1,0:T(8,128)S(1)}, f32[64,384]{1,0:T(8,128)S(1)}, u32[]{:S(2)}, u32[]{:S(2)}) collective-permute-start(f32[64,384]{1,0:T(8,128)S(1)} %sub.119), channel_id=1, source_target_pairs={{96,192},{112,208},{97,193},{113,209},{98,194},{114,210},{99,195},... | collective-permute-start | bytes 294920 | tf_op jit(solution)/shard_map/ppermute | solution.py:164
  76.5 4.1 %collective-permute-start.22 = (f32[64,384]{1,0:T(8,128)S(1)}, f32[64,384]{1,0:T(8,128)S(1)}, u32[]{:S(2)}, u32[]{:S(2)}) collective-permute-start(f32[64,384]{1,0:T(8,128)S(1)} %sub.123), channel_id=1, source_target_pairs={{160,224},{176,240},{161,225},{177,241},{162,226},{178,242},{163,2... | collective-permute-start | bytes 294920 | tf_op jit(solution)/shard_map/ppermute | solution.py:164
  77.2 2.2 %collective-permute-start.20 = (f32[64,384]{1,0:T(8,128)S(1)}, f32[64,384]{1,0:T(8,128)S(1)}, u32[]{:S(2)}, u32[]{:S(2)}) collective-permute-start(f32[64,384]{1,0:T(8,128)S(1)} %sub.123), channel_id=1, source_target_pairs={{160,192},{176,208},{161,193},{177,209},{162,194},{178,210},{163,1... | collective-permute-start | bytes 294920 | tf_op jit(solution)/shard_map/ppermute | solution.py:164
  77.8 3.1 %collective-permute-start.21 = (f32[64,384]{1,0:T(8,128)S(1)}, f32[64,384]{1,0:T(8,128)S(1)}, u32[]{:S(2)}, u32[]{:S(2)}) collective-permute-start(f32[64,384]{1,0:T(8,128)S(1)} %sub.123), channel_id=1, source_target_pairs={{128,224},{144,240},{129,225},{145,241},{130,226},{146,242},{131,2... | collective-permute-start | bytes 294920 | tf_op jit(solution)/shard_map/ppermute | solution.py:164
  81.9 5.8 %collective-permute-start.25 = (f32[64,384]{1,0:T(8,128)S(1)}, f32[64,384]{1,0:T(8,128)S(1)}, u32[]{:S(2)}, u32[]{:S(2)}) collective-permute-start(f32[64,384]{1,0:T(8,128)S(1)} %sub.129), channel_id=1, source_target_pairs={{0,16},{16,0},{32,48},{48,32},{64,80},{80,64},{96,112},{112,96},{1... | collective-permute-start | bytes 294920 | tf_op jit(solution)/shard_map/ppermute | solution.py:235
  83.3 6.6 %collective-permute-start.28 = (f32[64,384]{1,0:T(8,128)S(1)}, f32[64,384]{1,0:T(8,128)S(1)}, u32[]{:S(2)}, u32[]{:S(2)}) collective-permute-start(f32[64,384]{1,0:T(8,128)S(1)} %sub.129), channel_id=1, source_target_pairs={{0,8},{1,24},{2,10},{3,26},{4,12},{5,28},{6,14},{7,30},{8,9},{9,25... | collective-permute-start | bytes 294920 | tf_op jit(solution)/shard_map/ppermute | solution.py:233
  83.3 7.2 %collective-permute-start.27 = (f32[64,384]{1,0:T(8,128)S(1)}, f32[64,384]{1,0:T(8,128)S(1)}, u32[]{:S(2)}, u32[]{:S(2)}) collective-permute-start(f32[64,384]{1,0:T(8,128)S(1)} %sub.129), channel_id=1, source_target_pairs={{0,0},{1,16},{2,2},{3,18},{4,4},{5,20},{6,6},{7,22},{8,1},{9,17},{... | collective-permute-start | bytes 294920 | tf_op jit(solution)/shard_map/ppermute | solution.py:233
  87.7 6.9 %collective-permute-start.32 = (f32[128,384]{1,0:T(8,128)S(1)}, f32[128,384]{1,0:T(8,128)S(1)}, u32[]{:S(2)}, u32[]{:S(2)}) collective-permute-start(f32[128,384]{1,0:T(8,128)S(1)} %maximum_select_fusion), channel_id=1, source_target_pairs={{0,1},{1,0},{2,3},{3,2},{4,5},{5,4},{6,7},{7,6},{8,9},{9,8},{10,11... | collective-permute-start | bytes 589832 | tf_op jit(solution)/shard_map/ppermute | solution.py:238
  90.5 10.5 %collective-permute-start.31 = (f32[128,384]{1,0:T(8,128)S(1)}, f32[128,384]{1,0:T(8,128)S(1)}, u32[]{:S(2)}, u32[]{:S(2)}) collective-permute-start(f32[128,384]{1,0:T(8,128)S(1)} %maximum_select_fusion.1), channel_id=1, source_target_pairs={{0,6},{1,7},{2,4},{3,5},{4,2},{5,3},{6,0},{7,1},{8,14},{9,15},{10,... | collective-permute-start | bytes 589832 | tf_op jit(solution)/shard_map/ppermute | solution.py:241
  91.0 9.9 %collective-permute-start.30 = (f32[128,384]{1,0:T(8,128)S(1)}, f32[128,384]{1,0:T(8,128)S(1)}, u32[]{:S(2)}, u32[]{:S(2)}) collective-permute-start(f32[128,384]{1,0:T(8,128)S(1)} %maximum_select_fusion.1), channel_id=1, source_target_pairs={{0,4},{1,5},{2,6},{3,7},{4,0},{5,1},{6,2},{7,3},{8,12},{9,13},{10,... | collective-permute-start | bytes 589832 | tf_op jit(solution)/shard_map/ppermute | solution.py:241
  93.4 8.1 %collective-permute-start.29 = (f32[128,384]{1,0:T(8,128)S(1)}, f32[128,384]{1,0:T(8,128)S(1)}, u32[]{:S(2)}, u32[]{:S(2)}) collective-permute-start(f32[128,384]{1,0:T(8,128)S(1)} %maximum_select_fusion.1), channel_id=1, source_target_pairs={{0,2},{1,3},{2,0},{3,1},{4,6},{5,7},{6,4},{7,5},{8,10},{9,11},{10,... | collective-permute-start | bytes 589832 | tf_op jit(solution)/shard_map/ppermute | solution.py:241
  104.5 38.6 %all-to-all-start = ((f32[8,128,128]{2,1,0:T(8,128)}), f32[8,128,128]{2,1,0:T(8,128)S(1)}, u32[]{:S(2)}, u32[]{:S(2)}) async-start(f32[8,128,128]{2,1,0:T(8,128)} %bitcast.3), calls=%async_computation | async-start | bytes 1048576 | tf_op jit(solution)/shard_map/all_to_all | solution.py:254
  128.4 13.2 %collective-permute-start.26 = (f32[32,128]{1,0:T(8,128)S(1)}, f32[32,128]{1,0:T(8,128)S(1)}, u32[]{:S(2)}, u32[]{:S(2)}) collective-permute-start(f32[32,128]{1,0:T(8,128)S(1)} %broadcast_select_fusion.9), channel_id=1, source_target_pairs={{0,0},{1,16},{2,32},{3,48},{4,64},{5,80},{6,96},{7,112},{8,128},{9... | collective-permute-start | bytes 49160 | tf_op jit(solution)/shard_map/ppermute | solution.py:244
  (17 other events, 109.2 us)
